TPU v7x, 32 devices: a whole 2x2x4 slice. The times are simulated.
32 devices in a mesh: groups: 2 (over x), tile: 16 (over z, y, core).
Axes of the slice: x: 2, y: 2, z: 4, core: 2. Of those that a mesh axis runs over, the one named last changes fastest.
Arguments:
- bands: bfloat16 [6144, 1312], P(('groups', 'tile')), parts along dimension 0, may hold values from -6 to 6
- send_table: int32 [16, 384], P('tile'), may hold values from 0 to 191, as said below
- recv_table: int32 [4, 3072], P(None, 'tile'), may hold values from 0 to 383, as said below
- regrid_weight: bfloat16 [3072, 1024], P('tile'), may hold values from 0.0049743652 to 0.25
- embed_weight: bfloat16 [1312, 384], replicated, may hold values from -0.15625 to 0.15625
- norm1_gain: float32 [2, 384], replicated, may hold values from 0.5 to 1.5
- qkv_weight: bfloat16 [2, 384, 1152], replicated, may hold values from -0.3125 to 0.3125
- rel_bias: float32 [2, 12, 225], replicated, may hold values from -6 to 400
- proj_weight: bfloat16 [2, 384, 384], replicated, may hold values from -0.3125 to 0.3125
- norm2_gain: float32 [2, 384], replicated, may hold values from 0.5 to 1.5
- up_weight: bfloat16 [2, 384, 1536], replicated, may hold values from -0.3125 to 0.3125
- down_weight: bfloat16 [2, 1536, 384], replicated, may hold values from -0.15625 to 0.15625
- unembed_weight: bfloat16 [384, 1312], replicated, may hold values from -0.3125 to 0.3125
Outputs:
- increment: float32 [6144, 1312], P(('groups', 'tile')), parts along dimension 0
There are 2 independent parts, one for each index of `groups`. A program takes and returns all parts, laid end to end along the dimension named above; an argument that names none is the same for every part. Nothing has to cross between parts.
Inputs may be any that keep to these rules, and one draw needn't show every extreme that they name: `send_table`: row s lists 24 local block indices of device s for each receiving device in order; every local block appears exactly twice in a row. `recv_table`: slot s * 24 + c of a device is the c-th block that device s passes to it; for each l, rows 2 * l and 2 * l + 1 of a device's patches together name each of its 384 slots exactly once.
All inputs are finite; a program needn't handle non-finite values.
Results may differ from a plain program's by a relative error of at most 0.018.
Values may be sent and summed in bfloat16 or wider, within the bound.
No kernel may reach another device: no remote copies, remote signals or barrier semaphores. Data moves between devices by JAX's collectives and lax.ppermute only.
A program may use at most 128 MiB of HBM per device.

v0:
```python
import functools

import jax
import jax.numpy as jnp
import numpy as np
from jax import lax
from jax.experimental import pallas as pl
from jax.experimental.pallas import tpu as pltpu
from jax.sharding import PartitionSpec as P


WIN = 8
ROWS = 24
LANES = 128
GROUP = 8

norm_eps = 1e-05
F32 = jnp.float32
BF16 = jnp.bfloat16


def iota(shape, axis):
    return lax.broadcasted_iota(jnp.int32, shape, axis)


def mm(a, b):
    return jnp.dot(a, b, preferred_element_type=F32)


def mm_tn(a, b):
    return lax.dot_general(a, b, (((0,), (0,)), ((), ())), preferred_element_type=F32)


def mm_nt(a, b):
    return lax.dot_general(a, b, (((1,), (1,)), ((), ())), preferred_element_type=F32)


VMEM_LIMIT = 16 << 20


class In:
    def __init__(self, array, index=None):
        self.array = array
        self.index = index


def at(array, index):
    return In(array, index)


class Loaded:
    def __init__(self, ref):
        self.ref = ref

    def __call__(self):
        return self.ref


def call(kernel, ins, outs, scratch=(), table=None, flops=0, after=()):
    def run(*refs):
        refs = list(refs)
        lead = [refs.pop(0)] if table is not None else []
        loads = []
        for one in ins:
            ref = refs.pop(0)
            loads.append(Loaded(ref if one.index is None else ref.at[one.index]))
        del refs[: len(after)]
        held = [refs.pop(0) for _ in outs]
        kernel(*lead, loads, held, refs)

    vmem = pl.BlockSpec(memory_space=pltpu.VMEM)
    in_specs = [] if table is None else [pl.BlockSpec(memory_space=pltpu.SMEM)]
    moved = sum(int(np.prod(s.array.shape)) * s.array.dtype.itemsize for s in ins)
    got = pl.pallas_call(
        run,
        out_shape=list(outs),
        in_specs=in_specs + [vmem] * len(ins) + [pl.BlockSpec(memory_space=pl.ANY)] * len(after),
        out_specs=[vmem] * len(outs),
        scratch_shapes=list(scratch),
        compiler_params=pltpu.CompilerParams(vmem_limit_bytes=VMEM_LIMIT),
        cost_estimate=pl.CostEstimate(flops=int(flops), bytes_accessed=moved, transcendentals=0),
    )(*([] if table is None else [table]), *[one.array for one in ins], *after)
    return got if len(outs) > 1 else got[0]


def sds(shape, dtype):
    return jax.ShapeDtypeStruct(shape, dtype)


def chosen_rows(bands_ref, send_ref):
    rows, slots = bands_ref.shape[0], send_ref.shape[1]
    onehot = (iota((rows, slots), 0) == send_ref[...]).astype(F32).astype(BF16)
    return mm_tn(onehot, bands_ref[...])


def pick_kernel(loads, outs, scratch):
    send, bands = loads
    outs[0][...] = chosen_rows(bands(), send()).astype(BF16)


def pick_direct_kernel(my_ref, loads, outs, scratch):
    send, bands = loads
    held = scratch[0]
    held[...] = chosen_rows(bands(), send()).reshape(held.shape).astype(BF16)
    for s, out in enumerate(outs):
        for e in range(2):
            out[e] = held[my_ref[0] ^ (2 * s + e)]


def relay_kernel(loads, outs, scratch):
    for i, one in enumerate(loads):
        outs[0][i] = one()[...]


def spread(weights, fixed_first, pix):
    width = pix * GROUP
    shape = (pix * pix, pix * width)
    r, c = iota(shape, 0), iota(shape, 1)
    outer, inner = c // width, (c % width) // GROUP
    if fixed_first:
        sel = (r // pix == outer) & (r % pix == inner)
    else:
        sel = (r % pix == outer) & (r // pix == inner)
    out = mm(weights, sel.astype(F32).astype(BF16))
    own = iota(out.shape, 0) % GROUP == iota(out.shape, 1) % GROUP
    return jnp.where(own, out, 0.0)


def store_spread(out_ref, value, row0, col0, pix):
    groups = value.shape[0] // GROUP
    width = pix * GROUP
    for o in range(0, pix, 2):
        lo = value[:, o * width : (o + 1) * width].reshape(groups, GROUP, width)
        hi = value[:, (o + 1) * width : (o + 2) * width].reshape(groups, GROUP, width)
        both = jnp.concatenate([lo, hi], axis=1).astype(BF16)
        out_ref[:, row0 + o * GROUP : row0 + (o + 2) * GROUP, col0 : col0 + width] = both


def tile_move(ch, j, total):
    lo = (ch * j // LANES) * LANES
    hi = min(lo + 2 * LANES, total)
    shape = (hi - lo, LANES)
    move = (iota(shape, 0) - (ch * j - lo) == iota(shape, 1)) & (iota(shape, 1) < ch)
    return lo, hi, move.astype(F32).astype(BF16)


def weights_by_slot(recv, weight, slots, level):
    pixsq = weight.shape[1] // recv.shape[0]
    r = iota((slots, recv.shape[1]), 0)
    total = None
    for k in (2 * level, 2 * level + 1):
        hit = (recv[k : k + 1, :] == r).astype(F32).astype(BF16)
        term = mm(hit, weight[:, k * pixsq : (k + 1) * pixsq])
        total = term if total is None else total + term
    return total


def over(values, size):
    return jnp.floor((values.astype(F32) + 0.5) * (1.0 / size)).astype(jnp.int32)


def bias_rows(rel_ref, tab_ref, out_ref):
    heads, blocks, entries = rel_ref.shape
    span = WIN * WIN
    half = WIN // 2

    def row_col(pos):
        side = pos // (span // 2)
        return (pos % (span // 2)) // half, side * half + pos % half

    shape = (span, LANES)
    ra, ca = row_col(iota(shape, 0))
    rb, cb = row_col(iota(shape, 1) % span)
    index = (ra - rb + WIN - 1) * (2 * WIN - 1) + ca - cb + WIN - 1
    low = jnp.minimum(index, LANES - 1)
    high = jnp.maximum(index - LANES, 0)
    first = iota(shape, 1) < span
    for b in range(blocks):
        for h in range(heads):
            tab_ref[h : h + 1, :entries] = rel_ref[h, b : b + 1, :]
        for m in range(heads // 2):
            both = []
            for h in (2 * m, 2 * m + 1):
                lo = jnp.broadcast_to(tab_ref[h : h + 1, :LANES], shape)
                hi = jnp.broadcast_to(tab_ref[h : h + 1, LANES:], shape)
                got_lo = jnp.take_along_axis(lo, low, axis=1, mode="promise_in_bounds")
                got_hi = jnp.take_along_axis(hi, high, axis=1, mode="promise_in_bounds")
                both.append(jnp.where(index < LANES, got_lo, got_hi))
            out_ref[b, :, m * LANES : (m + 1) * LANES] = jnp.where(first, both[0], both[1])


def weights_kernel(loads, outs, scratch):
    recv, weight = (one() for one in loads)
    slots = 2 * recv.shape[1]
    pixsq = weight.shape[1] // recv.shape[0]
    totals = [weights_by_slot(recv, weight, slots, v).reshape(slots // GROUP, GROUP, pixsq) for v in range(2)]
    outs[0][...] = jnp.concatenate(totals, axis=1).reshape(2 * slots, pixsq).astype(BF16)


def split_slots(recv, cap, me):
    slot = recv[...]
    sender = over(slot, cap)
    inner = slot - sender * cap
    return sender ^ me, inner


def patch_turn(pd):
    half = WIN // 2
    r, c = iota((pd, pd), 0), iota((pd, pd), 1)
    side, rest = r // (ROWS * half), r % (ROWS * half)
    return ((rest // half) * WIN + side * half + rest % half == c).astype(F32).astype(BF16)


def chosen(shape, axis, row0, vals):
    r = iota(shape, axis) + row0
    slot = (r // (2 * GROUP)) * GROUP + r % GROUP
    level = (r // GROUP) % 2
    first = (vals(0) == slot) | (vals(1) == slot)
    second = (vals(2) == slot) | (vals(3) == slot)
    hit = (first & (level == 0)) | (second & (level == 1))
    return hit.astype(F32).astype(BF16)


def prep_kernel(cap, me_ref, loads, outs, scratch):
    recv, weight, embed, rel = (one() for one in loads)
    mix_ref, scatter_ref, embed_out, bias_ref, select_ref = outs
    kk, pd = recv.shape
    slots = 2 * pd
    pixsq = weight.shape[1] // kk
    pix = int(round(pixsq**0.5))
    ch = embed.shape[0] // pix
    sender, inner = split_slots(recv, cap, me_ref[0])
    slot = sender * cap + inner
    for level in range(2):
        total = weights_by_slot(slot, weight, slots, level)
        store_spread(mix_ref, spread(total.astype(BF16), True, pix), level * pix * GROUP, 0, pix)
    turn = patch_turn(pd)
    parts = [v.astype(F32).astype(BF16) for v in (sender, inner)]
    cols = (mm_nt(turn, parts[0]) * cap + mm_nt(turn, parts[1])).astype(jnp.int32)
    rows = (mm_nt(parts[0], turn) * cap + mm_nt(parts[1], turn)).astype(jnp.int32)
    select_ref[...] = chosen((2 * slots, pd), 0, 0, lambda k: rows[k : k + 1, :])
    stages, _, width = scatter_ref.shape
    for stage in range(stages):
        scatter_ref[stage] = chosen((pd, width), 1, stage * width, lambda k: cols[:, k : k + 1])
    for i in range(pix):
        lo, hi, move = tile_move(ch, i, embed.shape[0])
        embed_out[i * LANES : (i + 1) * LANES, :] = mm_tn(move, embed[lo:hi, :]).astype(BF16)
    bias_rows(rel, scratch[0], bias_ref)


def prep_back_kernel(loads, outs, scratch):
    weight_ref, unembed = (one() for one in loads)
    mix_ref, unembed_out = outs
    rows, pixsq = weight_ref.shape
    pix = int(round(pixsq**0.5))
    ch = unembed.shape[0] // pix
    groups = rows // (2 * GROUP)
    w3 = weight_ref[...].astype(F32).reshape(groups, 2, GROUP, pixsq)
    for level in range(2):
        w_l = w3[:, level].reshape(groups * GROUP, pixsq).astype(BF16)
        store_spread(mix_ref, spread(w_l, False, pix), 0, level * pix * GROUP, pix)
    for i in range(pix):
        lo, hi, move = tile_move(ch, i, unembed.shape[0])
        unembed_out[i * LANES : (i + 1) * LANES, :] = mm_tn(move, unembed[lo:hi, :]).astype(BF16)


def layer_norm(values, gain):
    average = jnp.mean(values, axis=-1, keepdims=True)
    centred = values - average
    spread_ = jnp.mean(centred * centred, axis=-1, keepdims=True)
    return centred * lax.rsqrt(spread_ + norm_eps) * gain


def head_mask(heads, span, d):
    head_of = iota((heads * span, d), 0) // span == iota((heads * span, d), 1) // (d // heads)
    return head_of.astype(F32).astype(BF16)


def softmax_parts(scores, side):
    out = []
    for m in range(scores.shape[1] // LANES):
        part = scores[:, m * LANES : (m + 1) * LANES]
        low = iota(part.shape, 1) % LANES < side
        top_lo = jnp.max(jnp.where(low, part, -3e38), axis=-1, keepdims=True)
        top_hi = jnp.max(jnp.where(low, -3e38, part), axis=-1, keepdims=True)
        out.append(jnp.exp(part - jnp.where(low, top_lo, top_hi)))
    return jnp.concatenate(out, axis=1)


def attend_rows(query, key, value, bias, heads, mask, blocked):
    d = query.shape[1]
    key_all = jnp.concatenate([key] * heads, axis=0) * mask
    value_all = jnp.concatenate([value] * heads, axis=0) * mask
    scores = mm_nt(query, key_all) * (d // heads) ** (-0.5) + bias
    if blocked is not None:
        scores = jnp.where(blocked, -1e30, scores)
    weights = softmax_parts(scores, key.shape[0]).astype(BF16)
    return mm(weights, value_all), weights


def feed_forward(residual, gain2, up, down):
    normed = layer_norm(residual, gain2).astype(BF16)
    hidden = jax.nn.gelu(mm(normed, up)).astype(BF16)
    return (residual + mm(hidden, down)).astype(BF16)


def lay_tiles(rows, count):
    return jnp.concatenate([rows[:, t * LANES : (t + 1) * LANES] for t in range(count)], axis=0)


def joined(chunks):
    pieces = [one()[...].astype(F32).reshape(-1, one.ref.shape[-1]) for one in chunks]
    return jnp.concatenate(pieces, axis=0).astype(BF16)


def regrid_part(data, x_ref, c_ref, mix, scatter, embed, pix):
    slots, width = data.shape
    ch = width // pix
    for j in range(pix):
        lo, hi, move = tile_move(ch, j, width)
        x_ref[:, j * LANES : (j + 1) * LANES] = mm(data[:, lo:hi], move)
    mix_ref = mix()

    def group(g, carry):
        tiles = lay_tiles(x_ref[pl.ds(pl.multiple_of(g * GROUP, GROUP), GROUP), :], pix).astype(BF16)
        out = mm(mix_ref[g], tiles)
        to = pl.ds(pl.multiple_of(g * 2 * GROUP, 2 * GROUP), 2 * GROUP)
        for i in range(pix):
            low = out[i * GROUP : (i + 1) * GROUP]
            high = out[(pix + i) * GROUP : (pix + i + 1) * GROUP]
            both = jnp.concatenate([low, high], axis=0).astype(BF16)
            c_ref[to, i * LANES : (i + 1) * LANES] = both
        return carry

    lax.fori_loop(0, slots // GROUP, group, 0, unroll=4)
    scatter_ref, embed_ref = scatter(), embed()
    total = None
    for j in range(0, pix, 2):
        cols = slice(j * LANES, (j + 2) * LANES)
        pixels = mm(scatter_ref[...], c_ref[:, cols])
        term = mm(pixels.astype(BF16), embed_ref[cols, :])
        total = term if total is None else total + term
    return total


def early_kernel(pix, loads, outs, scratch):
    *chunks, mix, scatter, embed = loads
    outs[0][...] = regrid_part(joined(chunks), *scratch, mix, scatter, embed, pix)


def first_kernel(pix, layer, loads, outs, scratch):
    *chunks, mix, scatter, embed, prior, gain1, gain2, qkv, bias, proj, up, down = loads
    total = regrid_part(joined(chunks), *scratch, mix, scatter, embed, pix)
    state = (prior()[...] + total).astype(BF16).astype(F32)
    pd, d = state.shape
    heads = bias.ref.shape[1] // (WIN * WIN)
    normed = layer_norm(state, gain1()[layer : layer + 1, :]).astype(BF16)
    packed = mm(normed, qkv()[...]).astype(BF16)
    query, key, value = packed[:, :d], packed[:, d : 2 * d], packed[:, 2 * d :]
    half = pd // 2
    win_rows = ROWS // WIN
    part_rows = half // win_rows
    bias_all = bias()[...]
    mask = head_mask(heads, WIN * WIN, d)
    mixed = [None] * (2 * win_rows)
    weights = [None] * (2 * win_rows)
    for w in range(win_rows):
        def rows(v):
            lo, hi = w * part_rows, (w + 1) * part_rows
            return jnp.concatenate([v[lo:hi], v[half + lo : half + hi]], axis=0)

        out, wts = attend_rows(rows(query), rows(key), rows(value), bias_all, heads, mask, None)
        mixed[w], mixed[win_rows + w] = out[:part_rows], out[part_rows:]
        weights[w], weights[win_rows + w] = wts[:part_rows], wts[part_rows:]
    total = mm(jnp.concatenate(weights, axis=0), mask)
    mixed = (jnp.concatenate(mixed, axis=0) / total).astype(BF16)
    attended = mm(mixed, proj()[...]).astype(BF16)
    residual = state + attended.astype(F32)
    new = feed_forward(residual, gain2()[layer : layer + 1, :], up()[...], down()[...])
    outs[0][...] = new[:half]
    outs[1][...] = new[half:]


def second_kernel(layer, loads, outs, scratch):
    low, high, gain1, gain2, qkv, bias, left, right, proj, up, down, select = loads
    half, d = low.ref.shape
    heads = bias.ref.shape[1] // (WIN * WIN)
    shift = half * (WIN // 2) // ROWS
    turn = lambda v: jnp.concatenate([v[shift:], v[:shift]], axis=0)
    back = lambda v: jnp.concatenate([v[half - shift :], v[: half - shift]], axis=0)
    own = jnp.concatenate([turn(low()[...]), turn(high()[...])], axis=0).astype(F32)
    gain = gain1()[layer : layer + 1, :]
    normed = layer_norm(own, gain).astype(BF16)
    strips = jnp.concatenate([turn(left()[...]), turn(right()[...])], axis=0).astype(F32)
    normed_s = layer_norm(strips, gain).astype(BF16)
    packed = mm(normed, qkv()[...]).astype(BF16)
    packed_s = mm(normed_s, qkv()[:, d:]).astype(BF16)
    query, key, value = packed[:, :d], packed[:, d : 2 * d], packed[:, 2 * d :]
    key_s, value_s = packed_s[:, :d], packed_s[:, d:]
    win_rows = ROWS // WIN
    part = half // win_rows
    span = WIN * WIN
    bias_all = bias()[...]
    mask = head_mask(heads, span, d)
    outs_m, outs_w = [[], []], [[], []]
    for w in range(win_rows):
        near = slice(w * part, (w + 1) * part)
        far = slice(half + w * part, half + (w + 1) * part)
        for side in range(2):
            if side == 0:
                q = query[near]
                k = jnp.concatenate([key_s[near], key[near]], axis=0)
                v = jnp.concatenate([value_s[near], value[near]], axis=0)
                b = bias_all[part:]
            else:
                q = query[far]
                k = jnp.concatenate([key[far], key_s[far]], axis=0)
                v = jnp.concatenate([value[far], value_s[far]], axis=0)
                b = bias_all[:part]
            blocked = None
            if w == win_rows - 1:
                shape = (part, heads * span)
                q_up = iota(shape, 0) % part >= part // 2
                k_up = iota(shape, 1) % part >= part // 2
                blocked = q_up != k_up
            out, wts = attend_rows(q, k, v, b, heads, mask, blocked)
            outs_m[side].append(out)
            outs_w[side].append(wts)
    total = mm(jnp.concatenate(outs_w[0] + outs_w[1], axis=0), mask)
    mixed = (jnp.concatenate(outs_m[0] + outs_m[1], axis=0) / total).astype(BF16)
    attended = mm(mixed, proj()[...]).astype(BF16)
    residual = own + attended.astype(F32)
    new = feed_forward(residual, gain2()[layer : layer + 1, :], up()[...], down()[...])
    state = jnp.concatenate([back(new[:half]), back(new[half:])], axis=0)
    sent = mm(select()[...], state).astype(BF16)
    if len(outs) == 1:
        outs[0][...] = sent
        return
    rows = sent.shape[0] // (2 * len(outs))
    for x in range(2 * len(outs)):
        outs[x // 2][x % 2] = sent[x * rows : (x + 1) * rows]


def back_part(size, first, me_ref, chunks, mix, unembed, p_ref, slot_ref):
    rows = jnp.concatenate([one()[...].reshape(-1, one.ref.shape[-1]) for one in chunks], axis=0)
    unembed_ref = unembed()
    pix = unembed_ref.shape[0] // LANES
    for j in range(0, pix, 2):
        cols = slice(j * LANES, (j + 2) * LANES)
        p_ref[:, cols] = mm_nt(rows, unembed_ref[cols, :])
    mix_ref = mix()

    def group(g, carry):
        got = p_ref[pl.ds(pl.multiple_of(g * 2 * GROUP, 2 * GROUP), 2 * GROUP), :]
        data = jnp.concatenate([lay_tiles(got[:GROUP], pix), lay_tiles(got[GROUP:], pix)], axis=0)
        where = first + g
        if size is not None:
            chunk = lax.div(where, size)
            where = (chunk ^ me_ref[0]) * size + where - chunk * size
        out = mm(mix_ref[where], data.astype(BF16))
        to = pl.ds(pl.multiple_of(g * GROUP, GROUP), GROUP)
        for i in range(pix):
            slot_ref[to, i * LANES : (i + 1) * LANES] = out[i * GROUP : (i + 1) * GROUP]
        return carry

    lax.fori_loop(0, rows.shape[0] // (2 * GROUP), group, 0, unroll=4)


def back_kernel(size, first, me_ref, loads, outs, scratch):
    *chunks, unembed, mix = loads
    back_part(size, first, me_ref, chunks, mix, unembed, *scratch)
    outs[0][...] = scratch[1][...].astype(BF16)


def last_kernel(size, first, me_ref, loads, outs, scratch):
    *chunks, unembed, mix, prior, send = loads
    back_part(size, first, me_ref, chunks, mix, unembed, *scratch)
    slot_ref, out_ref = scratch[1], outs[0]
    pix = unembed.ref.shape[0] // LANES
    pd, total = out_ref.shape
    ch = total // pix
    prior_ref = prior()
    owner = jnp.broadcast_to(send()[...], (GROUP, send.ref.shape[1]))
    if size is not None:
        cap = size * GROUP
        count = owner.shape[1] // cap
        chunk = over(iota(owner.shape, 1), cap)
        for bit in range(count.bit_length() - 1):
            gap = cap << bit
            up = pltpu.roll(owner, owner.shape[1] - gap, 1)
            down = pltpu.roll(owner, gap, 1)
            swapped = jnp.where((chunk >> bit) & 1 == 0, up, down)
            owner = jnp.where((me_ref[0] >> bit) & 1 == 1, swapped, owner)
    onehot = (iota((pd, owner.shape[1]), 0) == owner[:1]).astype(F32).astype(BF16)
    tiles = [None] * (-(-total // LANES))
    for j in range(0, pix, 2):
        cols = slice(j * LANES, (j + 2) * LANES)
        slots = jnp.concatenate([prior_ref[:, cols], slot_ref[:, cols].astype(BF16)], axis=0)
        both = mm(onehot, slots)
        for jj in (j, j + 1):
            val = both[:, (jj - j) * LANES : (jj - j + 1) * LANES]
            t, off = divmod(ch * jj, LANES)
            if off:
                val = pltpu.roll(val, off, 1)
            lane = iota(val.shape, 1)
            low, high = jnp.where(lane >= off, val, 0.0), jnp.where(lane < off, val, 0.0)
            for tt, piece in ((t, low), (t + 1, high)):
                if tt == t + 1 and off + ch <= LANES:
                    continue
                tiles[tt] = piece if tiles[tt] is None else tiles[tt] + piece
    for t, tile in enumerate(tiles):
        hi = min((t + 1) * LANES, total)
        out_ref[:, t * LANES : hi] = tile[:, : hi - t * LANES]


def swap(value, axis):
    return lax.all_to_all(value, axis, split_axis=0, concat_axis=0, tiled=True)


def swap_pairs(value, axis):
    count = lax.axis_size(axis)
    rows, width = value.shape
    cap = rows // (2 * count)
    if cap % GROUP == 0:
        return swap(value, axis)
    groups = rows // (2 * GROUP)
    v = value.reshape(groups, 2, GROUP, width).transpose(1, 0, 2, 3).reshape(2, count, cap, width)
    v = swap(v.transpose(1, 0, 2, 3).reshape(rows, width), axis)
    v = v.reshape(count, 2, cap, width).transpose(1, 0, 2, 3).reshape(2, groups, GROUP, width)
    return v.transpose(1, 0, 2, 3).reshape(rows, width)


def flip(value, axis, bits):
    count = lax.axis_size(axis)
    return lax.ppermute(value, axis, [(source, source ^ bits) for source in range(count)])


def from_behind(value, axis, steps):
    count = lax.axis_size(axis)
    pairs = [(source, (source + steps) % count) for source in range(count)]
    return lax.ppermute(value, axis, pairs)


STAGES = 2
NEAR = 4


def body(
    bands, send_table, recv_table, regrid_weight, embed_weight, norm1_gain, qkv_weight, rel_bias,
    proj_weight, norm2_gain, up_weight, down_weight, unembed_weight,
):
    pd, width = bands.shape
    slots = send_table.shape[1]
    kk = recv_table.shape[0]
    d = embed_weight.shape[1]
    pixsq = regrid_weight.shape[1] // kk
    pix = int(round(pixsq**0.5))
    wide = pix * LANES
    count = lax.axis_size("tile")
    cap = slots // count
    chips = count // 2
    direct = chips == 2 * NEAR and cap % GROUP == 0
    vm = pltpu.VMEM
    per = slots // STAGES
    groups = per // GROUP
    my = lax.axis_index("tile").astype(jnp.int32).reshape(1)
    if not direct:
        my = my * 0

    if direct:
        turns = [*range(NEAR, chips), *range(NEAR - 1, 0, -1)]

        outgoing = call(pick_direct_kernel, [In(send_table), In(bands)],
                        [sds((2, cap, width), BF16)] * chips, [vm((count, cap, width), BF16)], my)
        came = [outgoing[0]] + [None] * (chips - 1)
        for s in turns:
            came[s] = flip(outgoing[s], "tile", 2 * s)
    else:
        outgoing = call(pick_kernel, [In(send_table), In(bands)], [sds((slots, width), BF16)])
        incoming = swap(outgoing, "tile").reshape(STAGES, per, width)

    heads = rel_bias.shape[1]
    span = WIN * WIN
    wsend = call(weights_kernel, [In(recv_table), In(regrid_weight)], [sds((2 * slots, pixsq), BF16)],
                 flops=2e8)
    wback = swap_pairs(wsend, "tile")
    mix, scatter, embed_pad, bias, select = call(
        functools.partial(prep_kernel, cap),
        [In(recv_table), In(regrid_weight), In(embed_weight), In(rel_bias.transpose(1, 0, 2))],
        [sds((slots // GROUP, 2 * pix * GROUP, pix * GROUP), BF16), sds((STAGES, pd, 2 * per), BF16),
         sds((wide, d), BF16), sds((rel_bias.shape[0], span, heads * span), F32),
         sds((2 * slots, pd), BF16)],
        [vm((heads, 2 * LANES), F32)], my, flops=4e9, after=[wsend])

    def relay(arrays, after=()):
        shape = (len(arrays), *arrays[0].shape[1:])
        return call(relay_kernel, [at(x, 1) for x in arrays], [sds(shape, BF16)], after=after)

    def mix_rows(stage):
        return In(mix, slice(stage * groups, (stage + 1) * groups))

    regrid_scratch = [vm((per, wide), F32), vm((2 * per, wide), BF16)]
    if direct:
        near_all = relay(came[:NEAR], [wsend])
        near_pass = flip(near_all, "tile", 1)
        near = [y for i, x in enumerate(came[:NEAR]) for y in (at(x, 0), at(near_pass, i))]
    else:
        near, far = [at(incoming, 0)], [at(incoming, 1)]
    total = call(functools.partial(early_kernel, pix),
                 [*near, mix_rows(0), at(scatter, 0), In(embed_pad)], [sds((pd, d), F32)], regrid_scratch, flops=2e9)
    if direct:
        far_pass = flip(relay(came[NEAR:], [total]), "tile", 1)
        far = [y for i, x in enumerate(came[NEAR:]) for y in (at(x, 0), at(far_pass, i))]

    def layer(n):
        return [In(norm1_gain), In(norm2_gain), at(qkv_weight, n), at(bias, n)], [
            at(proj_weight, n), at(up_weight, n), at(down_weight, n)]

    half = pd // 2
    ins_a, ins_b = layer(0)
    low, high = call(
        functools.partial(first_kernel, pix, 0),
        [*far, mix_rows(1), at(scatter, 1), In(embed_pad), In(total), *ins_a, *ins_b],
        [sds((half, d), BF16)] * 2, regrid_scratch, flops=4e9)
    right = from_behind(low, "tile", -1)
    left = from_behind(high, "tile", 1)
    ins_a, ins_b = layer(1)
    rows = 2 * cap
    sent = call(
        functools.partial(second_kernel, 1),
        [In(low), In(high), *ins_a, In(left), In(right), *ins_b, In(select)],
        [sds((2, rows, d), BF16)] * chips if direct else [sds((2 * slots, d), BF16)], flops=2e9)
    one_sent = sent[0] if direct else sent
    mix_back, unembed_pad = call(
        prep_back_kernel, [In(wback), In(unembed_weight.T)],
        [sds((slots // GROUP, pix * GROUP, 2 * pix * GROUP), BF16), sds((wide, d), BF16)], flops=2e9, after=[one_sent])

    size = cap // GROUP if direct else None
    back_scratch = [vm((2 * per, wide), F32), vm((per, wide), F32)]
    if direct:
        got = [sent[0]] + [None] * (chips - 1)
        for s in turns:
            got[s] = flip(sent[s], "tile", 2 * s)
        near_pass = flip(relay(got[:NEAR]), "tile", 1)
        near = [y for i, x in enumerate(got[:NEAR]) for y in (at(x, 0), at(near_pass, i))]
    else:
        got = swap_pairs(sent, "tile").reshape(STAGES, 2 * per, d)
        near, far = [at(got, 0)], [at(got, 1)]
    prior = call(functools.partial(back_kernel, size, 0), [*near, In(unembed_pad), In(mix_back)],
                 [sds((per, wide), BF16)], back_scratch, my, flops=2e9)
    if direct:
        far_pass = flip(relay(got[NEAR:], [prior]), "tile", 1)
        far = [y for i, x in enumerate(got[NEAR:]) for y in (at(x, 0), at(far_pass, i))]
    return call(functools.partial(last_kernel, size, groups), [*far, In(unembed_pad), In(mix_back), In(prior), In(send_table)],
                [sds((pd, width), F32)], back_scratch, my, flops=3e9)


def solution(mesh):
    in_specs = (
        P(("groups", "tile"), None), P("tile", None), P(None, "tile"), P("tile", None),
        P(), P(), P(), P(), P(), P(), P(), P(), P(),
    )
    out_specs = P(("groups", "tile"), None)
    return jax.shard_map(body, mesh=mesh, in_specs=in_specs, out_specs=out_specs, check_vma=False)
```

profile of v0, /device:TPU:0, one launch (start us, length us, event | category | flops | bytes accessed | tf_op | source)
XLA Modules:
  0.0 95.5 jit_solution(1079933019913679255)
XLA Ops:
  0.0 1.1 %copy-done.5 = bf16[192,1312]{1,0:T(8,128)(2,1)S(1)} copy-done((bf16[192,1312]{1,0:T(8,128)(2,1)S(1)}, bf16[192,1312]{1,0:T(8,128)(2,1)}, u32[]{:S(2)}) %copy-start.5) | copy-done | bytes 503832
  1.1 0.7 copy-done.22
  1.7 0.6 shard_map.127
  2.3 3.1 %collective-permute-start.4 = (bf16[2,24,1312]{2,1,0:T(8,128)(2,1)S(1)}, bf16[2,24,1312]{2,1,0:T(8,128)(2,1)S(1)}, u32[]{:S(2)}, u32[]{:S(2)}) collective-permute-start(bf16[2,24,1312]{2,1,0:T(8,128)(2,1)S(1)} %get-tuple-element.35), channel_id=1, source_target_pairs={{0,2},{1,3},{2,0},{3,1},{4,6},{5,7},{6,4},{7,5},{8,10},{9,11},{10,... | collective-permute-start | bytes 377864 | tf_op jit(solution)/shard_map/ppermute | solution.py:535
  5.4 1.6 %collective-permute-start.5 = (bf16[2,24,1312]{2,1,0:T(8,128)(2,1)S(1)}, bf16[2,24,1312]{2,1,0:T(8,128)(2,1)S(1)}, u32[]{:S(2)}, u32[]{:S(2)}) collective-permute-start(bf16[2,24,1312]{2,1,0:T(8,128)(2,1)S(1)} %get-tuple-element.36), channel_id=1, source_target_pairs={{0,4},{1,5},{2,6},{3,7},{4,0},{5,1},{6,2},{7,3},{8,12},{9,13},{10,... | collective-permute-start | bytes 377864 | tf_op jit(solution)/shard_map/ppermute | solution.py:535
  7.0 3.0 %collective-permute-start = (bf16[2,24,1312]{2,1,0:T(8,128)(2,1)S(1)}, bf16[2,24,1312]{2,1,0:T(8,128)(2,1)S(1)}, u32[]{:S(2)}, u32[]{:S(2)}) collective-permute-start(bf16[2,24,1312]{2,1,0:T(8,128)(2,1)S(1)} %get-tuple-element.30), channel_id=1, source_target_pairs={{0,8},{1,9},{2,10},{3,11},{4,12},{5,13},{6,14},{7,15},{8,0},{9,1},... | collective-permute-start | bytes 377864 | tf_op jit(solution)/shard_map/ppermute | solution.py:535
  9.9 1.3 %collective-permute-start.1 = (bf16[2,24,1312]{2,1,0:T(8,128)(2,1)S(1)}, bf16[2,24,1312]{2,1,0:T(8,128)(2,1)S(1)}, u32[]{:S(2)}, u32[]{:S(2)}) collective-permute-start(bf16[2,24,1312]{2,1,0:T(8,128)(2,1)S(1)} %get-tuple-element.31), channel_id=1, source_target_pairs={{0,10},{1,11},{2,8},{3,9},{4,14},{5,15},{6,12},{7,13},{8,2},{9,3},... | collective-permute-start | bytes 377864 | tf_op jit(solution)/shard_map/ppermute | solution.py:535
  11.2 1.0 %copy-done.8 = bf16[192,1024]{1,0:T(8,128)(2,1)S(1)} copy-done((bf16[192,1024]{1,0:T(8,128)(2,1)S(1)}, bf16[192,1024]{1,0:T(8,128)(2,1)}, u32[]{:S(2)}) %copy-start.8) | copy-done | bytes 393240
  12.2 0.7 copy-done.18
  12.9 1.1 %shard_map.128.refs_4_.refs_5_ = bf16[768,256]{1,0:T(8,128)(2,1)} custom-call(s32[4,192]{1,0:T(4,128)S(1)} %copy-done.18, bf16[192,1024]{1,0:T(8,128)(2,1)S(1)} %copy-done.8), custom_call_target="tpu_custom_call" | custom-call | flops 200000000 | bytes 396288 | tf_op jit(solution)/shard_map/pallas_call | solution.py:74
  14.0 3.6 %collective-permute-start.2 = (bf16[2,24,1312]{2,1,0:T(8,128)(2,1)S(1)}, bf16[2,24,1312]{2,1,0:T(8,128)(2,1)S(1)}, u32[]{:S(2)}, u32[]{:S(2)}) collective-permute-start(bf16[2,24,1312]{2,1,0:T(8,128)(2,1)S(1)} %get-tuple-element.32), channel_id=1, source_target_pairs={{0,12},{1,13},{2,14},{3,15},{4,8},{5,9},{6,10},{7,11},{8,4},{9,5},... | collective-permute-start | bytes 377864 | tf_op jit(solution)/shard_map/ppermute | solution.py:535
  17.6 0.0 collective-permute-start.3
  17.7 0.1 collective-permute-start.7
  17.8 1.2 %copy-done.24 = bf16[1312,384]{1,0:T(8,128)(2,1)S(1)} copy-done((bf16[1312,384]{1,0:T(8,128)(2,1)S(1)}, bf16[1312,384]{1,0:T(8,128)(2,1)}, u32[]{:S(2)}) %copy-start.24) | copy-done | bytes 1007640
  19.0 2.7 %shard_map.130 = (bf16[48,256,128]{2,1,0:T(8,128)(2,1)S(1)}, bf16[2,192,384]{2,1,0:T(8,128)(2,1)S(1)}, bf16[2048,384]{1,0:T(8,128)(2,1)S(1)}, f32[2,64,768]{2,1,0:T(8,128)S(1)}, bf16[768,192]{1,0:T(8,128)(2,1)S(1)}) custom-call(s32[1]{0:T(128)} %bitcast.refs_0_, s32[4,192]{1,0:T(4,128)S(1)} %copy-done.19, bf16[192,1024]{1,0:T(8,128)(2,1)S(1)} %copy-done.9, ...), custom_call_target="tpu_custom_call" | custom-call | flops 4000000000 | bytes 1425504 | tf_op jit(solution)/shard_map/pallas_call | solution.py:74
  21.8 0.0 copy-start.4
  21.9 3.8 %shard_map.131.refs_4_.refs_11_ = f32[192,384]{1,0:T(8,128)S(1)} custom-call(bf16[2,24,1312]{2,1,0:T(8,128)(2,1)S(1)} %get-tuple-element.34.refs_0_, bf16[4,24,1312]{2,1,0:T(8,128)(2,1)S(1)} %collective-permute-done.7.refs_1_.refs_3_.refs_5_.refs_7_, bf16[2,24,1312]{2,1,0:T(8,128)(2,1)S(1)} %collective-permute-done.4.refs_1_.refs_2_, ...), custom_call_target="tpu_custom_call" | custom-call | flops 2000000000 | bytes 6524928 | tf_op jit(solution)/shard_map/pallas_call | solution.py:74
  25.7 4.1 %collective-permute-done.1.refs_1_.refs_2_ = bf16[2,24,1312]{2,1,0:T(8,128)(2,1)S(1)} collective-permute-done((bf16[2,24,1312]{2,1,0:T(8,128)(2,1)S(1)}, bf16[2,24,1312]{2,1,0:T(8,128)(2,1)S(1)}, u32[]{:S(2)}, u32[]{:S(2)}) %collective-permute-start.1) | collective-permute-done | bytes 125984 | tf_op jit(solution)/shard_map/ppermute | solution.py:535
  29.9 0.8 shard_map.132
  30.7 0.7 copy-done.10
  31.4 8.3 %all-to-all-start = ((bf16[16,48,256]{2,1,0:T(8,128)(2,1)}), bf16[16,48,256]{2,1,0:T(8,128)(2,1)}, u32[]{:S(2)}, u32[]{:S(2)}) async-start(bf16[16,48,256]{2,1,0:T(8,128)(2,1)} %bitcast.2), calls=%async_computation | async-start | bytes 786432 | tf_op jit(solution)/shard_map/all_to_all | solution.py:517
  39.8 1.7 %copy-done.1 = bf16[2,1536,384]{2,1,0:T(8,128)(2,1)S(1)} copy-done((bf16[2,1536,384]{2,1,0:T(8,128)(2,1)S(1)}, bf16[2,1536,384]{2,1,0:T(8,128)(2,1)}, u32[]{:S(2)}) %copy-start.1) | copy-done | bytes 2359320
  41.4 1.5 %copy-done.2 = bf16[2,384,1152]{2,1,0:T(8,128)(2,1)S(1)} copy-done((bf16[2,384,1152]{2,1,0:T(8,128)(2,1)S(1)}, bf16[2,384,1152]{2,1,0:T(8,128)(2,1)}, u32[]{:S(2)}) %copy-start.2) | copy-done | bytes 1769496
  42.9 1.0 %copy-done.11 = f32[192,384]{1,0:T(8,128)S(1)} copy-done((f32[192,384]{1,0:T(8,128)S(1)}, f32[192,384]{1,0:T(8,128)}, u32[]{:S(2)}) %copy-start.11) | copy-done | bytes 294936
  43.9 0.9 copy-done.13
  44.8 0.9 copy-done.15
  45.7 0.9 copy-done.17
  46.6 1.9 %copy-done.28 = bf16[48,256,128]{2,1,0:T(8,128)(2,1)S(1)} copy-done((bf16[48,256,128]{2,1,0:T(8,128)(2,1)S(1)}, bf16[48,256,128]{2,1,0:T(8,128)(2,1)}, u32[]{:S(2)}) %copy-start.28) | copy-done | bytes 3145752
  48.5 1.4 %copy-done.30 = bf16[2048,384]{1,0:T(8,128)(2,1)S(1)} copy-done((bf16[2048,384]{1,0:T(8,128)(2,1)S(1)}, bf16[2048,384]{1,0:T(8,128)(2,1)}, u32[]{:S(2)}) %copy-start.30) | copy-done | bytes 1572888
  49.9 1.0 %copy-done.32 = bf16[2,192,384]{2,1,0:T(8,128)(2,1)S(1)} copy-done((bf16[2,192,384]{2,1,0:T(8,128)(2,1)S(1)}, bf16[2,192,384]{2,1,0:T(8,128)(2,1)}, u32[]{:S(2)}) %copy-start.32) | copy-done | bytes 294936
  50.9 8.6 %shard_map.133 = (bf16[96,384]{1,0:T(8,128)(2,1)S(1)}, bf16[96,384]{1,0:T(8,128)(2,1)S(1)}) custom-call(bf16[2,24,1312]{2,1,0:T(8,128)(2,1)S(1)} %collective-permute-done.refs_0_, bf16[4,24,1312]{2,1,0:T(8,128)(2,1)} %collective-permute-done.8.refs_1_.refs_3_.refs_5_.refs_7_, bf16[2,24,1312]{2,1,0:T(8,128)(2,1)S(1)} %copy-done.13, ...), custom_call_target="tpu_custom_call" | custom-call | flops 4000000000 | bytes 14297088 | tf_op jit(solution)/shard_map/pallas_call | solution.py:74
  59.5 0.4 collective-permute-start.9
  59.9 4.2 %collective-permute-start.10 = (bf16[96,384]{1,0:T(8,128)(2,1)S(1)}, bf16[96,384]{1,0:T(8,128)(2,1)S(1)}, u32[]{:S(2)}, u32[]{:S(2)}) collective-permute-start(bf16[96,384]{1,0:T(8,128)(2,1)S(1)} %get-tuple-element.42.refs_0_), channel_id=1, source_target_pairs={{0,15},{1,0},{2,1},{3,2},{4,3},{5,4},{6,5},{7,6},{8,7},{9,8},{10,9... | collective-permute-start | bytes 221192 | tf_op jit(solution)/shard_map/ppermute | solution.py:541
  64.1 2.0 %collective-permute-done.9.refs_6_ = bf16[96,384]{1,0:T(8,128)(2,1)S(1)} collective-permute-done((bf16[96,384]{1,0:T(8,128)(2,1)S(1)}, bf16[96,384]{1,0:T(8,128)(2,1)S(1)}, u32[]{:S(2)}, u32[]{:S(2)}) %collective-permute-start.9) | collective-permute-done | bytes 73760 | tf_op jit(solution)/shard_map/ppermute | solution.py:541
  66.1 5.8 %shard_map.134 = (bf16[2,48,384]{2,1,0:T(8,128)(2,1)S(1)}, bf16[2,48,384]{2,1,0:T(8,128)(2,1)S(1)}, bf16[2,48,384]{2,1,0:T(8,128)(2,1)S(1)}, bf16[2,48,384]{2,1,...) custom-call(bf16[96,384]{1,0:T(8,128)(2,1)S(1)} %get-tuple-element.4, ...), custom_call_target="tpu_custom_call" | custom-call | flops 2000000000 | bytes 8067072 | tf_op jit(solution)/shard_map/pallas_call | solution.py:74
  71.9 0.5 collective-permute-start.16
  72.5 3.0 %collective-permute-start.17 = (bf16[2,48,384]{2,1,0:T(8,128)(2,1)S(1)}, bf16[2,48,384]{2,1,0:T(8,128)(2,1)S(1)}, u32[]{:S(2)}, u32[]{:S(2)}) collective-permute-start(bf16[2,48,384]{2,1,0:T(8,128)(2,1)S(1)} %get-tuple-element.52), channel_id=1, source_target_pairs={{0,6},{1,7},{2,4},{3,5},{4,2},{5,3},{6,0},{7,1},{8,14},{9,15},{10,... | collective-permute-start | bytes 221192 | tf_op jit(solution)/shard_map/ppermute | solution.py:535
  75.4 0.9 collective-permute-start.11
  76.3 1.5 %collective-permute-start.12 = (bf16[2,48,384]{2,1,0:T(8,128)(2,1)}, bf16[2,48,384]{2,1,0:T(8,128)(2,1)S(1)}, u32[]{:S(2)}, u32[]{:S(2)}) collective-permute-start(bf16[2,48,384]{2,1,0:T(8,128)(2,1)} %get-tuple-element.46), channel_id=1, source_target_pairs={{0,10},{1,11},{2,8},{3,9},{4,14},{5,15},{6,12},{7,13},{8,2},{9,3},... | collective-permute-start | bytes 221192 | tf_op jit(solution)/shard_map/ppermute | solution.py:535
  77.8 2.3 %collective-permute-start.13 = (bf16[2,48,384]{2,1,0:T(8,128)(2,1)}, bf16[2,48,384]{2,1,0:T(8,128)(2,1)S(1)}, u32[]{:S(2)}, u32[]{:S(2)}) collective-permute-start(bf16[2,48,384]{2,1,0:T(8,128)(2,1)} %get-tuple-element.47), channel_id=1, source_target_pairs={{0,12},{1,13},{2,14},{3,15},{4,8},{5,9},{6,10},{7,11},{8,4},{9,5},... | collective-permute-start | bytes 221192 | tf_op jit(solution)/shard_map/ppermute | solution.py:535
  80.1 2.9 %collective-permute-start.14 = (bf16[2,48,384]{2,1,0:T(8,128)(2,1)}, bf16[2,48,384]{2,1,0:T(8,128)(2,1)S(1)}, u32[]{:S(2)}, u32[]{:S(2)}) collective-permute-start(bf16[2,48,384]{2,1,0:T(8,128)(2,1)} %get-tuple-element.48), channel_id=1, source_target_pairs={{0,14},{1,15},{2,12},{3,13},{4,10},{5,11},{6,8},{7,9},{8,6},{9,7},... | collective-permute-start | bytes 221192 | tf_op jit(solution)/shard_map/ppermute | solution.py:535
  83.1 0.1 collective-permute-start.18
  83.2 1.2 %copy-done.25 = bf16[384,1312]{0,1:T(8,128)(2,1)S(1)} copy-done((bf16[384,1312]{0,1:T(8,128)(2,1)S(1)}, bf16[384,1312]{0,1:T(8,128)(2,1)}, u32[]{:S(2)}) %copy-start.25) | copy-done | bytes 1007640
  84.4 2.7 %shard_map.136 = (bf16[48,128,256]{2,1,0:T(8,128)(2,1)S(1)}, bf16[2048,384]{1,0:T(8,128)(2,1)S(1)}) custom-call(bf16[768,256]{1,0:T(8,128)(2,1)} %bitcast.3.refs_0_, bf16[1312,384]{1,0:T(8,128)(2,1)S(1)} %bitcast.5, bf16[2,48,384]{2,1,0:T(8,128)(2,1)S(1)} %get-tuple-element.49.refs_0_.refs_2_.refs_1_), custom_call_target="tpu_custom_call" | custom-call | flops 2000000000 | bytes 1400832 | tf_op jit(solution)/shard_map/pallas_call | solution.py:74
  87.1 2.5 %shard_map.137.refs_4_.refs_11_ = bf16[192,2048]{1,0:T(8,128)(2,1)S(1)} custom-call(s32[1]{0:T(128)} %bitcast.refs_0_, bf16[2,48,384]{2,1,0:T(8,128)(2,1)S(1)} %get-tuple-element.49.refs_0_.refs_2_.refs_1_, bf16[4,48,384]{2,1,0:T(8,128)(2,1)S(1)} %collective-permute-done.18.refs_2_.refs_4_.refs_6_.refs_8_, ...), custom_call_target="tpu_custom_call" | custom-call | flops 2000000000 | bytes 5603328 | tf_op jit(solution)/shard_map/pallas_call | solution.py:74
  89.7 0.6 collective-permute-start.19
  90.2 1.0 %collective-permute-done.19.refs_2_.refs_4_.refs_6_.refs_8_ = bf16[4,48,384]{2,1,0:T(8,128)(2,1)S(1)} collective-permute-done((bf16[4,48,384]{2,1,0:T(8,128)(2,1)S(1)}, bf16[4,48,384]{2,1,0:T(8,128)(2,1)S(1)}, u32[]{:S(2)}, u32[]{:S(2)}) %collective-permute-start.19) | collective-permute-done | bytes 147488 | tf_op jit(solution)/shard_map/ppermute | solution.py:535
  91.2 4.3 %shard_map.139 = f32[192,1312]{1,0:T(8,128)} custom-call(s32[1]{0:T(128)} %bitcast.refs_0_, bf16[2,48,384]{2,1,0:T(8,128)(2,1)S(1)} %collective-permute-done.11.refs_0_.refs_1_, bf16[4,48,384]{2,1,0:T(8,128)(2,1)S(1)} %collective-permute-done.19.refs_2_.refs_4_.refs_6_.refs_8_, bf16[2,48,384]{2,1,0:T(8,128)(2,1)S(1)} %collective-permute-done.12.refs_1_.refs_3_, ...), custom_call_target="tpu_custom_call" | custom-call | flops 3000000000 | bytes 6391296 | tf_op jit(solution)/shard_map/pallas_call | solution.py:74
  (73 shorter events, 0.2 us)
Async XLA Ops:
  0.0 17.8 %copy-start.19 = (s32[4,192]{1,0:T(4,128)S(1)}, s32[4,192]{1,0:T(4,128)}, u32[]{:S(2)}) copy-start(s32[4,192]{1,0:T(4,128)} %refs_1_.5) | copy-start | bytes 9220
  0.0 1.1 %copy-start.5 = (bf16[192,1312]{1,0:T(8,128)(2,1)S(1)}, bf16[192,1312]{1,0:T(8,128)(2,1)}, u32[]{:S(2)}) copy-start(bf16[192,1312]{1,0:T(8,128)(2,1)} %refs_2_.3) | copy-start | bytes 1511428
  1.7 16.0 %copy-start.9 = (bf16[192,1024]{1,0:T(8,128)(2,1)S(1)}, bf16[192,1024]{1,0:T(8,128)(2,1)}, u32[]{:S(2)}) copy-start(bf16[192,1024]{1,0:T(8,128)(2,1)} %refs_2_.4) | copy-start | bytes 1179652
  1.7 16.0 %copy-start.26 = (f32[2,12,225]{2,0,1:T(2,128)S(1)}, f32[2,12,225]{2,0,1:T(2,128)}, u32[]{:S(2)}) copy-start(f32[2,12,225]{2,0,1:T(2,128)} %param.20) | copy-start | bytes 64804
  2.3 11.7 %collective-permute-start.4 = (bf16[2,24,1312]{2,1,0:T(8,128)(2,1)S(1)}, bf16[2,24,1312]{2,1,0:T(8,128)(2,1)S(1)}, u32[]{:S(2)}, u32[]{:S(2)}) collective-permute-start(bf16[2,24,1312]{2,1,0:T(8,128)(2,1)S(1)} %get-tuple-element.35), channel_id=1, source_target_pairs={{0,2},{1,3},{2,0},{3,1},{4,6},{5,7},{6,4},{7,5},{8,10},{9,11},{10,... | collective-permute-start | bytes 377864 | tf_op jit(solution)/shard_map/ppermute | solution.py:535
  5.4 12.3 %collective-permute-start.5 = (bf16[2,24,1312]{2,1,0:T(8,128)(2,1)S(1)}, bf16[2,24,1312]{2,1,0:T(8,128)(2,1)S(1)}, u32[]{:S(2)}, u32[]{:S(2)}) collective-permute-start(bf16[2,24,1312]{2,1,0:T(8,128)(2,1)S(1)} %get-tuple-element.36), channel_id=1, source_target_pairs={{0,4},{1,5},{2,6},{3,7},{4,0},{5,1},{6,2},{7,3},{8,12},{9,13},{10,... | collective-permute-start | bytes 377864 | tf_op jit(solution)/shard_map/ppermute | solution.py:535
  7.0 10.7 %collective-permute-start.6 = (bf16[2,24,1312]{2,1,0:T(8,128)(2,1)S(1)}, bf16[2,24,1312]{2,1,0:T(8,128)(2,1)S(1)}, u32[]{:S(2)}, u32[]{:S(2)}) collective-permute-start(bf16[2,24,1312]{2,1,0:T(8,128)(2,1)S(1)} %get-tuple-element.37), channel_id=1, source_target_pairs={{0,6},{1,7},{2,4},{3,5},{4,2},{5,3},{6,0},{7,1},{8,14},{9,15},{10,... | collective-permute-start | bytes 377864 | tf_op jit(solution)/shard_map/ppermute | solution.py:535
  7.0 18.8 %collective-permute-start = (bf16[2,24,1312]{2,1,0:T(8,128)(2,1)S(1)}, bf16[2,24,1312]{2,1,0:T(8,128)(2,1)S(1)}, u32[]{:S(2)}, u32[]{:S(2)}) collective-permute-start(bf16[2,24,1312]{2,1,0:T(8,128)(2,1)S(1)} %get-tuple-element.30), channel_id=1, source_target_pairs={{0,8},{1,9},{2,10},{3,11},{4,12},{5,13},{6,14},{7,15},{8,0},{9,1},... | collective-permute-start | bytes 377864 | tf_op jit(solution)/shard_map/ppermute | solution.py:535
  9.9 19.9 %collective-permute-start.1 = (bf16[2,24,1312]{2,1,0:T(8,128)(2,1)S(1)}, bf16[2,24,1312]{2,1,0:T(8,128)(2,1)S(1)}, u32[]{:S(2)}, u32[]{:S(2)}) collective-permute-start(bf16[2,24,1312]{2,1,0:T(8,128)(2,1)S(1)} %get-tuple-element.31), channel_id=1, source_target_pairs={{0,10},{1,11},{2,8},{3,9},{4,14},{5,15},{6,12},{7,13},{8,2},{9,3},... | collective-permute-start | bytes 377864 | tf_op jit(solution)/shard_map/ppermute | solution.py:535
  11.2 1.0 %copy-start.8 = (bf16[192,1024]{1,0:T(8,128)(2,1)S(1)}, bf16[192,1024]{1,0:T(8,128)(2,1)}, u32[]{:S(2)}) copy-start(bf16[192,1024]{1,0:T(8,128)(2,1)} %refs_2_.4) | copy-start | bytes 1179652
  14.0 15.8 %collective-permute-start.2 = (bf16[2,24,1312]{2,1,0:T(8,128)(2,1)S(1)}, bf16[2,24,1312]{2,1,0:T(8,128)(2,1)S(1)}, u32[]{:S(2)}, u32[]{:S(2)}) collective-permute-start(bf16[2,24,1312]{2,1,0:T(8,128)(2,1)S(1)} %get-tuple-element.32), channel_id=1, source_target_pairs={{0,12},{1,13},{2,14},{3,15},{4,8},{5,9},{6,10},{7,11},{8,4},{9,5},... | collective-permute-start | bytes 377864 | tf_op jit(solution)/shard_map/ppermute | solution.py:535
  17.6 12.2 %collective-permute-start.3 = (bf16[2,24,1312]{2,1,0:T(8,128)(2,1)S(1)}, bf16[2,24,1312]{2,1,0:T(8,128)(2,1)S(1)}, u32[]{:S(2)}, u32[]{:S(2)}) collective-permute-start(bf16[2,24,1312]{2,1,0:T(8,128)(2,1)S(1)} %get-tuple-element.33), channel_id=1, source_target_pairs={{0,14},{1,15},{2,12},{3,13},{4,10},{5,11},{6,8},{7,9},{8,6},{9,7},... | collective-permute-start | bytes 377864 | tf_op jit(solution)/shard_map/ppermute | solution.py:535
  17.7 4.1 %collective-permute-start.7 = (bf16[4,24,1312]{2,1,0:T(8,128)(2,1)S(1)}, bf16[4,24,1312]{2,1,0:T(8,128)(2,1)S(1)}, u32[]{:S(2)}, u32[]{:S(2)}) collective-permute-start(bf16[4,24,1312]{2,1,0:T(8,128)(2,1)S(1)} %shard_map.129), channel_id=1, source_target_pairs={{0,1},{1,0},{2,3},{3,2},{4,5},{5,4},{6,7},{7,6},{8,9},{9,8},{10,11... | collective-permute-start | bytes 755720 | tf_op jit(solution)/shard_map/ppermute | solution.py:535
  17.8 1.2 %copy-start.24 = (bf16[1312,384]{1,0:T(8,128)(2,1)S(1)}, bf16[1312,384]{1,0:T(8,128)(2,1)}, u32[]{:S(2)}) copy-start(bf16[1312,384]{1,0:T(8,128)(2,1)} %refs_3_.2) | copy-start | bytes 3022852
  21.8 3.9 %copy-start.6 = (bf16[768,192]{1,0:T(8,128)(2,1)}, bf16[768,192]{1,0:T(8,128)(2,1)S(1)}, u32[]{:S(2)}) copy-start(bf16[768,192]{1,0:T(8,128)(2,1)S(1)} %get-tuple-element.44.refs_11_) | copy-start | bytes 884740
  21.8 3.9 %copy-start.27 = (bf16[48,256,128]{2,1,0:T(8,128)(2,1)}, bf16[48,256,128]{2,1,0:T(8,128)(2,1)S(1)}, u32[]{:S(2)}) copy-start(bf16[48,256,128]{2,1,0:T(8,128)(2,1)S(1)} %get-tuple-element.38.refs_8_) | copy-start | bytes 9437188
  21.8 3.9 %copy-start.29 = (bf16[2048,384]{1,0:T(8,128)(2,1)}, bf16[2048,384]{1,0:T(8,128)(2,1)S(1)}, u32[]{:S(2)}) copy-start(bf16[2048,384]{1,0:T(8,128)(2,1)S(1)} %get-tuple-element.40.refs_10_) | copy-start | bytes 4718596
  21.8 3.9 %copy-start.31 = (bf16[2,192,384]{2,1,0:T(8,128)(2,1)}, bf16[2,192,384]{2,1,0:T(8,128)(2,1)S(1)}, u32[]{:S(2)}) copy-start(bf16[2,192,384]{2,1,0:T(8,128)(2,1)S(1)} %get-tuple-element.39.refs_9_) | copy-start | bytes 884740
  21.8 17.9 %copy-start = (bf16[2,384,1536]{2,1,0:T(8,128)(2,1)S(1)}, bf16[2,384,1536]{2,1,0:T(8,128)(2,1)}, u32[]{:S(2)}) copy-start(bf16[2,384,1536]{2,1,0:T(8,128)(2,1)} %refs_9_.1) | copy-start | bytes 7077892
  21.8 17.9 %copy-start.4 = (bf16[2,384,384]{2,1,0:T(8,128)(2,1)S(1)}, bf16[2,384,384]{2,1,0:T(8,128)(2,1)}, u32[]{:S(2)}) copy-start(bf16[2,384,384]{2,1,0:T(8,128)(2,1)} %refs_8_.1) | copy-start | bytes 1769476
  21.8 17.9 %copy-start.20 = (f32[2,384]{1,0:T(2,128)S(1)}, f32[2,384]{1,0:T(2,128)}, u32[]{:S(2)}) copy-start(f32[2,384]{1,0:T(2,128)} %refs_2_.5) | copy-start | bytes 9220
  21.8 17.9 %copy-start.21 = (f32[2,384]{1,0:T(2,128)S(1)}, f32[2,384]{1,0:T(2,128)}, u32[]{:S(2)}) copy-start(f32[2,384]{1,0:T(2,128)} %refs_3_.3) | copy-start | bytes 9220
  29.9 1.5 %copy-start.14 = (bf16[2,24,1312]{2,1,0:T(8,128)(2,1)}, bf16[2,24,1312]{2,1,0:T(8,128)(2,1)S(1)}, u32[]{:S(2)}) copy-start(bf16[2,24,1312]{2,1,0:T(8,128)(2,1)S(1)} %collective-permute-done.2.refs_2_.refs_4_) | copy-start | bytes 377860
  29.9 1.5 %copy-start.16 = (bf16[2,24,1312]{2,1,0:T(8,128)(2,1)}, bf16[2,24,1312]{2,1,0:T(8,128)(2,1)S(1)}, u32[]{:S(2)}) copy-start(bf16[2,24,1312]{2,1,0:T(8,128)(2,1)S(1)} %collective-permute-done.3.refs_3_.refs_6_) | copy-start | bytes 377860
  31.4 8.3 %collective-permute-start.8 = (bf16[4,24,1312]{2,1,0:T(8,128)(2,1)}, bf16[4,24,1312]{2,1,0:T(8,128)(2,1)}, u32[]{:S(2)}, u32[]{:S(2)}) collective-permute-start(bf16[4,24,1312]{2,1,0:T(8,128)(2,1)} %shard_map.132), channel_id=1, source_target_pairs={{0,1},{1,0},{2,3},{3,2},{4,5},{5,4},{6,7},{7,6},{8,9},{9,8},{10,11... | collective-permute-start | bytes 755720 | tf_op jit(solution)/shard_map/ppermute | solution.py:535
  31.4 51.8 %all-to-all-start = ((bf16[16,48,256]{2,1,0:T(8,128)(2,1)}), bf16[16,48,256]{2,1,0:T(8,128)(2,1)}, u32[]{:S(2)}, u32[]{:S(2)}) async-start(bf16[16,48,256]{2,1,0:T(8,128)(2,1)} %bitcast.2), calls=%async_computation | async-start | bytes 786432 | tf_op jit(solution)/shard_map/all_to_all | solution.py:517
  39.8 1.7 %copy-start.1 = (bf16[2,1536,384]{2,1,0:T(8,128)(2,1)S(1)}, bf16[2,1536,384]{2,1,0:T(8,128)(2,1)}, u32[]{:S(2)}) copy-start(bf16[2,1536,384]{2,1,0:T(8,128)(2,1)} %refs_10_.1) | copy-start | bytes 7077892
  41.4 1.5 %copy-start.2 = (bf16[2,384,1152]{2,1,0:T(8,128)(2,1)S(1)}, bf16[2,384,1152]{2,1,0:T(8,128)(2,1)}, u32[]{:S(2)}) copy-start(bf16[2,384,1152]{2,1,0:T(8,128)(2,1)} %refs_4_.1) | copy-start | bytes 5308420
  42.9 1.0 %copy-start.11 = (f32[192,384]{1,0:T(8,128)S(1)}, f32[192,384]{1,0:T(8,128)}, u32[]{:S(2)}) copy-start(f32[192,384]{1,0:T(8,128)} %copy-done.10) | copy-start | bytes 884740
  43.9 0.9 copy-start.13
  46.6 1.9 %copy-start.28 = (bf16[48,256,128]{2,1,0:T(8,128)(2,1)S(1)}, bf16[48,256,128]{2,1,0:T(8,128)(2,1)}, u32[]{:S(2)}) copy-start(bf16[48,256,128]{2,1,0:T(8,128)(2,1)} %copy-done.27) | copy-start | bytes 9437188
  48.5 1.4 %copy-start.30 = (bf16[2048,384]{1,0:T(8,128)(2,1)S(1)}, bf16[2048,384]{1,0:T(8,128)(2,1)}, u32[]{:S(2)}) copy-start(bf16[2048,384]{1,0:T(8,128)(2,1)} %copy-done.29) | copy-start | bytes 4718596
  49.9 1.0 %copy-start.32 = (bf16[2,192,384]{2,1,0:T(8,128)(2,1)S(1)}, bf16[2,192,384]{2,1,0:T(8,128)(2,1)}, u32[]{:S(2)}) copy-start(bf16[2,192,384]{2,1,0:T(8,128)(2,1)} %copy-done.31) | copy-start | bytes 884740
  50.9 15.3 %copy-start.3 = (bf16[2,384,1152]{2,1,0:T(8,128)(2,1)S(1)}, bf16[2,384,1152]{2,1,0:T(8,128)(2,1)}, u32[]{:S(2)}) copy-start(bf16[2,384,1152]{2,1,0:T(8,128)(2,1)} %refs_4_.1) | copy-start | bytes 5308420
  50.9 15.3 %copy-start.7 = (bf16[768,192]{1,0:T(8,128)(2,1)S(1)}, bf16[768,192]{1,0:T(8,128)(2,1)}, u32[]{:S(2)}) copy-start(bf16[768,192]{1,0:T(8,128)(2,1)} %copy-done.6) | copy-start | bytes 884740
  59.5 6.6 %collective-permute-start.9 = (bf16[96,384]{1,0:T(8,128)(2,1)S(1)}, bf16[96,384]{1,0:T(8,128)(2,1)S(1)}, u32[]{:S(2)}, u32[]{:S(2)}) collective-permute-start(bf16[96,384]{1,0:T(8,128)(2,1)S(1)} %get-tuple-element.43.refs_1_), channel_id=1, source_target_pairs={{0,1},{1,2},{2,3},{3,4},{4,5},{5,6},{6,7},{7,8},{8,9},{9,10},{10,1... | collective-permute-start | bytes 221192 | tf_op jit(solution)/shard_map/ppermute | solution.py:541
  59.9 6.2 %collective-permute-start.10 = (bf16[96,384]{1,0:T(8,128)(2,1)S(1)}, bf16[96,384]{1,0:T(8,128)(2,1)S(1)}, u32[]{:S(2)}, u32[]{:S(2)}) collective-permute-start(bf16[96,384]{1,0:T(8,128)(2,1)S(1)} %get-tuple-element.42.refs_0_), channel_id=1, source_target_pairs={{0,15},{1,0},{2,1},{3,2},{4,3},{5,4},{6,5},{7,6},{8,7},{9,8},{10,9... | collective-permute-start | bytes 221192 | tf_op jit(solution)/shard_map/ppermute | solution.py:541
  71.9 5.9 %collective-permute-start.15 = (bf16[2,48,384]{2,1,0:T(8,128)(2,1)S(1)}, bf16[2,48,384]{2,1,0:T(8,128)(2,1)S(1)}, u32[]{:S(2)}, u32[]{:S(2)}) collective-permute-start(bf16[2,48,384]{2,1,0:T(8,128)(2,1)S(1)} %get-tuple-element.50), channel_id=1, source_target_pairs={{0,2},{1,3},{2,0},{3,1},{4,6},{5,7},{6,4},{7,5},{8,10},{9,11},{10,... | collective-permute-start | bytes 221192 | tf_op jit(solution)/shard_map/ppermute | solution.py:535
  71.9 8.2 %collective-permute-start.16 = (bf16[2,48,384]{2,1,0:T(8,128)(2,1)S(1)}, bf16[2,48,384]{2,1,0:T(8,128)(2,1)S(1)}, u32[]{:S(2)}, u32[]{:S(2)}) collective-permute-start(bf16[2,48,384]{2,1,0:T(8,128)(2,1)S(1)} %get-tuple-element.51), channel_id=1, source_target_pairs={{0,4},{1,5},{2,6},{3,7},{4,0},{5,1},{6,2},{7,3},{8,12},{9,13},{10,... | collective-permute-start | bytes 221192 | tf_op jit(solution)/shard_map/ppermute | solution.py:535
  72.5 10.6 %collective-permute-start.17 = (bf16[2,48,384]{2,1,0:T(8,128)(2,1)S(1)}, bf16[2,48,384]{2,1,0:T(8,128)(2,1)S(1)}, u32[]{:S(2)}, u32[]{:S(2)}) collective-permute-start(bf16[2,48,384]{2,1,0:T(8,128)(2,1)S(1)} %get-tuple-element.52), channel_id=1, source_target_pairs={{0,6},{1,7},{2,4},{3,5},{4,2},{5,3},{6,0},{7,1},{8,14},{9,15},{10,... | collective-permute-start | bytes 221192 | tf_op jit(solution)/shard_map/ppermute | solution.py:535
  75.4 14.2 %collective-permute-start.11 = (bf16[2,48,384]{2,1,0:T(8,128)(2,1)}, bf16[2,48,384]{2,1,0:T(8,128)(2,1)S(1)}, u32[]{:S(2)}, u32[]{:S(2)}) collective-permute-start(bf16[2,48,384]{2,1,0:T(8,128)(2,1)} %get-tuple-element.45), channel_id=1, source_target_pairs={{0,8},{1,9},{2,10},{3,11},{4,12},{5,13},{6,14},{7,15},{8,0},{9,1},... | collective-permute-start | bytes 221192 | tf_op jit(solution)/shard_map/ppermute | solution.py:535
  76.3 13.3 %collective-permute-start.12 = (bf16[2,48,384]{2,1,0:T(8,128)(2,1)}, bf16[2,48,384]{2,1,0:T(8,128)(2,1)S(1)}, u32[]{:S(2)}, u32[]{:S(2)}) collective-permute-start(bf16[2,48,384]{2,1,0:T(8,128)(2,1)} %get-tuple-element.46), channel_id=1, source_target_pairs={{0,10},{1,11},{2,8},{3,9},{4,14},{5,15},{6,12},{7,13},{8,2},{9,3},... | collective-permute-start | bytes 221192 | tf_op jit(solution)/shard_map/ppermute | solution.py:535
  77.8 11.8 %collective-permute-start.13 = (bf16[2,48,384]{2,1,0:T(8,128)(2,1)}, bf16[2,48,384]{2,1,0:T(8,128)(2,1)S(1)}, u32[]{:S(2)}, u32[]{:S(2)}) collective-permute-start(bf16[2,48,384]{2,1,0:T(8,128)(2,1)} %get-tuple-element.47), channel_id=1, source_target_pairs={{0,12},{1,13},{2,14},{3,15},{4,8},{5,9},{6,10},{7,11},{8,4},{9,5},... | collective-permute-start | bytes 221192 | tf_op jit(solution)/shard_map/ppermute | solution.py:535
  80.1 9.5 %collective-permute-start.14 = (bf16[2,48,384]{2,1,0:T(8,128)(2,1)}, bf16[2,48,384]{2,1,0:T(8,128)(2,1)S(1)}, u32[]{:S(2)}, u32[]{:S(2)}) collective-permute-start(bf16[2,48,384]{2,1,0:T(8,128)(2,1)} %get-tuple-element.48), channel_id=1, source_target_pairs={{0,14},{1,15},{2,12},{3,13},{4,10},{5,11},{6,8},{7,9},{8,6},{9,7},... | collective-permute-start | bytes 221192 | tf_op jit(solution)/shard_map/ppermute | solution.py:535
  83.1 4.0 %collective-permute-start.18 = (bf16[4,48,384]{2,1,0:T(8,128)(2,1)S(1)}, bf16[4,48,384]{2,1,0:T(8,128)(2,1)S(1)}, u32[]{:S(2)}, u32[]{:S(2)}) collective-permute-start(bf16[4,48,384]{2,1,0:T(8,128)(2,1)S(1)} %shard_map.135), channel_id=1, source_target_pairs={{0,1},{1,0},{2,3},{3,2},{4,5},{5,4},{6,7},{7,6},{8,9},{9,8},{10,11... | collective-permute-start | bytes 442376 | tf_op jit(solution)/shard_map/ppermute | solution.py:535
  83.2 1.2 %copy-start.25 = (bf16[384,1312]{0,1:T(8,128)(2,1)S(1)}, bf16[384,1312]{0,1:T(8,128)(2,1)}, u32[]{:S(2)}) copy-start(bf16[384,1312]{0,1:T(8,128)(2,1)} %param.25) | copy-start | bytes 3022852
  87.1 4.1 %copy-start.23 = (s32[1,384]{1,0:T(1,128)S(1)}, s32[1,384]{1,0:T(1,128)}, u32[]{:S(2)}) copy-start(s32[1,384]{1,0:T(1,128)} %refs_12_.3) | copy-start | bytes 4612
  89.7 1.6 %collective-permute-start.19 = (bf16[4,48,384]{2,1,0:T(8,128)(2,1)S(1)}, bf16[4,48,384]{2,1,0:T(8,128)(2,1)S(1)}, u32[]{:S(2)}, u32[]{:S(2)}) collective-permute-start(bf16[4,48,384]{2,1,0:T(8,128)(2,1)S(1)} %shard_map.138), channel_id=1, source_target_pairs={{0,1},{1,0},{2,3},{3,2},{4,5},{5,4},{6,7},{7,6},{8,9},{9,8},{10,11... | collective-permute-start | bytes 442376 | tf_op jit(solution)/shard_map/ppermute | solution.py:535
  (6 other events, 4.7 us)
where the time goes:
time: 96.3 us; the launch traced here: 95.5 us
  starting transfers between devices  37.2 us (39%)
  Pallas kernels  33 us (34%)
  local copies, waits for them, and re-layouts  17.7 us (18%)
  waiting for transfers between devices  7.22 us (7%)
    pallas_call x13, Pallas kernels, call(): pl.pallas_call(run, out_shape=list(outs), in_specs=in_specs + [vmem] * le...  33 us
    ppermute x18, starting transfers between devices, flip(): lax.ppermute(value, axis, [(source, source ^ bits) for source in range(co...  24.4 us
    unnamed x66, local copies, waits for them, and re-layouts  17.7 us
    all_to_all x1, starting transfers between devices, swap(): return lax.all_to_all(value, axis, split_axis=0, concat_axis=0, tiled=True)  8.29 us
    ppermute x18, waiting for transfers between devices, flip(): lax.ppermute(value, axis, [(source, source ^ bits) for source in range(co...  5.18 us
    ppermute x2, starting transfers between devices, from_behind(): return lax.ppermute(value, axis, pairs)  4.6 us
    ppermute x2, waiting for transfers between devices, from_behind(): return lax.ppermute(value, axis, pairs)  2.03 us
  transfers between devices with their start and end apart: 21, of which 3 were waited for; matrix products, arithmetic and copies ran while one was open for 0% of the time, Pallas kernels for 29%

commit v1 on v0

--- a/solution.py
+++ b/solution.py
@@ -211,8 +211,11 @@
     return ((rest // half) * WIN + side * half + rest % half == c).astype(F32).astype(BF16)
 
 
-def chosen(shape, axis, row0, vals):
-    r = iota(shape, axis) + row0
+def chosen(shape, axis, vals, chunk_of=None, size=1):
+    r = iota(shape, axis)
+    if chunk_of is not None:
+        chunk = over(r, size)
+        r = chunk_of(chunk) * size + r - chunk * size
     slot = (r // (2 * GROUP)) * GROUP + r % GROUP
     level = (r // GROUP) % 2
     first = (vals(0) == slot) | (vals(1) == slot)
@@ -221,9 +224,9 @@
     return hit.astype(F32).astype(BF16)
 
 
-def prep_kernel(cap, me_ref, loads, outs, scratch):
+def prep_kernel(cap, direct, me_ref, loads, outs, scratch):
     recv, weight, embed, rel = (one() for one in loads)
-    mix_ref, scatter_ref, embed_out, bias_ref, select_ref = outs
+    mix_ref, *scatter_refs, embed_out, bias_ref, select_ref = outs
     kk, pd = recv.shape
     slots = 2 * pd
     pixsq = weight.shape[1] // kk
@@ -238,19 +241,32 @@
     parts = [v.astype(F32).astype(BF16) for v in (sender, inner)]
     cols = (mm_nt(turn, parts[0]) * cap + mm_nt(turn, parts[1])).astype(jnp.int32)
     rows = (mm_nt(parts[0], turn) * cap + mm_nt(parts[1], turn)).astype(jnp.int32)
-    select_ref[...] = chosen((2 * slots, pd), 0, 0, lambda k: rows[k : k + 1, :])
-    stages, _, width = scatter_ref.shape
-    for stage in range(stages):
-        scatter_ref[stage] = chosen((pd, width), 1, stage * width, lambda k: cols[:, k : k + 1])
+    select_ref[...] = chosen((2 * slots, pd), 0, lambda k: rows[k : k + 1, :])
+    for stage, ref in enumerate(scatter_refs):
+        ref[...] = chosen(ref.shape, 1, lambda k: cols[:, k : k + 1],
+                          functools.partial(stage_chunk, stage, direct), 2 * slots // (4 * NEAR))
     for i in range(pix):
         lo, hi, move = tile_move(ch, i, embed.shape[0])
         embed_out[i * LANES : (i + 1) * LANES, :] = mm_tn(move, embed[lo:hi, :]).astype(BF16)
     bias_rows(rel, scratch[0], bias_ref)
 
 
-def prep_back_kernel(loads, outs, scratch):
-    weight_ref, unembed = (one() for one in loads)
-    mix_ref, unembed_out = outs
+def prep_back_kernel(size, me_ref, loads, outs, scratch):
+    weight, unembed, send = loads
+    weight_ref, unembed = weight(), unembed()
+    mix_ref, unembed_out, owner_ref = outs
+    owner = jnp.broadcast_to(send()[...], (GROUP, send.ref.shape[1]))
+    if size is not None:
+        cap = size * GROUP
+        count = owner.shape[1] // cap
+        chunk = over(iota(owner.shape, 1), cap)
+        for bit in range(count.bit_length() - 1):
+            gap = cap << bit
+            up = pltpu.roll(owner, owner.shape[1] - gap, 1)
+            down = pltpu.roll(owner, gap, 1)
+            swapped = jnp.where((chunk >> bit) & 1 == 0, up, down)
+            owner = jnp.where((me_ref[0] >> bit) & 1 == 1, swapped, owner)
+    owner_ref[...] = owner
     rows, pixsq = weight_ref.shape
     pix = int(round(pixsq**0.5))
     ch = unembed.shape[0] // pix
@@ -313,17 +329,28 @@
     return jnp.concatenate(pieces, axis=0).astype(BF16)
 
 
-def regrid_part(data, x_ref, c_ref, mix, scatter, embed, pix):
+def stage_chunk(stage, direct, i):
+    if not direct:
+        return i + (0 if stage == 0 else NEAR)
+    if stage == 0:
+        return 2 * i
+    return jnp.where(i < NEAR, 2 * i + 1, i + NEAR)
+
+
+def regrid_part(stage, direct, data, x_ref, c_ref, mix, scatter, embed, pix):
     slots, width = data.shape
     ch = width // pix
     for j in range(pix):
         lo, hi, move = tile_move(ch, j, width)
         x_ref[:, j * LANES : (j + 1) * LANES] = mm(data[:, lo:hi], move)
     mix_ref = mix()
+    size = mix_ref.shape[0] // (4 * NEAR)
 
     def group(g, carry):
+        chunk = lax.div(g, size)
+        where = stage_chunk(stage, direct, chunk) * size + g - chunk * size
         tiles = lay_tiles(x_ref[pl.ds(pl.multiple_of(g * GROUP, GROUP), GROUP), :], pix).astype(BF16)
-        out = mm(mix_ref[g], tiles)
+        out = mm(mix_ref[where], tiles)
         to = pl.ds(pl.multiple_of(g * 2 * GROUP, 2 * GROUP), 2 * GROUP)
         for i in range(pix):
             low = out[i * GROUP : (i + 1) * GROUP]
@@ -343,14 +370,14 @@
     return total
 
 
-def early_kernel(pix, loads, outs, scratch):
+def early_kernel(pix, direct, loads, outs, scratch):
     *chunks, mix, scatter, embed = loads
-    outs[0][...] = regrid_part(joined(chunks), *scratch, mix, scatter, embed, pix)
-
-
-def first_kernel(pix, layer, loads, outs, scratch):
+    outs[0][...] = regrid_part(0, direct, joined(chunks), *scratch, mix, scatter, embed, pix)
+
+
+def first_kernel(pix, direct, layer, loads, outs, scratch):
     *chunks, mix, scatter, embed, prior, gain1, gain2, qkv, bias, proj, up, down = loads
-    total = regrid_part(joined(chunks), *scratch, mix, scatter, embed, pix)
+    total = regrid_part(1, direct, joined(chunks), *scratch, mix, scatter, embed, pix)
     state = (prior()[...] + total).astype(BF16).astype(F32)
     pd, d = state.shape
     heads = bias.ref.shape[1] // (WIN * WIN)
@@ -480,18 +507,8 @@
     pd, total = out_ref.shape
     ch = total // pix
     prior_ref = prior()
-    owner = jnp.broadcast_to(send()[...], (GROUP, send.ref.shape[1]))
-    if size is not None:
-        cap = size * GROUP
-        count = owner.shape[1] // cap
-        chunk = over(iota(owner.shape, 1), cap)
-        for bit in range(count.bit_length() - 1):
-            gap = cap << bit
-            up = pltpu.roll(owner, owner.shape[1] - gap, 1)
-            down = pltpu.roll(owner, gap, 1)
-            swapped = jnp.where((chunk >> bit) & 1 == 0, up, down)
-            owner = jnp.where((me_ref[0] >> bit) & 1 == 1, swapped, owner)
-    onehot = (iota((pd, owner.shape[1]), 0) == owner[:1]).astype(F32).astype(BF16)
+    owner = send()
+    onehot = (iota((pd, owner.shape[1]), 0) == owner[:1, :]).astype(F32).astype(BF16)
     tiles = [None] * (-(-total // LANES))
     for j in range(0, pix, 2):
         cols = slice(j * LANES, (j + 2) * LANES)
@@ -577,17 +594,17 @@
             came[s] = flip(outgoing[s], "tile", 2 * s)
     else:
         outgoing = call(pick_kernel, [In(send_table), In(bands)], [sds((slots, width), BF16)])
-        incoming = swap(outgoing, "tile").reshape(STAGES, per, width)
+        incoming = swap(outgoing, "tile")
 
     heads = rel_bias.shape[1]
     span = WIN * WIN
     wsend = call(weights_kernel, [In(recv_table), In(regrid_weight)], [sds((2 * slots, pixsq), BF16)],
-                 flops=2e8)
+                 flops=2e8, after=[outgoing[0] if direct else outgoing])
     wback = swap_pairs(wsend, "tile")
-    mix, scatter, embed_pad, bias, select = call(
-        functools.partial(prep_kernel, cap),
+    mix, scatter_a, scatter_b, embed_pad, bias, select = call(
+        functools.partial(prep_kernel, cap, direct),
         [In(recv_table), In(regrid_weight), In(embed_weight), In(rel_bias.transpose(1, 0, 2))],
-        [sds((slots // GROUP, 2 * pix * GROUP, pix * GROUP), BF16), sds((STAGES, pd, 2 * per), BF16),
+        [sds((slots // GROUP, 2 * pix * GROUP, pix * GROUP), BF16), sds((pd, slots // 2), BF16), sds((pd, 3 * slots // 2), BF16),
          sds((wide, d), BF16), sds((rel_bias.shape[0], span, heads * span), F32),
          sds((2 * slots, pd), BF16)],
         [vm((heads, 2 * LANES), F32)], my, flops=4e9, after=[wsend])
@@ -596,21 +613,21 @@
         shape = (len(arrays), *arrays[0].shape[1:])
         return call(relay_kernel, [at(x, 1) for x in arrays], [sds(shape, BF16)], after=after)
 
-    def mix_rows(stage):
-        return In(mix, slice(stage * groups, (stage + 1) * groups))
-
-    regrid_scratch = [vm((per, wide), F32), vm((2 * per, wide), BF16)]
+    def regrid_scratch(rows):
+        return [vm((rows, wide), F32), vm((2 * rows, wide), BF16)]
+
     if direct:
-        near_all = relay(came[:NEAR], [wsend])
-        near_pass = flip(near_all, "tile", 1)
-        near = [y for i, x in enumerate(came[:NEAR]) for y in (at(x, 0), at(near_pass, i))]
+        near = [at(x, 0) for x in came[:NEAR]]
     else:
-        near, far = [at(incoming, 0)], [at(incoming, 1)]
-    total = call(functools.partial(early_kernel, pix),
-                 [*near, mix_rows(0), at(scatter, 0), In(embed_pad)], [sds((pd, d), F32)], regrid_scratch, flops=2e9)
+        near, far = [at(incoming, slice(0, slots // 4))], [at(incoming, slice(slots // 4, slots))]
+    total = call(functools.partial(early_kernel, pix, direct),
+                 [*near, In(mix), In(scatter_a), In(embed_pad)], [sds((pd, d), F32)],
+                 regrid_scratch(slots // 4), flops=2e9)
     if direct:
-        far_pass = flip(relay(came[NEAR:], [total]), "tile", 1)
-        far = [y for i, x in enumerate(came[NEAR:]) for y in (at(x, 0), at(far_pass, i))]
+        for_partner = relay(came, [total])
+        passed = flip(for_partner, "tile", 1)
+        far = [at(passed, i) for i in range(NEAR)]
+        far += [y for i in range(NEAR, chips) for y in (at(came[i], 0), at(passed, i))]
 
     def layer(n):
         return [In(norm1_gain), In(norm2_gain), at(qkv_weight, n), at(bias, n)], [
@@ -619,9 +636,9 @@
     half = pd // 2
     ins_a, ins_b = layer(0)
     low, high = call(
-        functools.partial(first_kernel, pix, 0),
-        [*far, mix_rows(1), at(scatter, 1), In(embed_pad), In(total), *ins_a, *ins_b],
-        [sds((half, d), BF16)] * 2, regrid_scratch, flops=4e9)
+        functools.partial(first_kernel, pix, direct, 0),
+        [*far, In(mix), In(scatter_b), In(embed_pad), In(total), *ins_a, *ins_b],
+        [sds((half, d), BF16)] * 2, regrid_scratch(3 * slots // 4), flops=4e9)
     right = from_behind(low, "tile", -1)
     left = from_behind(high, "tile", 1)
     ins_a, ins_b = layer(1)
@@ -631,17 +648,18 @@
         [In(low), In(high), *ins_a, In(left), In(right), *ins_b, In(select)],
         [sds((2, rows, d), BF16)] * chips if direct else [sds((2 * slots, d), BF16)], flops=2e9)
     one_sent = sent[0] if direct else sent
-    mix_back, unembed_pad = call(
-        prep_back_kernel, [In(wback), In(unembed_weight.T)],
-        [sds((slots // GROUP, pix * GROUP, 2 * pix * GROUP), BF16), sds((wide, d), BF16)], flops=2e9, after=[one_sent])
-
     size = cap // GROUP if direct else None
+    mix_back, unembed_pad, owner = call(
+        functools.partial(prep_back_kernel, size), [In(wback), In(unembed_weight.T), In(send_table)],
+        [sds((slots // GROUP, pix * GROUP, 2 * pix * GROUP), BF16), sds((wide, d), BF16),
+         sds((GROUP, slots), jnp.int32)], (), my, flops=2e9, after=[one_sent])
+
     back_scratch = [vm((2 * per, wide), F32), vm((per, wide), F32)]
     if direct:
         got = [sent[0]] + [None] * (chips - 1)
         for s in turns:
             got[s] = flip(sent[s], "tile", 2 * s)
-        near_pass = flip(relay(got[:NEAR]), "tile", 1)
+        near_pass = flip(relay(got[:NEAR], [mix_back]), "tile", 1)
         near = [y for i, x in enumerate(got[:NEAR]) for y in (at(x, 0), at(near_pass, i))]
     else:
         got = swap_pairs(sent, "tile").reshape(STAGES, 2 * per, d)
@@ -651,7 +669,7 @@
     if direct:
         far_pass = flip(relay(got[NEAR:], [prior]), "tile", 1)
         far = [y for i, x in enumerate(got[NEAR:]) for y in (at(x, 0), at(far_pass, i))]
-    return call(functools.partial(last_kernel, size, groups), [*far, In(unembed_pad), In(mix_back), In(prior), In(send_table)],
+    return call(functools.partial(last_kernel, size, groups), [*far, In(unembed_pad), In(mix_back), In(prior), In(owner)],
                 [sds((pd, width), F32)], back_scratch, my, flops=3e9)
 
 

time: 96.3 us -> 106 us (1.10); the launches traced: 95.5 us -> 104 us
  waiting for transfers between devices: 7.22 us -> 16 us
  local copies, waits for them, and re-layouts: 17.7 us -> 22.1 us
  Pallas kernels: 33 us -> 30.3 us
  starting transfers between devices: 37.2 us -> 35.1 us
    ppermute x2, waiting for transfers between devices: 2.03 us -> 6.47 us  [from_behind(): return lax.ppermute(value, axis, pairs)]
    unnamed x66 -> x76, local copies, waits for them, and re-layouts: 17.7 us -> 22.1 us
    ppermute x18 -> x17, waiting for transfers between devices: 5.18 us -> 9.5 us  [flip(): lax.ppermute(value, axis, [(source, source ^ bits) for source in range(co...]
    pallas_call x13 -> x12, Pallas kernels: 33 us -> 30.3 us  [call(): pl.pallas_call(run, out_shape=list(outs), in_specs=in_specs + [vmem] * le...]
    all_to_all x1, starting transfers between devices: 8.29 us -> 6.81 us  [swap(): return lax.all_to_all(value, axis, split_axis=0, concat_axis=0, tiled=True)]
    ppermute x18 -> x17, starting transfers between devices: 24.4 us -> 23.9 us  [flip(): lax.ppermute(value, axis, [(source, source ^ bits) for source in range(co...]
  transfers between devices with their start and end apart: 21 -> 20, of which waited for: 3 -> 8; matrix products, arithmetic and copies ran while one was open for 0% -> 0% of each run, Pallas kernels for 29% -> 24%
where the time goes in v1:
time: 106 us; the launch traced here: 104 us
  starting transfers between devices  35.1 us (33%)
  Pallas kernels  30.3 us (29%)
  local copies, waits for them, and re-layouts  22.1 us (21%)
  waiting for transfers between devices  16 us (15%)
    pallas_call x12, Pallas kernels, call(): pl.pallas_call(run, out_shape=list(outs), in_specs=in_specs + [vmem] * le...  30.3 us
    ppermute x17, starting transfers between devices, flip(): lax.ppermute(value, axis, [(source, source ^ bits) for source in range(co...  23.9 us
    unnamed x76, local copies, waits for them, and re-layouts  22.1 us
    ppermute x17, waiting for transfers between devices, flip(): lax.ppermute(value, axis, [(source, source ^ bits) for source in range(co...  9.5 us
    all_to_all x1, starting transfers between devices, swap(): return lax.all_to_all(value, axis, split_axis=0, concat_axis=0, tiled=True)  6.81 us
    ppermute x2, waiting for transfers between devices, from_behind(): return lax.ppermute(value, axis, pairs)  6.47 us
    ppermute x2, starting transfers between devices, from_behind(): return lax.ppermute(value, axis, pairs)  4.36 us
  transfers between devices with their start and end apart: 20, of which 8 were waited for; matrix products, arithmetic and copies ran while one was open for 0% of the time, Pallas kernels for 24%

profile of v1, /device:TPU:0, one launch (start us, length us, event | category | flops | bytes accessed | tf_op | source)
XLA Modules:
  0.0 103.9 jit_solution(9226248865337618664)
XLA Ops:
  0.0 1.0 %copy-done.22 = bf16[192,1312]{1,0:T(8,128)(2,1)S(1)} copy-done((bf16[192,1312]{1,0:T(8,128)(2,1)S(1)}, bf16[192,1312]{1,0:T(8,128)(2,1)}, u32[]{:S(2)}) %copy-start.22) | copy-done | bytes 503832
  1.1 0.7 copy-done.33
  1.7 0.6 shard_map.127
  2.3 3.1 %collective-permute-start = (bf16[2,24,1312]{2,1,0:T(8,128)(2,1)S(1)}, bf16[2,24,1312]{2,1,0:T(8,128)(2,1)S(1)}, u32[]{:S(2)}, u32[]{:S(2)}) collective-permute-start(bf16[2,24,1312]{2,1,0:T(8,128)(2,1)S(1)} %get-tuple-element.33), channel_id=1, source_target_pairs={{0,2},{1,3},{2,0},{3,1},{4,6},{5,7},{6,4},{7,5},{8,10},{9,11},{10,... | collective-permute-start | bytes 377864 | tf_op jit(solution)/shard_map/ppermute | solution.py:552
  5.4 1.6 %collective-permute-start.1 = (bf16[2,24,1312]{2,1,0:T(8,128)(2,1)S(1)}, bf16[2,24,1312]{2,1,0:T(8,128)(2,1)S(1)}, u32[]{:S(2)}, u32[]{:S(2)}) collective-permute-start(bf16[2,24,1312]{2,1,0:T(8,128)(2,1)S(1)} %get-tuple-element.34), channel_id=1, source_target_pairs={{0,4},{1,5},{2,6},{3,7},{4,0},{5,1},{6,2},{7,3},{8,12},{9,13},{10,... | collective-permute-start | bytes 377864 | tf_op jit(solution)/shard_map/ppermute | solution.py:552
  7.0 3.0 %collective-permute-start.3 = (bf16[2,24,1312]{2,1,0:T(8,128)(2,1)S(1)}, bf16[2,24,1312]{2,1,0:T(8,128)(2,1)S(1)}, u32[]{:S(2)}, u32[]{:S(2)}) collective-permute-start(bf16[2,24,1312]{2,1,0:T(8,128)(2,1)S(1)} %get-tuple-element.36), channel_id=1, source_target_pairs={{0,8},{1,9},{2,10},{3,11},{4,12},{5,13},{6,14},{7,15},{8,0},{9,1},... | collective-permute-start | bytes 377864 | tf_op jit(solution)/shard_map/ppermute | solution.py:552
  9.9 1.3 %collective-permute-start.4 = (bf16[2,24,1312]{2,1,0:T(8,128)(2,1)S(1)}, bf16[2,24,1312]{2,1,0:T(8,128)(2,1)S(1)}, u32[]{:S(2)}, u32[]{:S(2)}) collective-permute-start(bf16[2,24,1312]{2,1,0:T(8,128)(2,1)S(1)} %get-tuple-element.37), channel_id=1, source_target_pairs={{0,10},{1,11},{2,8},{3,9},{4,14},{5,15},{6,12},{7,13},{8,2},{9,3},... | collective-permute-start | bytes 377864 | tf_op jit(solution)/shard_map/ppermute | solution.py:552
  11.2 1.0 copy-done.25
  12.2 0.7 copy-done.31
  13.3 1.1 %copy-done.26 = bf16[192,1024]{1,0:T(8,128)(2,1)S(1)} copy-done((bf16[192,1024]{1,0:T(8,128)(2,1)S(1)}, bf16[192,1024]{1,0:T(8,128)(2,1)}, u32[]{:S(2)}) %copy-start.26) | copy-done | bytes 393240
  14.4 0.7 copy-done.32
  15.1 1.2 %copy-done.35 = bf16[1312,384]{1,0:T(8,128)(2,1)S(1)} copy-done((bf16[1312,384]{1,0:T(8,128)(2,1)S(1)}, bf16[1312,384]{1,0:T(8,128)(2,1)}, u32[]{:S(2)}) %copy-start.35) | copy-done | bytes 1007640
  16.3 0.7 copy-done.37
  17.1 2.8 %shard_map.129 = (bf16[48,256,128]{2,1,0:T(8,128)(2,1)S(1)}, bf16[192,192]{1,0:T(8,128)(2,1)S(1)}, bf16[192,576]{1,0:T(8,128)(2,1)S(1)}, bf16[2048,384]{1,0:T(8,...) custom-call(s32[1]{0:T(128)} %bitcast.refs_0_, s32[4,192]{1,0:T(4,128)S(1)} %copy-done.32, ...), custom_call_target="tpu_custom_call" | custom-call | flops 4000000000 | bytes 1425504 | tf_op jit(solution)/shard_map/pallas_call | solution.py:74
  19.9 3.7 %collective-permute-start.5 = (bf16[2,24,1312]{2,1,0:T(8,128)(2,1)S(1)}, bf16[2,24,1312]{2,1,0:T(8,128)(2,1)S(1)}, u32[]{:S(2)}, u32[]{:S(2)}) collective-permute-start(bf16[2,24,1312]{2,1,0:T(8,128)(2,1)S(1)} %get-tuple-element.38), channel_id=1, source_target_pairs={{0,12},{1,13},{2,14},{3,15},{4,8},{5,9},{6,10},{7,11},{8,4},{9,5},... | collective-permute-start | bytes 377864 | tf_op jit(solution)/shard_map/ppermute | solution.py:552
  23.6 2.6 %shard_map.130.refs_8_.refs_15_ = f32[192,384]{1,0:T(8,128)S(1)} custom-call(bf16[2,24,1312]{2,1,0:T(8,128)(2,1)S(1)} %get-tuple-element.32.refs_2_.refs_0_, bf16[2,24,1312]{2,1,0:T(8,128)(2,1)S(1)} %collective-permute-done.refs_1_, bf16[2,24,1312]{2,1,0:T(8,128)(2,1)S(1)} %collective-permute-done.1.refs_2_, ...), custom_call_target="tpu_custom_call" | custom-call | flops 2000000000 | bytes 5296128 | tf_op jit(solution)/shard_map/pallas_call | solution.py:74
  26.7 0.9 collective-permute-done.5.refs_6_.refs_8_
  27.6 3.8 %collective-permute-done.6.refs_7_.refs_10_ = bf16[2,24,1312]{2,1,0:T(8,128)(2,1)S(1)} collective-permute-done((bf16[2,24,1312]{2,1,0:T(8,128)(2,1)S(1)}, bf16[2,24,1312]{2,1,0:T(8,128)(2,1)S(1)}, u32[]{:S(2)}, u32[]{:S(2)}) %collective-permute-start.6) | collective-permute-done | bytes 125984 | tf_op jit(solution)/shard_map/ppermute | solution.py:552
  31.4 0.8 shard_map.131
  32.2 0.7 copy-done.12
  33.0 6.8 %all-to-all-start = ((bf16[16,48,256]{2,1,0:T(8,128)(2,1)}), bf16[16,48,256]{2,1,0:T(8,128)(2,1)}, u32[]{:S(2)}, u32[]{:S(2)}) async-start(bf16[16,48,256]{2,1,0:T(8,128)(2,1)} %bitcast.5), calls=%async_computation | async-start | bytes 786432 | tf_op jit(solution)/shard_map/all_to_all | solution.py:534
  39.8 1.7 %copy-done.1 = bf16[2,1536,384]{2,1,0:T(8,128)(2,1)S(1)} copy-done((bf16[2,1536,384]{2,1,0:T(8,128)(2,1)S(1)}, bf16[2,1536,384]{2,1,0:T(8,128)(2,1)}, u32[]{:S(2)}) %copy-start.1) | copy-done | bytes 2359320
  41.5 1.5 %copy-done.2 = bf16[2,384,1152]{2,1,0:T(8,128)(2,1)S(1)} copy-done((bf16[2,384,1152]{2,1,0:T(8,128)(2,1)S(1)}, bf16[2,384,1152]{2,1,0:T(8,128)(2,1)}, u32[]{:S(2)}) %copy-start.2) | copy-done | bytes 1769496
  43.0 1.9 %copy-done.5 = bf16[48,256,128]{2,1,0:T(8,128)(2,1)S(1)} copy-done((bf16[48,256,128]{2,1,0:T(8,128)(2,1)S(1)}, bf16[48,256,128]{2,1,0:T(8,128)(2,1)}, u32[]{:S(2)}) %copy-start.5) | copy-done | bytes 3145752
  44.9 1.4 %copy-done.8 = bf16[2048,384]{1,0:T(8,128)(2,1)S(1)} copy-done((bf16[2048,384]{1,0:T(8,128)(2,1)S(1)}, bf16[2048,384]{1,0:T(8,128)(2,1)}, u32[]{:S(2)}) %copy-start.8) | copy-done | bytes 1572888
  46.3 1.0 copy-done.10
  47.3 1.0 copy-done.13
  48.2 0.9 copy-done.15
  49.1 0.9 copy-done.17
  50.0 0.9 copy-done.19
  50.9 0.9 copy-done.21
  51.9 0.9 copy-done.28
  52.8 8.4 %shard_map.132 = (bf16[96,384]{1,0:T(8,128)(2,1)S(1)}, bf16[96,384]{1,0:T(8,128)(2,1)S(1)}) custom-call(bf16[8,24,1312]{2,1,0:T(8,128)(2,1)S(1)} %collective-permute-done.7.refs_0_.refs_1_.refs_2_.refs_3_.refs_5_.refs_7_.refs_9_.refs_11_, bf16[8,24,1312]{2,1,0:T(8,128)(2,1)S(1)} %collective-permute-done.7.refs_0_.refs_1_.refs_2_.refs_3_.refs_5_.refs_7_.refs_9_.refs_11_, ...), custom_call_target="tpu_custom_call" | custom-call | flops 4000000000 | bytes 17246208 | tf_op jit(solution)/shard_map/pallas_call | solution.py:74
  61.2 4.4 %collective-permute-start.9 = (bf16[96,384]{1,0:T(8,128)(2,1)S(1)}, bf16[96,384]{1,0:T(8,128)(2,1)S(1)}, u32[]{:S(2)}, u32[]{:S(2)}) collective-permute-start(bf16[96,384]{1,0:T(8,128)(2,1)S(1)} %get-tuple-element.45.refs_0_), channel_id=1, source_target_pairs={{0,15},{1,0},{2,1},{3,2},{4,3},{5,4},{6,5},{7,6},{8,7},{9,8},{10,9... | collective-permute-start | bytes 221192 | tf_op jit(solution)/shard_map/ppermute | solution.py:558
  65.5 2.0 %collective-permute-done.9.refs_7_ = bf16[96,384]{1,0:T(8,128)(2,1)S(1)} collective-permute-done((bf16[96,384]{1,0:T(8,128)(2,1)S(1)}, bf16[96,384]{1,0:T(8,128)(2,1)S(1)}, u32[]{:S(2)}, u32[]{:S(2)}) %collective-permute-start.9) | collective-permute-done | bytes 73760 | tf_op jit(solution)/shard_map/ppermute | solution.py:558
  67.5 4.5 %collective-permute-done.8.refs_6_ = bf16[96,384]{1,0:T(8,128)(2,1)S(1)} collective-permute-done((bf16[96,384]{1,0:T(8,128)(2,1)S(1)}, bf16[96,384]{1,0:T(8,128)(2,1)S(1)}, u32[]{:S(2)}, u32[]{:S(2)}) %collective-permute-start.8) | collective-permute-done | bytes 73760 | tf_op jit(solution)/shard_map/ppermute | solution.py:558
  72.0 5.6 %shard_map.133 = (bf16[2,48,384]{2,1,0:T(8,128)(2,1)S(1)}, bf16[2,48,384]{2,1,0:T(8,128)(2,1)}, bf16[2,48,384]{2,1,0:T(8,128)(2,1)S(1)}, bf16[2,48,384]{2,1,0:T(...) custom-call(bf16[96,384]{1,0:T(8,128)(2,1)S(1)} %get-tuple-element.4, ...), custom_call_target="tpu_custom_call" | custom-call | flops 2000000000 | bytes 8067072 | tf_op jit(solution)/shard_map/pallas_call | solution.py:74
  77.6 3.5 %collective-permute-start.16 = (bf16[2,48,384]{2,1,0:T(8,128)(2,1)S(1)}, bf16[2,48,384]{2,1,0:T(8,128)(2,1)S(1)}, u32[]{:S(2)}, u32[]{:S(2)}) collective-permute-start(bf16[2,48,384]{2,1,0:T(8,128)(2,1)S(1)} %get-tuple-element.55), channel_id=1, source_target_pairs={{0,6},{1,7},{2,4},{3,5},{4,2},{5,3},{6,0},{7,1},{8,14},{9,15},{10,... | collective-permute-start | bytes 221192 | tf_op jit(solution)/shard_map/ppermute | solution.py:552
  81.1 1.2 %copy-done.36 = bf16[384,1312]{0,1:T(8,128)(2,1)S(1)} copy-done((bf16[384,1312]{0,1:T(8,128)(2,1)S(1)}, bf16[384,1312]{0,1:T(8,128)(2,1)}, u32[]{:S(2)}) %copy-start.36) | copy-done | bytes 1007640
  82.3 2.8 %shard_map.134 = (bf16[48,128,256]{2,1,0:T(8,128)(2,1)S(1)}, bf16[2048,384]{1,0:T(8,128)(2,1)S(1)}, s32[8,384]{1,0:T(8,128)S(1)}) custom-call(s32[1]{0:T(128)} %bitcast.refs_0_, bf16[768,256]{1,0:T(8,128)(2,1)} %bitcast.3.refs_1_, bf16[1312,384]{1,0:T(8,128)(2,1)S(1)} %bitcast.6, s32[1,384]{1,0:T(1,128)S(1)} %copy-done.34, ...), custom_call_target="tpu_custom_call" | custom-call | flops 2000000000 | bytes 1402368 | tf_op jit(solution)/shard_map/pallas_call | solution.py:74
  85.3 2.3 %collective-permute-start.11 = (bf16[2,48,384]{2,1,0:T(8,128)(2,1)S(1)}, bf16[2,48,384]{2,1,0:T(8,128)(2,1)S(1)}, u32[]{:S(2)}, u32[]{:S(2)}) collective-permute-start(bf16[2,48,384]{2,1,0:T(8,128)(2,1)S(1)} %get-tuple-element.49), channel_id=1, source_target_pairs={{0,10},{1,11},{2,8},{3,9},{4,14},{5,15},{6,12},{7,13},{8,2},{9,3},... | collective-permute-start | bytes 221192 | tf_op jit(solution)/shard_map/ppermute | solution.py:552
  87.7 1.3 %collective-permute-start.12 = (bf16[2,48,384]{2,1,0:T(8,128)(2,1)S(1)}, bf16[2,48,384]{2,1,0:T(8,128)(2,1)S(1)}, u32[]{:S(2)}, u32[]{:S(2)}) collective-permute-start(bf16[2,48,384]{2,1,0:T(8,128)(2,1)S(1)} %get-tuple-element.50), channel_id=1, source_target_pairs={{0,12},{1,13},{2,14},{3,15},{4,8},{5,9},{6,10},{7,11},{8,4},{9,5},... | collective-permute-start | bytes 221192 | tf_op jit(solution)/shard_map/ppermute | solution.py:552
  89.0 4.0 %collective-permute-start.13 = (bf16[2,48,384]{2,1,0:T(8,128)(2,1)S(1)}, bf16[2,48,384]{2,1,0:T(8,128)(2,1)S(1)}, u32[]{:S(2)}, u32[]{:S(2)}) collective-permute-start(bf16[2,48,384]{2,1,0:T(8,128)(2,1)S(1)} %get-tuple-element.51), channel_id=1, source_target_pairs={{0,14},{1,15},{2,12},{3,13},{4,10},{5,11},{6,8},{7,9},{8,6},{9,7},... | collective-permute-start | bytes 221192 | tf_op jit(solution)/shard_map/ppermute | solution.py:552
  93.0 2.4 %shard_map.136.refs_4_.refs_11_ = bf16[192,2048]{1,0:T(8,128)(2,1)S(1)} custom-call(s32[1]{0:T(128)} %bitcast.refs_0_, bf16[2,48,384]{2,1,0:T(8,128)(2,1)S(1)} %get-tuple-element.52.refs_4_.refs_0_.refs_1_, bf16[4,48,384]{2,1,0:T(8,128)(2,1)S(1)} %collective-permute-done.17.refs_2_.refs_4_.refs_6_.refs_8_, ...), custom_call_target="tpu_custom_call" | custom-call | flops 2000000000 | bytes 5603328 | tf_op jit(solution)/shard_map/pallas_call | solution.py:74
  95.4 1.2 %collective-permute-done.10.refs_0_.refs_1_ = bf16[2,48,384]{2,1,0:T(8,128)(2,1)S(1)} collective-permute-done((bf16[2,48,384]{2,1,0:T(8,128)(2,1)S(1)}, bf16[2,48,384]{2,1,0:T(8,128)(2,1)S(1)}, u32[]{:S(2)}, u32[]{:S(2)}) %collective-permute-start.10) | collective-permute-done | bytes 73760 | tf_op jit(solution)/shard_map/ppermute | solution.py:552
  96.6 1.8 %collective-permute-done.11.refs_1_.refs_3_ = bf16[2,48,384]{2,1,0:T(8,128)(2,1)S(1)} collective-permute-done((bf16[2,48,384]{2,1,0:T(8,128)(2,1)S(1)}, bf16[2,48,384]{2,1,0:T(8,128)(2,1)S(1)}, u32[]{:S(2)}, u32[]{:S(2)}) %collective-permute-start.11) | collective-permute-done | bytes 73760 | tf_op jit(solution)/shard_map/ppermute | solution.py:552
  98.5 1.4 %collective-permute-done.18.refs_2_.refs_4_.refs_6_.refs_8_ = bf16[4,48,384]{2,1,0:T(8,128)(2,1)S(1)} collective-permute-done((bf16[4,48,384]{2,1,0:T(8,128)(2,1)S(1)}, bf16[4,48,384]{2,1,0:T(8,128)(2,1)S(1)}, u32[]{:S(2)}, u32[]{:S(2)}) %collective-permute-start.18) | collective-permute-done | bytes 147488 | tf_op jit(solution)/shard_map/ppermute | solution.py:552
  99.9 4.0 %shard_map.138 = f32[192,1312]{1,0:T(8,128)} custom-call(s32[1]{0:T(128)} %bitcast.refs_0_, bf16[2,48,384]{2,1,0:T(8,128)(2,1)S(1)} %collective-permute-done.10.refs_0_.refs_1_, bf16[4,48,384]{2,1,0:T(8,128)(2,1)S(1)} %collective-permute-done.18.refs_2_.refs_4_.refs_6_.refs_8_, bf16[2,48,384]{2,1,0:T(8,128)(2,1)S(1)} %collective-permute-done.11.refs_1_.refs_3_, ...), custom_call_target="tpu_custom_call" | custom-call | flops 3000000000 | bytes 6402048 | tf_op jit(solution)/shard_map/pallas_call | solution.py:74
  (80 shorter events, 1.2 us)
Async XLA Ops:
  0.0 1.0 %copy-start.22 = (bf16[192,1312]{1,0:T(8,128)(2,1)S(1)}, bf16[192,1312]{1,0:T(8,128)(2,1)}, u32[]{:S(2)}) copy-start(bf16[192,1312]{1,0:T(8,128)(2,1)} %refs_2_.3) | copy-start | bytes 1511428
  2.3 17.6 %collective-permute-start = (bf16[2,24,1312]{2,1,0:T(8,128)(2,1)S(1)}, bf16[2,24,1312]{2,1,0:T(8,128)(2,1)S(1)}, u32[]{:S(2)}, u32[]{:S(2)}) collective-permute-start(bf16[2,24,1312]{2,1,0:T(8,128)(2,1)S(1)} %get-tuple-element.33), channel_id=1, source_target_pairs={{0,2},{1,3},{2,0},{3,1},{4,6},{5,7},{6,4},{7,5},{8,10},{9,11},{10,... | collective-permute-start | bytes 377864 | tf_op jit(solution)/shard_map/ppermute | solution.py:552
  5.4 18.2 %collective-permute-start.1 = (bf16[2,24,1312]{2,1,0:T(8,128)(2,1)S(1)}, bf16[2,24,1312]{2,1,0:T(8,128)(2,1)S(1)}, u32[]{:S(2)}, u32[]{:S(2)}) collective-permute-start(bf16[2,24,1312]{2,1,0:T(8,128)(2,1)S(1)} %get-tuple-element.34), channel_id=1, source_target_pairs={{0,4},{1,5},{2,6},{3,7},{4,0},{5,1},{6,2},{7,3},{8,12},{9,13},{10,... | collective-permute-start | bytes 377864 | tf_op jit(solution)/shard_map/ppermute | solution.py:552
  6.9 16.7 %collective-permute-start.2 = (bf16[2,24,1312]{2,1,0:T(8,128)(2,1)S(1)}, bf16[2,24,1312]{2,1,0:T(8,128)(2,1)S(1)}, u32[]{:S(2)}, u32[]{:S(2)}) collective-permute-start(bf16[2,24,1312]{2,1,0:T(8,128)(2,1)S(1)} %get-tuple-element.35), channel_id=1, source_target_pairs={{0,6},{1,7},{2,4},{3,5},{4,2},{5,3},{6,0},{7,1},{8,14},{9,15},{10,... | collective-permute-start | bytes 377864 | tf_op jit(solution)/shard_map/ppermute | solution.py:552
  7.0 19.3 %collective-permute-start.3 = (bf16[2,24,1312]{2,1,0:T(8,128)(2,1)S(1)}, bf16[2,24,1312]{2,1,0:T(8,128)(2,1)S(1)}, u32[]{:S(2)}, u32[]{:S(2)}) collective-permute-start(bf16[2,24,1312]{2,1,0:T(8,128)(2,1)S(1)} %get-tuple-element.36), channel_id=1, source_target_pairs={{0,8},{1,9},{2,10},{3,11},{4,12},{5,13},{6,14},{7,15},{8,0},{9,1},... | collective-permute-start | bytes 377864 | tf_op jit(solution)/shard_map/ppermute | solution.py:552
  9.9 16.8 %collective-permute-start.4 = (bf16[2,24,1312]{2,1,0:T(8,128)(2,1)S(1)}, bf16[2,24,1312]{2,1,0:T(8,128)(2,1)S(1)}, u32[]{:S(2)}, u32[]{:S(2)}) collective-permute-start(bf16[2,24,1312]{2,1,0:T(8,128)(2,1)S(1)} %get-tuple-element.37), channel_id=1, source_target_pairs={{0,10},{1,11},{2,8},{3,9},{4,14},{5,15},{6,12},{7,13},{8,2},{9,3},... | collective-permute-start | bytes 377864 | tf_op jit(solution)/shard_map/ppermute | solution.py:552
  11.2 1.0 copy-start.25
  13.3 6.6 %copy-start.11 = (bf16[768,256]{1,0:T(8,128)(2,1)}, bf16[768,256]{1,0:T(8,128)(2,1)S(1)}, u32[]{:S(2)}) copy-start(bf16[768,256]{1,0:T(8,128)(2,1)S(1)} %shard_map.128.refs_5_) | copy-start | bytes 1179652
  13.3 1.1 %copy-start.26 = (bf16[192,1024]{1,0:T(8,128)(2,1)S(1)}, bf16[192,1024]{1,0:T(8,128)(2,1)}, u32[]{:S(2)}) copy-start(bf16[192,1024]{1,0:T(8,128)(2,1)} %refs_2_.4) | copy-start | bytes 1179652
  15.1 1.2 %copy-start.35 = (bf16[1312,384]{1,0:T(8,128)(2,1)S(1)}, bf16[1312,384]{1,0:T(8,128)(2,1)}, u32[]{:S(2)}) copy-start(bf16[1312,384]{1,0:T(8,128)(2,1)} %refs_3_.3) | copy-start | bytes 3022852
  19.8 6.3 %copy-start.4 = (bf16[48,256,128]{2,1,0:T(8,128)(2,1)}, bf16[48,256,128]{2,1,0:T(8,128)(2,1)S(1)}, u32[]{:S(2)}) copy-start(bf16[48,256,128]{2,1,0:T(8,128)(2,1)S(1)} %get-tuple-element.40.refs_4_.refs_12_) | copy-start | bytes 9437188
  19.9 6.3 %copy-start.7 = (bf16[2048,384]{1,0:T(8,128)(2,1)}, bf16[2048,384]{1,0:T(8,128)(2,1)S(1)}, u32[]{:S(2)}) copy-start(bf16[2048,384]{1,0:T(8,128)(2,1)S(1)} %get-tuple-element.42.refs_6_.refs_14_) | copy-start | bytes 4718596
  19.9 6.3 %copy-start.9 = (f32[2,64,768]{2,1,0:T(8,128)}, f32[2,64,768]{2,1,0:T(8,128)S(1)}, u32[]{:S(2)}) copy-start(f32[2,64,768]{2,1,0:T(8,128)S(1)} %get-tuple-element.44.refs_19_.refs_5_) | copy-start | bytes 1179652
  19.9 6.3 %copy-start.23 = (bf16[768,192]{1,0:T(8,128)(2,1)}, bf16[768,192]{1,0:T(8,128)(2,1)S(1)}, u32[]{:S(2)}) copy-start(bf16[768,192]{1,0:T(8,128)(2,1)S(1)} %get-tuple-element.47.refs_11_) | copy-start | bytes 884740
  19.9 6.3 %copy-start.27 = (bf16[192,576]{1,0:T(8,128)(2,1)}, bf16[192,576]{1,0:T(8,128)(2,1)S(1)}, u32[]{:S(2)}) copy-start(bf16[192,576]{1,0:T(8,128)(2,1)S(1)} %get-tuple-element.43.refs_13_) | copy-start | bytes 663556
  19.9 7.7 %collective-permute-start.5 = (bf16[2,24,1312]{2,1,0:T(8,128)(2,1)S(1)}, bf16[2,24,1312]{2,1,0:T(8,128)(2,1)S(1)}, u32[]{:S(2)}, u32[]{:S(2)}) collective-permute-start(bf16[2,24,1312]{2,1,0:T(8,128)(2,1)S(1)} %get-tuple-element.38), channel_id=1, source_target_pairs={{0,12},{1,13},{2,14},{3,15},{4,8},{5,9},{6,10},{7,11},{8,4},{9,5},... | collective-permute-start | bytes 377864 | tf_op jit(solution)/shard_map/ppermute | solution.py:552
  23.6 7.8 %collective-permute-start.6 = (bf16[2,24,1312]{2,1,0:T(8,128)(2,1)S(1)}, bf16[2,24,1312]{2,1,0:T(8,128)(2,1)S(1)}, u32[]{:S(2)}, u32[]{:S(2)}) collective-permute-start(bf16[2,24,1312]{2,1,0:T(8,128)(2,1)S(1)} %get-tuple-element.39), channel_id=1, source_target_pairs={{0,14},{1,15},{2,12},{3,13},{4,10},{5,11},{6,8},{7,9},{8,6},{9,7},... | collective-permute-start | bytes 377864 | tf_op jit(solution)/shard_map/ppermute | solution.py:552
  23.6 16.2 %copy-start.6 = (bf16[2,384,384]{2,1,0:T(8,128)(2,1)S(1)}, bf16[2,384,384]{2,1,0:T(8,128)(2,1)}, u32[]{:S(2)}) copy-start(bf16[2,384,384]{2,1,0:T(8,128)(2,1)} %refs_8_.1) | copy-start | bytes 1769476
  26.2 13.6 %copy-start = (bf16[2,384,1536]{2,1,0:T(8,128)(2,1)S(1)}, bf16[2,384,1536]{2,1,0:T(8,128)(2,1)}, u32[]{:S(2)}) copy-start(bf16[2,384,1536]{2,1,0:T(8,128)(2,1)} %refs_9_.1) | copy-start | bytes 7077892
  26.2 13.6 %copy-start.29 = (f32[2,384]{1,0:T(2,128)S(1)}, f32[2,384]{1,0:T(2,128)}, u32[]{:S(2)}) copy-start(f32[2,384]{1,0:T(2,128)} %refs_2_.5) | copy-start | bytes 9220
  26.2 13.6 %copy-start.30 = (f32[2,384]{1,0:T(2,128)S(1)}, f32[2,384]{1,0:T(2,128)}, u32[]{:S(2)}) copy-start(f32[2,384]{1,0:T(2,128)} %refs_3_.4) | copy-start | bytes 9220
  26.3 6.0 %copy-start.14 = (bf16[2,24,1312]{2,1,0:T(8,128)(2,1)}, bf16[2,24,1312]{2,1,0:T(8,128)(2,1)S(1)}, u32[]{:S(2)}) copy-start(bf16[2,24,1312]{2,1,0:T(8,128)(2,1)S(1)} %collective-permute-done.3.refs_4_) | copy-start | bytes 377860
  26.7 6.2 %copy-start.16 = (bf16[2,24,1312]{2,1,0:T(8,128)(2,1)}, bf16[2,24,1312]{2,1,0:T(8,128)(2,1)S(1)}, u32[]{:S(2)}) copy-start(bf16[2,24,1312]{2,1,0:T(8,128)(2,1)S(1)} %collective-permute-done.4.refs_5_.refs_6_) | copy-start | bytes 377860
  27.6 5.3 %copy-start.18 = (bf16[2,24,1312]{2,1,0:T(8,128)(2,1)}, bf16[2,24,1312]{2,1,0:T(8,128)(2,1)S(1)}, u32[]{:S(2)}) copy-start(bf16[2,24,1312]{2,1,0:T(8,128)(2,1)S(1)} %collective-permute-done.5.refs_6_.refs_8_) | copy-start | bytes 377860
  31.4 1.6 %copy-start.20 = (bf16[2,24,1312]{2,1,0:T(8,128)(2,1)}, bf16[2,24,1312]{2,1,0:T(8,128)(2,1)S(1)}, u32[]{:S(2)}) copy-start(bf16[2,24,1312]{2,1,0:T(8,128)(2,1)S(1)} %collective-permute-done.6.refs_7_.refs_10_) | copy-start | bytes 377860
  32.9 6.8 %collective-permute-start.7 = (bf16[8,24,1312]{2,1,0:T(8,128)(2,1)}, bf16[8,24,1312]{2,1,0:T(8,128)(2,1)S(1)}, u32[]{:S(2)}, u32[]{:S(2)}) collective-permute-start(bf16[8,24,1312]{2,1,0:T(8,128)(2,1)} %shard_map.131), channel_id=1, source_target_pairs={{0,1},{1,0},{2,3},{3,2},{4,5},{5,4},{6,7},{7,6},{8,9},{9,8},{10,11... | collective-permute-start | bytes 1511432 | tf_op jit(solution)/shard_map/ppermute | solution.py:552
  33.0 48.2 %all-to-all-start = ((bf16[16,48,256]{2,1,0:T(8,128)(2,1)}), bf16[16,48,256]{2,1,0:T(8,128)(2,1)}, u32[]{:S(2)}, u32[]{:S(2)}) async-start(bf16[16,48,256]{2,1,0:T(8,128)(2,1)} %bitcast.5), calls=%async_computation | async-start | bytes 786432 | tf_op jit(solution)/shard_map/all_to_all | solution.py:534
  39.8 1.7 %copy-start.1 = (bf16[2,1536,384]{2,1,0:T(8,128)(2,1)S(1)}, bf16[2,1536,384]{2,1,0:T(8,128)(2,1)}, u32[]{:S(2)}) copy-start(bf16[2,1536,384]{2,1,0:T(8,128)(2,1)} %refs_10_.1) | copy-start | bytes 7077892
  41.5 1.5 %copy-start.2 = (bf16[2,384,1152]{2,1,0:T(8,128)(2,1)S(1)}, bf16[2,384,1152]{2,1,0:T(8,128)(2,1)}, u32[]{:S(2)}) copy-start(bf16[2,384,1152]{2,1,0:T(8,128)(2,1)} %refs_4_.1) | copy-start | bytes 5308420
  43.0 1.9 %copy-start.5 = (bf16[48,256,128]{2,1,0:T(8,128)(2,1)S(1)}, bf16[48,256,128]{2,1,0:T(8,128)(2,1)}, u32[]{:S(2)}) copy-start(bf16[48,256,128]{2,1,0:T(8,128)(2,1)} %copy-done.4) | copy-start | bytes 9437188
  44.9 1.4 %copy-start.8 = (bf16[2048,384]{1,0:T(8,128)(2,1)S(1)}, bf16[2048,384]{1,0:T(8,128)(2,1)}, u32[]{:S(2)}) copy-start(bf16[2048,384]{1,0:T(8,128)(2,1)} %copy-done.7) | copy-start | bytes 4718596
  46.3 1.0 copy-start.10
  47.3 1.0 copy-start.13
  52.8 19.2 %copy-start.3 = (bf16[2,384,1152]{2,1,0:T(8,128)(2,1)S(1)}, bf16[2,384,1152]{2,1,0:T(8,128)(2,1)}, u32[]{:S(2)}) copy-start(bf16[2,384,1152]{2,1,0:T(8,128)(2,1)} %refs_4_.1) | copy-start | bytes 5308420
  52.8 19.2 %copy-start.24 = (bf16[768,192]{1,0:T(8,128)(2,1)S(1)}, bf16[768,192]{1,0:T(8,128)(2,1)}, u32[]{:S(2)}) copy-start(bf16[768,192]{1,0:T(8,128)(2,1)} %copy-done.23) | copy-start | bytes 884740
  61.2 6.3 %collective-permute-start.9 = (bf16[96,384]{1,0:T(8,128)(2,1)S(1)}, bf16[96,384]{1,0:T(8,128)(2,1)S(1)}, u32[]{:S(2)}, u32[]{:S(2)}) collective-permute-start(bf16[96,384]{1,0:T(8,128)(2,1)S(1)} %get-tuple-element.45.refs_0_), channel_id=1, source_target_pairs={{0,15},{1,0},{2,1},{3,2},{4,3},{5,4},{6,5},{7,6},{8,7},{9,8},{10,9... | collective-permute-start | bytes 221192 | tf_op jit(solution)/shard_map/ppermute | solution.py:558
  65.5 6.5 %collective-permute-start.8 = (bf16[96,384]{1,0:T(8,128)(2,1)S(1)}, bf16[96,384]{1,0:T(8,128)(2,1)S(1)}, u32[]{:S(2)}, u32[]{:S(2)}) collective-permute-start(bf16[96,384]{1,0:T(8,128)(2,1)S(1)} %get-tuple-element.46.refs_1_), channel_id=1, source_target_pairs={{0,1},{1,2},{2,3},{3,4},{4,5},{5,6},{6,7},{7,8},{8,9},{9,10},{10,1... | collective-permute-start | bytes 221192 | tf_op jit(solution)/shard_map/ppermute | solution.py:558
  72.0 9.1 %copy-start.34 = (s32[1,384]{1,0:T(1,128)S(1)}, s32[1,384]{1,0:T(1,128)}, u32[]{:S(2)}) copy-start(s32[1,384]{1,0:T(1,128)} %refs_3_.5) | copy-start | bytes 4612
  77.6 7.5 %collective-permute-start.14 = (bf16[2,48,384]{2,1,0:T(8,128)(2,1)}, bf16[2,48,384]{2,1,0:T(8,128)(2,1)S(1)}, u32[]{:S(2)}, u32[]{:S(2)}) collective-permute-start(bf16[2,48,384]{2,1,0:T(8,128)(2,1)} %get-tuple-element.53), channel_id=1, source_target_pairs={{0,2},{1,3},{2,0},{3,1},{4,6},{5,7},{6,4},{7,5},{8,10},{9,11},{10,... | collective-permute-start | bytes 221192 | tf_op jit(solution)/shard_map/ppermute | solution.py:552
  77.6 7.5 %collective-permute-start.15 = (bf16[2,48,384]{2,1,0:T(8,128)(2,1)S(1)}, bf16[2,48,384]{2,1,0:T(8,128)(2,1)S(1)}, u32[]{:S(2)}, u32[]{:S(2)}) collective-permute-start(bf16[2,48,384]{2,1,0:T(8,128)(2,1)S(1)} %get-tuple-element.54), channel_id=1, source_target_pairs={{0,4},{1,5},{2,6},{3,7},{4,0},{5,1},{6,2},{7,3},{8,12},{9,13},{10,... | collective-permute-start | bytes 221192 | tf_op jit(solution)/shard_map/ppermute | solution.py:552
  77.6 7.5 %collective-permute-start.16 = (bf16[2,48,384]{2,1,0:T(8,128)(2,1)S(1)}, bf16[2,48,384]{2,1,0:T(8,128)(2,1)S(1)}, u32[]{:S(2)}, u32[]{:S(2)}) collective-permute-start(bf16[2,48,384]{2,1,0:T(8,128)(2,1)S(1)} %get-tuple-element.55), channel_id=1, source_target_pairs={{0,6},{1,7},{2,4},{3,5},{4,2},{5,3},{6,0},{7,1},{8,14},{9,15},{10,... | collective-permute-start | bytes 221192 | tf_op jit(solution)/shard_map/ppermute | solution.py:552
  81.1 1.2 %copy-start.36 = (bf16[384,1312]{0,1:T(8,128)(2,1)S(1)}, bf16[384,1312]{0,1:T(8,128)(2,1)}, u32[]{:S(2)}) copy-start(bf16[384,1312]{0,1:T(8,128)(2,1)} %param.25) | copy-start | bytes 3022852
  85.2 7.8 %collective-permute-start.17 = (bf16[4,48,384]{2,1,0:T(8,128)(2,1)S(1)}, bf16[4,48,384]{2,1,0:T(8,128)(2,1)S(1)}, u32[]{:S(2)}, u32[]{:S(2)}) collective-permute-start(bf16[4,48,384]{2,1,0:T(8,128)(2,1)S(1)} %shard_map.135), channel_id=1, source_target_pairs={{0,1},{1,0},{2,3},{3,2},{4,5},{5,4},{6,7},{7,6},{8,9},{9,8},{10,11... | collective-permute-start | bytes 442376 | tf_op jit(solution)/shard_map/ppermute | solution.py:552
  85.3 11.4 %collective-permute-start.10 = (bf16[2,48,384]{2,1,0:T(8,128)(2,1)S(1)}, bf16[2,48,384]{2,1,0:T(8,128)(2,1)S(1)}, u32[]{:S(2)}, u32[]{:S(2)}) collective-permute-start(bf16[2,48,384]{2,1,0:T(8,128)(2,1)S(1)} %get-tuple-element.48), channel_id=1, source_target_pairs={{0,8},{1,9},{2,10},{3,11},{4,12},{5,13},{6,14},{7,15},{8,0},{9,1},... | collective-permute-start | bytes 221192 | tf_op jit(solution)/shard_map/ppermute | solution.py:552
  85.3 13.1 %collective-permute-start.11 = (bf16[2,48,384]{2,1,0:T(8,128)(2,1)S(1)}, bf16[2,48,384]{2,1,0:T(8,128)(2,1)S(1)}, u32[]{:S(2)}, u32[]{:S(2)}) collective-permute-start(bf16[2,48,384]{2,1,0:T(8,128)(2,1)S(1)} %get-tuple-element.49), channel_id=1, source_target_pairs={{0,10},{1,11},{2,8},{3,9},{4,14},{5,15},{6,12},{7,13},{8,2},{9,3},... | collective-permute-start | bytes 221192 | tf_op jit(solution)/shard_map/ppermute | solution.py:552
  87.7 10.7 %collective-permute-start.12 = (bf16[2,48,384]{2,1,0:T(8,128)(2,1)S(1)}, bf16[2,48,384]{2,1,0:T(8,128)(2,1)S(1)}, u32[]{:S(2)}, u32[]{:S(2)}) collective-permute-start(bf16[2,48,384]{2,1,0:T(8,128)(2,1)S(1)} %get-tuple-element.50), channel_id=1, source_target_pairs={{0,12},{1,13},{2,14},{3,15},{4,8},{5,9},{6,10},{7,11},{8,4},{9,5},... | collective-permute-start | bytes 221192 | tf_op jit(solution)/shard_map/ppermute | solution.py:552
  89.0 9.5 %collective-permute-start.13 = (bf16[2,48,384]{2,1,0:T(8,128)(2,1)S(1)}, bf16[2,48,384]{2,1,0:T(8,128)(2,1)S(1)}, u32[]{:S(2)}, u32[]{:S(2)}) collective-permute-start(bf16[2,48,384]{2,1,0:T(8,128)(2,1)S(1)} %get-tuple-element.51), channel_id=1, source_target_pairs={{0,14},{1,15},{2,12},{3,13},{4,10},{5,11},{6,8},{7,9},{8,6},{9,7},... | collective-permute-start | bytes 221192 | tf_op jit(solution)/shard_map/ppermute | solution.py:552
  98.4 1.4 %collective-permute-start.18 = (bf16[4,48,384]{2,1,0:T(8,128)(2,1)S(1)}, bf16[4,48,384]{2,1,0:T(8,128)(2,1)S(1)}, u32[]{:S(2)}, u32[]{:S(2)}) collective-permute-start(bf16[4,48,384]{2,1,0:T(8,128)(2,1)S(1)} %shard_map.137), channel_id=1, source_target_pairs={{0,1},{1,0},{2,3},{3,2},{4,5},{5,4},{6,7},{7,6},{8,9},{9,8},{10,11... | collective-permute-start | bytes 442376 | tf_op jit(solution)/shard_map/ppermute | solution.py:552
  (10 other events, 8.1 us)

commit v2 on v1

--- a/solution.py
+++ b/solution.py
@@ -224,21 +224,15 @@
     return hit.astype(F32).astype(BF16)
 
 
-def prep_kernel(cap, direct, me_ref, loads, outs, scratch):
-    recv, weight, embed, rel = (one() for one in loads)
-    mix_ref, *scatter_refs, embed_out, bias_ref, select_ref = outs
-    kk, pd = recv.shape
+def tables_kernel(cap, direct, me_ref, loads, outs, scratch):
+    recv, embed, rel = (one() for one in loads)
+    *scatter_refs, embed_out, bias_ref, select_ref = outs
+    pd = recv.shape[1]
     slots = 2 * pd
-    pixsq = weight.shape[1] // kk
-    pix = int(round(pixsq**0.5))
+    pix = embed_out.shape[0] // LANES
     ch = embed.shape[0] // pix
-    sender, inner = split_slots(recv, cap, me_ref[0])
-    slot = sender * cap + inner
-    for level in range(2):
-        total = weights_by_slot(slot, weight, slots, level)
-        store_spread(mix_ref, spread(total.astype(BF16), True, pix), level * pix * GROUP, 0, pix)
     turn = patch_turn(pd)
-    parts = [v.astype(F32).astype(BF16) for v in (sender, inner)]
+    parts = [v.astype(F32).astype(BF16) for v in split_slots(recv, cap, me_ref[0])]
     cols = (mm_nt(turn, parts[0]) * cap + mm_nt(turn, parts[1])).astype(jnp.int32)
     rows = (mm_nt(parts[0], turn) * cap + mm_nt(parts[1], turn)).astype(jnp.int32)
     select_ref[...] = chosen((2 * slots, pd), 0, lambda k: rows[k : k + 1, :])
@@ -249,6 +243,16 @@
         lo, hi, move = tile_move(ch, i, embed.shape[0])
         embed_out[i * LANES : (i + 1) * LANES, :] = mm_tn(move, embed[lo:hi, :]).astype(BF16)
     bias_rows(rel, scratch[0], bias_ref)
+
+
+def mix_kernel(cap, me_ref, loads, outs, scratch):
+    recv, weight = (one() for one in loads)
+    slots = 2 * recv.shape[1]
+    pix = int(round((weight.shape[1] // recv.shape[0]) ** 0.5))
+    sender, inner = split_slots(recv, cap, me_ref[0])
+    for level in range(2):
+        total = weights_by_slot(sender * cap + inner, weight, slots, level)
+        store_spread(outs[0], spread(total.astype(BF16), True, pix), level * pix * GROUP, 0, pix)
 
 
 def prep_back_kernel(size, me_ref, loads, outs, scratch):
@@ -408,19 +412,28 @@
     outs[1][...] = new[half:]
 
 
+def turned(low, high):
+    shift = low.shape[0] * (WIN // 2) // ROWS
+    turn = lambda v: jnp.concatenate([v[shift:], v[:shift]], axis=0)
+    return jnp.concatenate([turn(low[...]), turn(high[...])], axis=0).astype(F32)
+
+
+def own_kernel(layer, loads, outs, scratch):
+    low, high, gain1, qkv = loads
+    normed = layer_norm(turned(low(), high()), gain1()[layer : layer + 1, :]).astype(BF16)
+    outs[0][...] = mm(normed, qkv()[...]).astype(BF16)
+
+
 def second_kernel(layer, loads, outs, scratch):
-    low, high, gain1, gain2, qkv, bias, left, right, proj, up, down, select = loads
+    packed, low, high, gain1, gain2, qkv, bias, left, right, proj, up, down, select = loads
     half, d = low.ref.shape
     heads = bias.ref.shape[1] // (WIN * WIN)
     shift = half * (WIN // 2) // ROWS
-    turn = lambda v: jnp.concatenate([v[shift:], v[:shift]], axis=0)
     back = lambda v: jnp.concatenate([v[half - shift :], v[: half - shift]], axis=0)
-    own = jnp.concatenate([turn(low()[...]), turn(high()[...])], axis=0).astype(F32)
+    own = turned(low(), high())
     gain = gain1()[layer : layer + 1, :]
-    normed = layer_norm(own, gain).astype(BF16)
-    strips = jnp.concatenate([turn(left()[...]), turn(right()[...])], axis=0).astype(F32)
-    normed_s = layer_norm(strips, gain).astype(BF16)
-    packed = mm(normed, qkv()[...]).astype(BF16)
+    normed_s = layer_norm(turned(left(), right()), gain).astype(BF16)
+    packed = packed()[...]
     packed_s = mm(normed_s, qkv()[:, d:]).astype(BF16)
     query, key, value = packed[:, :d], packed[:, d : 2 * d], packed[:, 2 * d :]
     key_s, value_s = packed_s[:, :d], packed_s[:, d:]
@@ -588,7 +601,7 @@
         turns = [*range(NEAR, chips), *range(NEAR - 1, 0, -1)]
 
         outgoing = call(pick_direct_kernel, [In(send_table), In(bands)],
-                        [sds((2, cap, width), BF16)] * chips, [vm((count, cap, width), BF16)], my)
+                        [sds((2, cap, width), BF16)] * chips, [vm((count, cap, width), BF16)], my, flops=1e10)
         came = [outgoing[0]] + [None] * (chips - 1)
         for s in turns:
             came[s] = flip(outgoing[s], "tile", 2 * s)
@@ -599,15 +612,16 @@
     heads = rel_bias.shape[1]
     span = WIN * WIN
     wsend = call(weights_kernel, [In(recv_table), In(regrid_weight)], [sds((2 * slots, pixsq), BF16)],
-                 flops=2e8, after=[outgoing[0] if direct else outgoing])
+                 flops=1e10, after=[outgoing[0] if direct else outgoing])
     wback = swap_pairs(wsend, "tile")
-    mix, scatter_a, scatter_b, embed_pad, bias, select = call(
-        functools.partial(prep_kernel, cap, direct),
-        [In(recv_table), In(regrid_weight), In(embed_weight), In(rel_bias.transpose(1, 0, 2))],
-        [sds((slots // GROUP, 2 * pix * GROUP, pix * GROUP), BF16), sds((pd, slots // 2), BF16), sds((pd, 3 * slots // 2), BF16),
-         sds((wide, d), BF16), sds((rel_bias.shape[0], span, heads * span), F32),
-         sds((2 * slots, pd), BF16)],
-        [vm((heads, 2 * LANES), F32)], my, flops=4e9, after=[wsend])
+    scatter_a, scatter_b, embed_pad, bias, select = call(
+        functools.partial(tables_kernel, cap, direct),
+        [In(recv_table), In(embed_weight), In(rel_bias.transpose(1, 0, 2))],
+        [sds((pd, slots // 2), BF16), sds((pd, 3 * slots // 2), BF16), sds((wide, d), BF16),
+         sds((rel_bias.shape[0], span, heads * span), F32), sds((2 * slots, pd), BF16)],
+        [vm((heads, 2 * LANES), F32)], my, flops=2e9, after=[wsend])
+    mix = call(functools.partial(mix_kernel, cap), [In(recv_table), In(regrid_weight)],
+               [sds((slots // GROUP, 2 * pix * GROUP, pix * GROUP), BF16)], (), my, flops=2e9, after=[embed_pad])
 
     def relay(arrays, after=()):
         shape = (len(arrays), *arrays[0].shape[1:])
@@ -642,10 +656,12 @@
     right = from_behind(low, "tile", -1)
     left = from_behind(high, "tile", 1)
     ins_a, ins_b = layer(1)
+    packed = call(functools.partial(own_kernel, 1), [In(low), In(high), In(norm1_gain), at(qkv_weight, 1)],
+                  [sds((pd, 3 * d), BF16)], flops=2e8)
     rows = 2 * cap
     sent = call(
         functools.partial(second_kernel, 1),
-        [In(low), In(high), *ins_a, In(left), In(right), *ins_b, In(select)],
+        [In(packed), In(low), In(high), *ins_a, In(left), In(right), *ins_b, In(select)],
         [sds((2, rows, d), BF16)] * chips if direct else [sds((2 * slots, d), BF16)], flops=2e9)
     one_sent = sent[0] if direct else sent
     size = cap // GROUP if direct else None
@@ -659,7 +675,8 @@
         got = [sent[0]] + [None] * (chips - 1)
         for s in turns:
             got[s] = flip(sent[s], "tile", 2 * s)
-        near_pass = flip(relay(got[:NEAR], [mix_back]), "tile", 1)
+        near_all = relay(got[:NEAR], [mix_back])
+        near_pass = flip(near_all, "tile", 1)
         near = [y for i, x in enumerate(got[:NEAR]) for y in (at(x, 0), at(near_pass, i))]
     else:
         got = swap_pairs(sent, "tile").reshape(STAGES, 2 * per, d)

time: 106 us -> 103 us (0.972)
  local copies, waits for them, and re-layouts: 22.1 us -> 17.2 us
  starting transfers between devices: 35.1 us -> 36.6 us
  Pallas kernels: 30.3 us -> 31.4 us
    unnamed x76 -> x64, local copies, waits for them, and re-layouts: 22.1 us -> 17.2 us
    all_to_all x1, starting transfers between devices: 6.81 us -> 8.25 us  [swap(): return lax.all_to_all(value, axis, split_axis=0, concat_axis=0, tiled=True)]
    pallas_call x12 -> x14, Pallas kernels: 30.3 us -> 31.4 us  [call(): pl.pallas_call(run, out_shape=list(outs), in_specs=in_specs + [vmem] * le...]
  transfers between devices with their start and end apart: 20 -> 20, of which waited for: 8 -> 6; matrix products, arithmetic and copies ran while one was open for 0% -> 0% of each run, Pallas kernels for 24% -> 25%
where the time goes in v2:
time: 103 us; the launch traced here: 102 us
  starting transfers between devices  36.6 us (36%)
  Pallas kernels  31.4 us (30%)
  local copies, waits for them, and re-layouts  17.2 us (17%)
  waiting for transfers between devices  16.2 us (16%)
    pallas_call x14, Pallas kernels, call(): pl.pallas_call(run, out_shape=list(outs), in_specs=in_specs + [vmem] * le...  31.4 us
    ppermute x17, starting transfers between devices, flip(): lax.ppermute(value, axis, [(source, source ^ bits) for source in range(co...  24 us
    unnamed x64, local copies, waits for them, and re-layouts  17.2 us
    ppermute x17, waiting for transfers between devices, flip(): lax.ppermute(value, axis, [(source, source ^ bits) for source in range(co...  10.3 us
    all_to_all x1, starting transfers between devices, swap(): return lax.all_to_all(value, axis, split_axis=0, concat_axis=0, tiled=True)  8.25 us
    ppermute x2, waiting for transfers between devices, from_behind(): return lax.ppermute(value, axis, pairs)  5.87 us
    ppermute x2, starting transfers between devices, from_behind(): return lax.ppermute(value, axis, pairs)  4.35 us
  transfers between devices with their start and end apart: 20, of which 6 were waited for; matrix products, arithmetic and copies ran while one was open for 0% of the time, Pallas kernels for 25%

profile of v2, /device:TPU:0, one launch (start us, length us, event | category | flops | bytes accessed | tf_op | source)
XLA Modules:
  0.0 101.7 jit_solution(9265136267323338073)
XLA Ops:
  0.0 1.0 %copy-done.26 = bf16[192,1312]{1,0:T(8,128)(2,1)S(1)} copy-done((bf16[192,1312]{1,0:T(8,128)(2,1)S(1)}, bf16[192,1312]{1,0:T(8,128)(2,1)}, u32[]{:S(2)}) %copy-start.26) | copy-done | bytes 503832
  1.1 0.7 copy-done.30
  1.7 0.6 shard_map.127
  2.3 3.1 %collective-permute-start = (bf16[2,24,1312]{2,1,0:T(8,128)(2,1)S(1)}, bf16[2,24,1312]{2,1,0:T(8,128)(2,1)S(1)}, u32[]{:S(2)}, u32[]{:S(2)}) collective-permute-start(bf16[2,24,1312]{2,1,0:T(8,128)(2,1)S(1)} %get-tuple-element.32), channel_id=1, source_target_pairs={{0,2},{1,3},{2,0},{3,1},{4,6},{5,7},{6,4},{7,5},{8,10},{9,11},{10,... | collective-permute-start | bytes 377864 | tf_op jit(solution)/shard_map/ppermute | solution.py:565
  5.4 1.6 %collective-permute-start.1 = (bf16[2,24,1312]{2,1,0:T(8,128)(2,1)S(1)}, bf16[2,24,1312]{2,1,0:T(8,128)(2,1)S(1)}, u32[]{:S(2)}, u32[]{:S(2)}) collective-permute-start(bf16[2,24,1312]{2,1,0:T(8,128)(2,1)S(1)} %get-tuple-element.33), channel_id=1, source_target_pairs={{0,4},{1,5},{2,6},{3,7},{4,0},{5,1},{6,2},{7,3},{8,12},{9,13},{10,... | collective-permute-start | bytes 377864 | tf_op jit(solution)/shard_map/ppermute | solution.py:565
  7.0 3.0 %collective-permute-start.3 = (bf16[2,24,1312]{2,1,0:T(8,128)(2,1)S(1)}, bf16[2,24,1312]{2,1,0:T(8,128)(2,1)S(1)}, u32[]{:S(2)}, u32[]{:S(2)}) collective-permute-start(bf16[2,24,1312]{2,1,0:T(8,128)(2,1)S(1)} %get-tuple-element.35), channel_id=1, source_target_pairs={{0,8},{1,9},{2,10},{3,11},{4,12},{5,13},{6,14},{7,15},{8,0},{9,1},... | collective-permute-start | bytes 377864 | tf_op jit(solution)/shard_map/ppermute | solution.py:565
  9.9 1.3 %collective-permute-start.4 = (bf16[2,24,1312]{2,1,0:T(8,128)(2,1)S(1)}, bf16[2,24,1312]{2,1,0:T(8,128)(2,1)S(1)}, u32[]{:S(2)}, u32[]{:S(2)}) collective-permute-start(bf16[2,24,1312]{2,1,0:T(8,128)(2,1)S(1)} %get-tuple-element.36), channel_id=1, source_target_pairs={{0,10},{1,11},{2,8},{3,9},{4,14},{5,15},{6,12},{7,13},{8,2},{9,3},... | collective-permute-start | bytes 377864 | tf_op jit(solution)/shard_map/ppermute | solution.py:565
  11.2 0.4 shard_map.128.refs_4_
  11.6 0.8 copy-done.24
  12.4 2.4 %shard_map.129 = (bf16[192,192]{1,0:T(8,128)(2,1)S(1)}, bf16[192,576]{1,0:T(8,128)(2,1)S(1)}, bf16[2048,384]{1,0:T(8,128)(2,1)S(1)}, f32[2,64,768]{2,1,0:T(8,128)S(1)}, bf16[768,192]{1,0:T(8,128)(2,1)S(1)}) custom-call(s32[1]{0:T(128)} %bitcast.refs_0_, s32[4,192]{1,0:T(4,128)S(1)} %copy-done.29, bf16[1312,384]{1,0:T(8,128)(2,1)S(1)} %copy-done.24, ...), custom_call_target="tpu_custom_call" | custom-call | flops 2000000000 | bytes 1032288 | tf_op jit(solution)/shard_map/pallas_call | solution.py:74
  14.9 0.7 copy-done.17
  15.6 0.7 copy-done.20
  16.3 1.4 %shard_map.130.refs_4_.refs_12_ = bf16[48,256,128]{2,1,0:T(8,128)(2,1)S(1)} custom-call(s32[1]{0:T(128)} %bitcast.refs_0_, s32[4,192]{1,0:T(4,128)S(1)} %copy-done.29, bf16[192,1024]{1,0:T(8,128)(2,1)S(1)} %copy-done.27, bf16[2048,384]{1,0:T(8,128)(2,1)S(1)} %get-tuple-element.39.refs_3_.refs_6_.refs_14_), custom_call_target="tpu_custom_call" | custom-call | flops 2000000000 | bytes 396288 | tf_op jit(solution)/shard_map/pallas_call | solution.py:74
  17.8 3.7 %collective-permute-start.5 = (bf16[2,24,1312]{2,1,0:T(8,128)(2,1)S(1)}, bf16[2,24,1312]{2,1,0:T(8,128)(2,1)S(1)}, u32[]{:S(2)}, u32[]{:S(2)}) collective-permute-start(bf16[2,24,1312]{2,1,0:T(8,128)(2,1)S(1)} %get-tuple-element.37), channel_id=1, source_target_pairs={{0,12},{1,13},{2,14},{3,15},{4,8},{5,9},{6,10},{7,11},{8,4},{9,5},... | collective-permute-start | bytes 377864 | tf_op jit(solution)/shard_map/ppermute | solution.py:565
  21.5 2.6 %shard_map.131.refs_8_.refs_15_ = f32[192,384]{1,0:T(8,128)S(1)} custom-call(bf16[2,24,1312]{2,1,0:T(8,128)(2,1)S(1)} %get-tuple-element.31.refs_2_.refs_0_, bf16[2,24,1312]{2,1,0:T(8,128)(2,1)S(1)} %collective-permute-done.refs_1_, bf16[2,24,1312]{2,1,0:T(8,128)(2,1)S(1)} %collective-permute-done.1.refs_2_, ...), custom_call_target="tpu_custom_call" | custom-call | flops 2000000000 | bytes 5296128 | tf_op jit(solution)/shard_map/pallas_call | solution.py:74
  24.1 5.7 %collective-permute-done.4.refs_5_.refs_6_ = bf16[2,24,1312]{2,1,0:T(8,128)(2,1)S(1)} collective-permute-done((bf16[2,24,1312]{2,1,0:T(8,128)(2,1)S(1)}, bf16[2,24,1312]{2,1,0:T(8,128)(2,1)S(1)}, u32[]{:S(2)}, u32[]{:S(2)}) %collective-permute-start.4) | collective-permute-done | bytes 125984 | tf_op jit(solution)/shard_map/ppermute | solution.py:565
  29.9 0.9 shard_map.132
  30.8 0.7 copy-done.9
  31.5 8.2 %all-to-all-start = ((bf16[16,48,256]{2,1,0:T(8,128)(2,1)}), bf16[16,48,256]{2,1,0:T(8,128)(2,1)}, u32[]{:S(2)}, u32[]{:S(2)}) async-start(bf16[16,48,256]{2,1,0:T(8,128)(2,1)} %bitcast.5), calls=%async_computation | async-start | bytes 786432 | tf_op jit(solution)/shard_map/all_to_all | solution.py:547
  39.8 1.7 %copy-done.1 = bf16[2,384,1536]{2,1,0:T(8,128)(2,1)S(1)} copy-done((bf16[2,384,1536]{2,1,0:T(8,128)(2,1)S(1)}, bf16[2,384,1536]{2,1,0:T(8,128)(2,1)}, u32[]{:S(2)}) %copy-start.1) | copy-done | bytes 2359320
  41.5 1.7 %copy-done.3 = bf16[2,1536,384]{2,1,0:T(8,128)(2,1)S(1)} copy-done((bf16[2,1536,384]{2,1,0:T(8,128)(2,1)S(1)}, bf16[2,1536,384]{2,1,0:T(8,128)(2,1)}, u32[]{:S(2)}) %copy-start.3) | copy-done | bytes 2359320
  43.2 1.9 %copy-done.5 = bf16[48,256,128]{2,1,0:T(8,128)(2,1)S(1)} copy-done((bf16[48,256,128]{2,1,0:T(8,128)(2,1)S(1)}, bf16[48,256,128]{2,1,0:T(8,128)(2,1)}, u32[]{:S(2)}) %copy-start.5) | copy-done | bytes 3145752
  45.1 1.4 %copy-done.8 = bf16[2048,384]{1,0:T(8,128)(2,1)S(1)} copy-done((bf16[2048,384]{1,0:T(8,128)(2,1)S(1)}, bf16[2048,384]{1,0:T(8,128)(2,1)}, u32[]{:S(2)}) %copy-start.8) | copy-done | bytes 1572888
  46.5 1.0 copy-done.10
  47.4 0.9 copy-done.12
  48.3 0.9 copy-done.14
  49.2 0.9 copy-done.16
  50.2 0.9 copy-done.21
  51.1 8.4 %shard_map.133 = (bf16[96,384]{1,0:T(8,128)(2,1)S(1)}, bf16[96,384]{1,0:T(8,128)(2,1)S(1)}) custom-call(bf16[8,24,1312]{2,1,0:T(8,128)(2,1)S(1)} %collective-permute-done.7.refs_0_.refs_1_.refs_2_.refs_3_.refs_5_.refs_7_.refs_9_.refs_11_, bf16[8,24,1312]{2,1,0:T(8,128)(2,1)S(1)} %collective-permute-done.7.refs_0_.refs_1_.refs_2_.refs_3_.refs_5_.refs_7_.refs_9_.refs_11_, ...), custom_call_target="tpu_custom_call" | custom-call | flops 4000000000 | bytes 17246208 | tf_op jit(solution)/shard_map/pallas_call | solution.py:74
  59.5 4.3 %collective-permute-start.9 = (bf16[96,384]{1,0:T(8,128)(2,1)S(1)}, bf16[96,384]{1,0:T(8,128)(2,1)S(1)}, u32[]{:S(2)}, u32[]{:S(2)}) collective-permute-start(bf16[96,384]{1,0:T(8,128)(2,1)S(1)} %get-tuple-element.43.refs_0_.refs_1_), channel_id=1, source_target_pairs={{0,15},{1,0},{2,1},{3,2},{4,3},{5,4},{6,5},{7,6},{8,7},{9,8},{10,9... | collective-permute-start | bytes 221192 | tf_op jit(solution)/shard_map/ppermute | solution.py:571
  63.9 0.6 shard_map.134.refs_0_
  64.5 1.4 %collective-permute-done.9.refs_8_ = bf16[96,384]{1,0:T(8,128)(2,1)S(1)} collective-permute-done((bf16[96,384]{1,0:T(8,128)(2,1)S(1)}, bf16[96,384]{1,0:T(8,128)(2,1)S(1)}, u32[]{:S(2)}, u32[]{:S(2)}) %collective-permute-start.9) | collective-permute-done | bytes 73760 | tf_op jit(solution)/shard_map/ppermute | solution.py:571
  65.8 4.5 %collective-permute-done.8.refs_7_ = bf16[96,384]{1,0:T(8,128)(2,1)S(1)} collective-permute-done((bf16[96,384]{1,0:T(8,128)(2,1)S(1)}, bf16[96,384]{1,0:T(8,128)(2,1)S(1)}, u32[]{:S(2)}, u32[]{:S(2)}) %collective-permute-start.8) | collective-permute-done | bytes 73760 | tf_op jit(solution)/shard_map/ppermute | solution.py:571
  70.3 4.9 %shard_map.135 = (bf16[2,48,384]{2,1,0:T(8,128)(2,1)S(1)}, bf16[2,48,384]{2,1,0:T(8,128)(2,1)S(1)}, bf16[2,48,384]{2,1,0:T(8,128)(2,1)S(1)}, bf16[2,48,384]{2,1,...) custom-call(bf16[192,1152]{1,0:T(8,128)(2,1)S(1)} %shard_map.134.ref, ...), custom_call_target="tpu_custom_call" | custom-call | flops 2000000000 | bytes 8509440 | tf_op jit(solution)/shard_map/pallas_call | solution.py:74
  75.2 0.1 collective-permute-start.14
  75.4 3.4 %collective-permute-start.16 = (bf16[2,48,384]{2,1,0:T(8,128)(2,1)S(1)}, bf16[2,48,384]{2,1,0:T(8,128)(2,1)S(1)}, u32[]{:S(2)}, u32[]{:S(2)}) collective-permute-start(bf16[2,48,384]{2,1,0:T(8,128)(2,1)S(1)} %get-tuple-element.53), channel_id=1, source_target_pairs={{0,6},{1,7},{2,4},{3,5},{4,2},{5,3},{6,0},{7,1},{8,14},{9,15},{10,... | collective-permute-start | bytes 221192 | tf_op jit(solution)/shard_map/ppermute | solution.py:565
  78.8 1.2 %copy-done.25 = bf16[384,1312]{0,1:T(8,128)(2,1)S(1)} copy-done((bf16[384,1312]{0,1:T(8,128)(2,1)S(1)}, bf16[384,1312]{0,1:T(8,128)(2,1)}, u32[]{:S(2)}) %copy-start.25) | copy-done | bytes 1007640
  80.0 2.8 %shard_map.136 = (bf16[48,128,256]{2,1,0:T(8,128)(2,1)S(1)}, bf16[2048,384]{1,0:T(8,128)(2,1)S(1)}, s32[8,384]{1,0:T(8,128)S(1)}) custom-call(s32[1]{0:T(128)} %bitcast.refs_0_, bf16[768,256]{1,0:T(8,128)(2,1)} %bitcast.3.refs_1_, bf16[1312,384]{1,0:T(8,128)(2,1)S(1)} %bitcast.6, s32[1,384]{1,0:T(1,128)S(1)} %copy-done.31, ...), custom_call_target="tpu_custom_call" | custom-call | flops 2000000000 | bytes 1402368 | tf_op jit(solution)/shard_map/pallas_call | solution.py:74
  82.9 0.1 collective-permute-start.10
  83.0 2.4 %collective-permute-start.11 = (bf16[2,48,384]{2,1,0:T(8,128)(2,1)S(1)}, bf16[2,48,384]{2,1,0:T(8,128)(2,1)S(1)}, u32[]{:S(2)}, u32[]{:S(2)}) collective-permute-start(bf16[2,48,384]{2,1,0:T(8,128)(2,1)S(1)} %get-tuple-element.47), channel_id=1, source_target_pairs={{0,10},{1,11},{2,8},{3,9},{4,14},{5,15},{6,12},{7,13},{8,2},{9,3},... | collective-permute-start | bytes 221192 | tf_op jit(solution)/shard_map/ppermute | solution.py:565
  85.4 1.2 %collective-permute-start.12 = (bf16[2,48,384]{2,1,0:T(8,128)(2,1)S(1)}, bf16[2,48,384]{2,1,0:T(8,128)(2,1)S(1)}, u32[]{:S(2)}, u32[]{:S(2)}) collective-permute-start(bf16[2,48,384]{2,1,0:T(8,128)(2,1)S(1)} %get-tuple-element.48), channel_id=1, source_target_pairs={{0,12},{1,13},{2,14},{3,15},{4,8},{5,9},{6,10},{7,11},{8,4},{9,5},... | collective-permute-start | bytes 221192 | tf_op jit(solution)/shard_map/ppermute | solution.py:565
  86.6 4.0 %collective-permute-start.13 = (bf16[2,48,384]{2,1,0:T(8,128)(2,1)S(1)}, bf16[2,48,384]{2,1,0:T(8,128)(2,1)S(1)}, u32[]{:S(2)}, u32[]{:S(2)}) collective-permute-start(bf16[2,48,384]{2,1,0:T(8,128)(2,1)S(1)} %get-tuple-element.49), channel_id=1, source_target_pairs={{0,14},{1,15},{2,12},{3,13},{4,10},{5,11},{6,8},{7,9},{8,6},{9,7},... | collective-permute-start | bytes 221192 | tf_op jit(solution)/shard_map/ppermute | solution.py:565
  90.6 2.4 %shard_map.138.refs_4_.refs_11_ = bf16[192,2048]{1,0:T(8,128)(2,1)S(1)} custom-call(s32[1]{0:T(128)} %bitcast.refs_0_, bf16[2,48,384]{2,1,0:T(8,128)(2,1)S(1)} %get-tuple-element.50.refs_4_.refs_0_.refs_1_, bf16[4,48,384]{2,1,0:T(8,128)(2,1)S(1)} %collective-permute-done.17.refs_2_.refs_4_.refs_6_.refs_8_, ...), custom_call_target="tpu_custom_call" | custom-call | flops 2000000000 | bytes 5603328 | tf_op jit(solution)/shard_map/pallas_call | solution.py:74
  93.1 1.2 %collective-permute-done.10.refs_0_.refs_1_ = bf16[2,48,384]{2,1,0:T(8,128)(2,1)S(1)} collective-permute-done((bf16[2,48,384]{2,1,0:T(8,128)(2,1)S(1)}, bf16[2,48,384]{2,1,0:T(8,128)(2,1)S(1)}, u32[]{:S(2)}, u32[]{:S(2)}) %collective-permute-start.10) | collective-permute-done | bytes 73760 | tf_op jit(solution)/shard_map/ppermute | solution.py:565
  94.3 1.9 %collective-permute-done.11.refs_1_.refs_3_ = bf16[2,48,384]{2,1,0:T(8,128)(2,1)S(1)} collective-permute-done((bf16[2,48,384]{2,1,0:T(8,128)(2,1)S(1)}, bf16[2,48,384]{2,1,0:T(8,128)(2,1)S(1)}, u32[]{:S(2)}, u32[]{:S(2)}) %collective-permute-start.11) | collective-permute-done | bytes 73760 | tf_op jit(solution)/shard_map/ppermute | solution.py:565
  96.3 0.1 collective-permute-start.18
  96.3 1.4 %collective-permute-done.18.refs_2_.refs_4_.refs_6_.refs_8_ = bf16[4,48,384]{2,1,0:T(8,128)(2,1)S(1)} collective-permute-done((bf16[4,48,384]{2,1,0:T(8,128)(2,1)S(1)}, bf16[4,48,384]{2,1,0:T(8,128)(2,1)S(1)}, u32[]{:S(2)}, u32[]{:S(2)}) %collective-permute-start.18) | collective-permute-done | bytes 147488 | tf_op jit(solution)/shard_map/ppermute | solution.py:565
  97.7 4.0 %shard_map.140 = f32[192,1312]{1,0:T(8,128)} custom-call(s32[1]{0:T(128)} %bitcast.refs_0_, bf16[2,48,384]{2,1,0:T(8,128)(2,1)S(1)} %collective-permute-done.10.refs_0_.refs_1_, bf16[4,48,384]{2,1,0:T(8,128)(2,1)S(1)} %collective-permute-done.18.refs_2_.refs_4_.refs_6_.refs_8_, bf16[2,48,384]{2,1,0:T(8,128)(2,1)S(1)} %collective-permute-done.11.refs_1_.refs_3_, ...), custom_call_target="tpu_custom_call" | custom-call | flops 3000000000 | bytes 6402048 | tf_op jit(solution)/shard_map/pallas_call | solution.py:74
  (70 shorter events, 0.3 us)
Async XLA Ops:
  0.0 1.0 %copy-start.26 = (bf16[192,1312]{1,0:T(8,128)(2,1)S(1)}, bf16[192,1312]{1,0:T(8,128)(2,1)}, u32[]{:S(2)}) copy-start(bf16[192,1312]{1,0:T(8,128)(2,1)} %refs_2_.4) | copy-start | bytes 1511428
  1.7 9.5 %copy-start.27 = (bf16[192,1024]{1,0:T(8,128)(2,1)S(1)}, bf16[192,1024]{1,0:T(8,128)(2,1)}, u32[]{:S(2)}) copy-start(bf16[192,1024]{1,0:T(8,128)(2,1)} %refs_2_.6) | copy-start | bytes 1179652
  1.7 9.5 %copy-start.29 = (s32[4,192]{1,0:T(4,128)S(1)}, s32[4,192]{1,0:T(4,128)}, u32[]{:S(2)}) copy-start(s32[4,192]{1,0:T(4,128)} %refs_1_.7) | copy-start | bytes 9220
  2.3 15.5 %collective-permute-start = (bf16[2,24,1312]{2,1,0:T(8,128)(2,1)S(1)}, bf16[2,24,1312]{2,1,0:T(8,128)(2,1)S(1)}, u32[]{:S(2)}, u32[]{:S(2)}) collective-permute-start(bf16[2,24,1312]{2,1,0:T(8,128)(2,1)S(1)} %get-tuple-element.32), channel_id=1, source_target_pairs={{0,2},{1,3},{2,0},{3,1},{4,6},{5,7},{6,4},{7,5},{8,10},{9,11},{10,... | collective-permute-start | bytes 377864 | tf_op jit(solution)/shard_map/ppermute | solution.py:565
  5.4 16.1 %collective-permute-start.1 = (bf16[2,24,1312]{2,1,0:T(8,128)(2,1)S(1)}, bf16[2,24,1312]{2,1,0:T(8,128)(2,1)S(1)}, u32[]{:S(2)}, u32[]{:S(2)}) collective-permute-start(bf16[2,24,1312]{2,1,0:T(8,128)(2,1)S(1)} %get-tuple-element.33), channel_id=1, source_target_pairs={{0,4},{1,5},{2,6},{3,7},{4,0},{5,1},{6,2},{7,3},{8,12},{9,13},{10,... | collective-permute-start | bytes 377864 | tf_op jit(solution)/shard_map/ppermute | solution.py:565
  7.0 14.5 %collective-permute-start.2 = (bf16[2,24,1312]{2,1,0:T(8,128)(2,1)S(1)}, bf16[2,24,1312]{2,1,0:T(8,128)(2,1)S(1)}, u32[]{:S(2)}, u32[]{:S(2)}) collective-permute-start(bf16[2,24,1312]{2,1,0:T(8,128)(2,1)S(1)} %get-tuple-element.34), channel_id=1, source_target_pairs={{0,6},{1,7},{2,4},{3,5},{4,2},{5,3},{6,0},{7,1},{8,14},{9,15},{10,... | collective-permute-start | bytes 377864 | tf_op jit(solution)/shard_map/ppermute | solution.py:565
  7.0 17.2 %collective-permute-start.3 = (bf16[2,24,1312]{2,1,0:T(8,128)(2,1)S(1)}, bf16[2,24,1312]{2,1,0:T(8,128)(2,1)S(1)}, u32[]{:S(2)}, u32[]{:S(2)}) collective-permute-start(bf16[2,24,1312]{2,1,0:T(8,128)(2,1)S(1)} %get-tuple-element.35), channel_id=1, source_target_pairs={{0,8},{1,9},{2,10},{3,11},{4,12},{5,13},{6,14},{7,15},{8,0},{9,1},... | collective-permute-start | bytes 377864 | tf_op jit(solution)/shard_map/ppermute | solution.py:565
  9.9 19.9 %collective-permute-start.4 = (bf16[2,24,1312]{2,1,0:T(8,128)(2,1)S(1)}, bf16[2,24,1312]{2,1,0:T(8,128)(2,1)S(1)}, u32[]{:S(2)}, u32[]{:S(2)}) collective-permute-start(bf16[2,24,1312]{2,1,0:T(8,128)(2,1)S(1)} %get-tuple-element.36), channel_id=1, source_target_pairs={{0,10},{1,11},{2,8},{3,9},{4,14},{5,15},{6,12},{7,13},{8,2},{9,3},... | collective-permute-start | bytes 377864 | tf_op jit(solution)/shard_map/ppermute | solution.py:565
  11.2 1.2 %copy-start.24 = (bf16[1312,384]{1,0:T(8,128)(2,1)S(1)}, bf16[1312,384]{1,0:T(8,128)(2,1)}, u32[]{:S(2)}) copy-start(bf16[1312,384]{1,0:T(8,128)(2,1)} %refs_2_.5) | copy-start | bytes 3022852
  11.2 1.2 %copy-start.28 = (f32[2,12,225]{2,0,1:T(2,128)S(1)}, f32[2,12,225]{2,0,1:T(2,128)}, u32[]{:S(2)}) copy-start(f32[2,12,225]{2,0,1:T(2,128)} %param.20) | copy-start | bytes 64804
  11.6 3.3 %copy-start.19 = (bf16[768,256]{1,0:T(8,128)(2,1)}, bf16[768,256]{1,0:T(8,128)(2,1)S(1)}, u32[]{:S(2)}) copy-start(bf16[768,256]{1,0:T(8,128)(2,1)S(1)} %shard_map.128.refs_4_) | copy-start | bytes 1179652
  16.3 5.2 %copy-start.7 = (bf16[2048,384]{1,0:T(8,128)(2,1)}, bf16[2048,384]{1,0:T(8,128)(2,1)S(1)}, u32[]{:S(2)}) copy-start(bf16[2048,384]{1,0:T(8,128)(2,1)S(1)} %get-tuple-element.39.refs_3_.refs_6_.refs_14_) | copy-start | bytes 4718596
  17.8 6.3 %copy-start.4 = (bf16[48,256,128]{2,1,0:T(8,128)(2,1)}, bf16[48,256,128]{2,1,0:T(8,128)(2,1)S(1)}, u32[]{:S(2)}) copy-start(bf16[48,256,128]{2,1,0:T(8,128)(2,1)S(1)} %shard_map.130.refs_4_.refs_12_) | copy-start | bytes 9437188
  17.8 12.1 %collective-permute-start.5 = (bf16[2,24,1312]{2,1,0:T(8,128)(2,1)S(1)}, bf16[2,24,1312]{2,1,0:T(8,128)(2,1)S(1)}, u32[]{:S(2)}, u32[]{:S(2)}) collective-permute-start(bf16[2,24,1312]{2,1,0:T(8,128)(2,1)S(1)} %get-tuple-element.37), channel_id=1, source_target_pairs={{0,12},{1,13},{2,14},{3,15},{4,8},{5,9},{6,10},{7,11},{8,4},{9,5},... | collective-permute-start | bytes 377864 | tf_op jit(solution)/shard_map/ppermute | solution.py:565
  21.5 8.4 %collective-permute-start.6 = (bf16[2,24,1312]{2,1,0:T(8,128)(2,1)S(1)}, bf16[2,24,1312]{2,1,0:T(8,128)(2,1)S(1)}, u32[]{:S(2)}, u32[]{:S(2)}) collective-permute-start(bf16[2,24,1312]{2,1,0:T(8,128)(2,1)S(1)} %get-tuple-element.38), channel_id=1, source_target_pairs={{0,14},{1,15},{2,12},{3,13},{4,10},{5,11},{6,8},{7,9},{8,6},{9,7},... | collective-permute-start | bytes 377864 | tf_op jit(solution)/shard_map/ppermute | solution.py:565
  24.1 15.7 %copy-start = (bf16[2,384,1152]{2,1,0:T(8,128)(2,1)S(1)}, bf16[2,384,1152]{2,1,0:T(8,128)(2,1)}, u32[]{:S(2)}) copy-start(bf16[2,384,1152]{2,1,0:T(8,128)(2,1)} %refs_5_.1) | copy-start | bytes 5308420
  24.1 15.7 %copy-start.6 = (bf16[2,384,384]{2,1,0:T(8,128)(2,1)S(1)}, bf16[2,384,384]{2,1,0:T(8,128)(2,1)}, u32[]{:S(2)}) copy-start(bf16[2,384,384]{2,1,0:T(8,128)(2,1)} %refs_9_.1) | copy-start | bytes 1769476
  24.1 15.7 %copy-start.22 = (f32[2,384]{1,0:T(2,128)S(1)}, f32[2,384]{1,0:T(2,128)}, u32[]{:S(2)}) copy-start(f32[2,384]{1,0:T(2,128)} %refs_3_.4) | copy-start | bytes 9220
  24.1 15.7 %copy-start.23 = (f32[2,384]{1,0:T(2,128)S(1)}, f32[2,384]{1,0:T(2,128)}, u32[]{:S(2)}) copy-start(f32[2,384]{1,0:T(2,128)} %refs_4_.1) | copy-start | bytes 9220
  29.9 0.9 copy-start.11
  29.9 1.7 %copy-start.13 = (bf16[2,24,1312]{2,1,0:T(8,128)(2,1)}, bf16[2,24,1312]{2,1,0:T(8,128)(2,1)S(1)}, u32[]{:S(2)}) copy-start(bf16[2,24,1312]{2,1,0:T(8,128)(2,1)S(1)} %collective-permute-done.5.refs_6_.refs_8_) | copy-start | bytes 377860
  29.9 1.6 %copy-start.15 = (bf16[2,24,1312]{2,1,0:T(8,128)(2,1)}, bf16[2,24,1312]{2,1,0:T(8,128)(2,1)S(1)}, u32[]{:S(2)}) copy-start(bf16[2,24,1312]{2,1,0:T(8,128)(2,1)S(1)} %collective-permute-done.6.refs_7_.refs_10_) | copy-start | bytes 377860
  31.5 8.3 %collective-permute-start.7 = (bf16[8,24,1312]{2,1,0:T(8,128)(2,1)}, bf16[8,24,1312]{2,1,0:T(8,128)(2,1)S(1)}, u32[]{:S(2)}, u32[]{:S(2)}) collective-permute-start(bf16[8,24,1312]{2,1,0:T(8,128)(2,1)} %shard_map.132), channel_id=1, source_target_pairs={{0,1},{1,0},{2,3},{3,2},{4,5},{5,4},{6,7},{7,6},{8,9},{9,8},{10,11... | collective-permute-start | bytes 1511432 | tf_op jit(solution)/shard_map/ppermute | solution.py:565
  31.5 47.3 %all-to-all-start = ((bf16[16,48,256]{2,1,0:T(8,128)(2,1)}), bf16[16,48,256]{2,1,0:T(8,128)(2,1)}, u32[]{:S(2)}, u32[]{:S(2)}) async-start(bf16[16,48,256]{2,1,0:T(8,128)(2,1)} %bitcast.5), calls=%async_computation | async-start | bytes 786432 | tf_op jit(solution)/shard_map/all_to_all | solution.py:547
  39.8 1.7 %copy-start.1 = (bf16[2,384,1536]{2,1,0:T(8,128)(2,1)S(1)}, bf16[2,384,1536]{2,1,0:T(8,128)(2,1)}, u32[]{:S(2)}) copy-start(bf16[2,384,1536]{2,1,0:T(8,128)(2,1)} %refs_10_.1) | copy-start | bytes 7077892
  41.5 1.7 %copy-start.3 = (bf16[2,1536,384]{2,1,0:T(8,128)(2,1)S(1)}, bf16[2,1536,384]{2,1,0:T(8,128)(2,1)}, u32[]{:S(2)}) copy-start(bf16[2,1536,384]{2,1,0:T(8,128)(2,1)} %refs_11_.1) | copy-start | bytes 7077892
  43.2 1.9 %copy-start.5 = (bf16[48,256,128]{2,1,0:T(8,128)(2,1)S(1)}, bf16[48,256,128]{2,1,0:T(8,128)(2,1)}, u32[]{:S(2)}) copy-start(bf16[48,256,128]{2,1,0:T(8,128)(2,1)} %copy-done.4) | copy-start | bytes 9437188
  45.1 1.4 %copy-start.8 = (bf16[2048,384]{1,0:T(8,128)(2,1)S(1)}, bf16[2048,384]{1,0:T(8,128)(2,1)}, u32[]{:S(2)}) copy-start(bf16[2048,384]{1,0:T(8,128)(2,1)} %copy-done.7) | copy-start | bytes 4718596
  46.5 1.0 copy-start.10
  47.4 0.9 copy-start.12
  48.3 0.9 copy-start.14
  49.2 0.9 copy-start.16
  50.2 0.9 copy-start.21
  51.1 19.2 %copy-start.18 = (bf16[768,192]{1,0:T(8,128)(2,1)S(1)}, bf16[768,192]{1,0:T(8,128)(2,1)}, u32[]{:S(2)}) copy-start(bf16[768,192]{1,0:T(8,128)(2,1)} %copy-done.17) | copy-start | bytes 884740
  59.5 10.8 %copy-start.2 = (bf16[2,384,1536]{2,1,0:T(8,128)(2,1)S(1)}, bf16[2,384,1536]{2,1,0:T(8,128)(2,1)}, u32[]{:S(2)}) copy-start(bf16[2,384,1536]{2,1,0:T(8,128)(2,1)} %refs_10_.1) | copy-start | bytes 7077892
  59.5 6.3 %collective-permute-start.9 = (bf16[96,384]{1,0:T(8,128)(2,1)S(1)}, bf16[96,384]{1,0:T(8,128)(2,1)S(1)}, u32[]{:S(2)}, u32[]{:S(2)}) collective-permute-start(bf16[96,384]{1,0:T(8,128)(2,1)S(1)} %get-tuple-element.43.refs_0_.refs_1_), channel_id=1, source_target_pairs={{0,15},{1,0},{2,1},{3,2},{4,3},{5,4},{6,5},{7,6},{8,7},{9,8},{10,9... | collective-permute-start | bytes 221192 | tf_op jit(solution)/shard_map/ppermute | solution.py:571
  63.9 6.5 %collective-permute-start.8 = (bf16[96,384]{1,0:T(8,128)(2,1)S(1)}, bf16[96,384]{1,0:T(8,128)(2,1)S(1)}, u32[]{:S(2)}, u32[]{:S(2)}) collective-permute-start(bf16[96,384]{1,0:T(8,128)(2,1)S(1)} %get-tuple-element.44.refs_1_.refs_2_), channel_id=1, source_target_pairs={{0,1},{1,2},{2,3},{3,4},{4,5},{5,6},{6,7},{7,8},{8,9},{9,10},{10,1... | collective-permute-start | bytes 221192 | tf_op jit(solution)/shard_map/ppermute | solution.py:571
  70.3 8.4 %copy-start.31 = (s32[1,384]{1,0:T(1,128)S(1)}, s32[1,384]{1,0:T(1,128)}, u32[]{:S(2)}) copy-start(s32[1,384]{1,0:T(1,128)} %refs_3_.5) | copy-start | bytes 4612
  75.2 7.5 %collective-permute-start.14 = (bf16[2,48,384]{2,1,0:T(8,128)(2,1)S(1)}, bf16[2,48,384]{2,1,0:T(8,128)(2,1)S(1)}, u32[]{:S(2)}, u32[]{:S(2)}) collective-permute-start(bf16[2,48,384]{2,1,0:T(8,128)(2,1)S(1)} %get-tuple-element.51), channel_id=1, source_target_pairs={{0,2},{1,3},{2,0},{3,1},{4,6},{5,7},{6,4},{7,5},{8,10},{9,11},{10,... | collective-permute-start | bytes 221192 | tf_op jit(solution)/shard_map/ppermute | solution.py:565
  75.3 7.5 %collective-permute-start.15 = (bf16[2,48,384]{2,1,0:T(8,128)(2,1)S(1)}, bf16[2,48,384]{2,1,0:T(8,128)(2,1)S(1)}, u32[]{:S(2)}, u32[]{:S(2)}) collective-permute-start(bf16[2,48,384]{2,1,0:T(8,128)(2,1)S(1)} %get-tuple-element.52), channel_id=1, source_target_pairs={{0,4},{1,5},{2,6},{3,7},{4,0},{5,1},{6,2},{7,3},{8,12},{9,13},{10,... | collective-permute-start | bytes 221192 | tf_op jit(solution)/shard_map/ppermute | solution.py:565
  75.4 7.4 %collective-permute-start.16 = (bf16[2,48,384]{2,1,0:T(8,128)(2,1)S(1)}, bf16[2,48,384]{2,1,0:T(8,128)(2,1)S(1)}, u32[]{:S(2)}, u32[]{:S(2)}) collective-permute-start(bf16[2,48,384]{2,1,0:T(8,128)(2,1)S(1)} %get-tuple-element.53), channel_id=1, source_target_pairs={{0,6},{1,7},{2,4},{3,5},{4,2},{5,3},{6,0},{7,1},{8,14},{9,15},{10,... | collective-permute-start | bytes 221192 | tf_op jit(solution)/shard_map/ppermute | solution.py:565
  78.8 1.2 %copy-start.25 = (bf16[384,1312]{0,1:T(8,128)(2,1)S(1)}, bf16[384,1312]{0,1:T(8,128)(2,1)}, u32[]{:S(2)}) copy-start(bf16[384,1312]{0,1:T(8,128)(2,1)} %param.25) | copy-start | bytes 3022852
  82.8 7.8 %collective-permute-start.17 = (bf16[4,48,384]{2,1,0:T(8,128)(2,1)S(1)}, bf16[4,48,384]{2,1,0:T(8,128)(2,1)S(1)}, u32[]{:S(2)}, u32[]{:S(2)}) collective-permute-start(bf16[4,48,384]{2,1,0:T(8,128)(2,1)S(1)} %shard_map.137), channel_id=1, source_target_pairs={{0,1},{1,0},{2,3},{3,2},{4,5},{5,4},{6,7},{7,6},{8,9},{9,8},{10,11... | collective-permute-start | bytes 442376 | tf_op jit(solution)/shard_map/ppermute | solution.py:565
  82.9 11.4 %collective-permute-start.10 = (bf16[2,48,384]{2,1,0:T(8,128)(2,1)S(1)}, bf16[2,48,384]{2,1,0:T(8,128)(2,1)S(1)}, u32[]{:S(2)}, u32[]{:S(2)}) collective-permute-start(bf16[2,48,384]{2,1,0:T(8,128)(2,1)S(1)} %get-tuple-element.46), channel_id=1, source_target_pairs={{0,8},{1,9},{2,10},{3,11},{4,12},{5,13},{6,14},{7,15},{8,0},{9,1},... | collective-permute-start | bytes 221192 | tf_op jit(solution)/shard_map/ppermute | solution.py:565
  83.0 13.2 %collective-permute-start.11 = (bf16[2,48,384]{2,1,0:T(8,128)(2,1)S(1)}, bf16[2,48,384]{2,1,0:T(8,128)(2,1)S(1)}, u32[]{:S(2)}, u32[]{:S(2)}) collective-permute-start(bf16[2,48,384]{2,1,0:T(8,128)(2,1)S(1)} %get-tuple-element.47), channel_id=1, source_target_pairs={{0,10},{1,11},{2,8},{3,9},{4,14},{5,15},{6,12},{7,13},{8,2},{9,3},... | collective-permute-start | bytes 221192 | tf_op jit(solution)/shard_map/ppermute | solution.py:565
  85.4 10.8 %collective-permute-start.12 = (bf16[2,48,384]{2,1,0:T(8,128)(2,1)S(1)}, bf16[2,48,384]{2,1,0:T(8,128)(2,1)S(1)}, u32[]{:S(2)}, u32[]{:S(2)}) collective-permute-start(bf16[2,48,384]{2,1,0:T(8,128)(2,1)S(1)} %get-tuple-element.48), channel_id=1, source_target_pairs={{0,12},{1,13},{2,14},{3,15},{4,8},{5,9},{6,10},{7,11},{8,4},{9,5},... | collective-permute-start | bytes 221192 | tf_op jit(solution)/shard_map/ppermute | solution.py:565
  86.6 9.6 %collective-permute-start.13 = (bf16[2,48,384]{2,1,0:T(8,128)(2,1)S(1)}, bf16[2,48,384]{2,1,0:T(8,128)(2,1)S(1)}, u32[]{:S(2)}, u32[]{:S(2)}) collective-permute-start(bf16[2,48,384]{2,1,0:T(8,128)(2,1)S(1)} %get-tuple-element.49), channel_id=1, source_target_pairs={{0,14},{1,15},{2,12},{3,13},{4,10},{5,11},{6,8},{7,9},{8,6},{9,7},... | collective-permute-start | bytes 221192 | tf_op jit(solution)/shard_map/ppermute | solution.py:565
  96.3 1.4 %collective-permute-start.18 = (bf16[4,48,384]{2,1,0:T(8,128)(2,1)S(1)}, bf16[4,48,384]{2,1,0:T(8,128)(2,1)S(1)}, u32[]{:S(2)}, u32[]{:S(2)}) collective-permute-start(bf16[4,48,384]{2,1,0:T(8,128)(2,1)S(1)} %shard_map.139), channel_id=1, source_target_pairs={{0,1},{1,0},{2,3},{3,2},{4,5},{5,4},{6,7},{7,6},{8,9},{9,8},{10,11... | collective-permute-start | bytes 442376 | tf_op jit(solution)/shard_map/ppermute | solution.py:565
  (4 other events, 2.8 us)

commit v3 on v2

--- a/solution.py
+++ b/solution.py
@@ -11,6 +11,7 @@
 
 WIN = 8
 ROWS = 24
+K = 4
 LANES = 128
 GROUP = 8
 
@@ -56,10 +57,10 @@
         return self.ref
 
 
-def call(kernel, ins, outs, scratch=(), table=None, flops=0, after=()):
+def call(kernel, ins, outs, scratch=(), table=(), flops=0, after=()):
     def run(*refs):
         refs = list(refs)
-        lead = [refs.pop(0)] if table is not None else []
+        lead = [refs.pop(0) for _ in table]
         loads = []
         for one in ins:
             ref = refs.pop(0)
@@ -69,7 +70,7 @@
         kernel(*lead, loads, held, refs)
 
     vmem = pl.BlockSpec(memory_space=pltpu.VMEM)
-    in_specs = [] if table is None else [pl.BlockSpec(memory_space=pltpu.SMEM)]
+    in_specs = [pl.BlockSpec(memory_space=pltpu.SMEM)] * len(table)
     moved = sum(int(np.prod(s.array.shape)) * s.array.dtype.itemsize for s in ins)
     got = pl.pallas_call(
         run,
@@ -79,7 +80,7 @@
         scratch_shapes=list(scratch),
         compiler_params=pltpu.CompilerParams(vmem_limit_bytes=VMEM_LIMIT),
         cost_estimate=pl.CostEstimate(flops=int(flops), bytes_accessed=moved, transcendentals=0),
-    )(*([] if table is None else [table]), *[one.array for one in ins], *after)
+    )(*table, *[one.array for one in ins], *after)
     return got if len(outs) > 1 else got[0]
 
 
@@ -144,13 +145,15 @@
     return lo, hi, move.astype(F32).astype(BF16)
 
 
-def weights_by_slot(recv, weight, slots, level):
+def weights_by_slot(recv, weight, slots, level, share=0, width=None):
     pixsq = weight.shape[1] // recv.shape[0]
+    width = width or pixsq
     r = iota((slots, recv.shape[1]), 0)
     total = None
     for k in (2 * level, 2 * level + 1):
         hit = (recv[k : k + 1, :] == r).astype(F32).astype(BF16)
-        term = mm(hit, weight[:, k * pixsq : (k + 1) * pixsq])
+        first = k * pixsq if width == pixsq else pl.multiple_of(k * pixsq + share * width, LANES)
+        term = mm(hit, weight[:, pl.ds(first, width)])
         total = term if total is None else total + term
     return total
 
@@ -189,12 +192,13 @@
             out_ref[b, :, m * LANES : (m + 1) * LANES] = jnp.where(first, both[0], both[1])
 
 
-def weights_kernel(loads, outs, scratch):
+def weights_kernel(group_ref, loads, outs, scratch):
     recv, weight = (one() for one in loads)
     slots = 2 * recv.shape[1]
-    pixsq = weight.shape[1] // recv.shape[0]
-    totals = [weights_by_slot(recv, weight, slots, v).reshape(slots // GROUP, GROUP, pixsq) for v in range(2)]
-    outs[0][...] = jnp.concatenate(totals, axis=1).reshape(2 * slots, pixsq).astype(BF16)
+    width = outs[0].shape[1]
+    totals = [weights_by_slot(recv, weight, slots, v, group_ref[0], width) for v in range(2)]
+    totals = [t.reshape(slots // GROUP, GROUP, width) for t in totals]
+    outs[0][...] = jnp.concatenate(totals, axis=1).reshape(2 * slots, width).astype(BF16)
 
 
 def split_slots(recv, cap, me):
@@ -226,7 +230,7 @@
 
 def tables_kernel(cap, direct, me_ref, loads, outs, scratch):
     recv, embed, rel = (one() for one in loads)
-    *scatter_refs, embed_out, bias_ref, select_ref = outs
+    *scatter_refs, embed_out, bias_ref, select_ref, digits_ref = outs
     pd = recv.shape[1]
     slots = 2 * pd
     pix = embed_out.shape[0] // LANES
@@ -234,8 +238,11 @@
     turn = patch_turn(pd)
     parts = [v.astype(F32).astype(BF16) for v in split_slots(recv, cap, me_ref[0])]
     cols = (mm_nt(turn, parts[0]) * cap + mm_nt(turn, parts[1])).astype(jnp.int32)
-    rows = (mm_nt(parts[0], turn) * cap + mm_nt(parts[1], turn)).astype(jnp.int32)
-    select_ref[...] = chosen((2 * slots, pd), 0, lambda k: rows[k : k + 1, :])
+    digits = [mm_nt(v, turn) for v in parts]
+    rows = (digits[0] * cap + digits[1]).astype(jnp.int32)
+    select_ref[...] = chosen(select_ref.shape, 0, lambda k: rows[k : k + 1, :])
+    digits_ref[...] = jnp.zeros_like(digits_ref)
+    digits_ref[:, :pd] = jnp.concatenate(digits, axis=0).astype(BF16)
     for stage, ref in enumerate(scatter_refs):
         ref[...] = chosen(ref.shape, 1, lambda k: cols[:, k : k + 1],
                           functools.partial(stage_chunk, stage, direct), 2 * slots // (4 * NEAR))
@@ -255,9 +262,9 @@
         store_spread(outs[0], spread(total.astype(BF16), True, pix), level * pix * GROUP, 0, pix)
 
 
-def prep_back_kernel(size, me_ref, loads, outs, scratch):
-    weight, unembed, send = loads
-    weight_ref, unembed = weight(), unembed()
+def prep_back_kernel(size, me_ref, group_ref, loads, outs, scratch):
+    *weight, unembed, send = loads
+    unembed = unembed()
     mix_ref, unembed_out, owner_ref = outs
     owner = jnp.broadcast_to(send()[...], (GROUP, send.ref.shape[1]))
     if size is not None:
@@ -271,11 +278,18 @@
             swapped = jnp.where((chunk >> bit) & 1 == 0, up, down)
             owner = jnp.where((me_ref[0] >> bit) & 1 == 1, swapped, owner)
     owner_ref[...] = owner
-    rows, pixsq = weight_ref.shape
+    if len(weight) == 2:
+        mine, other = (one()[...].astype(F32) for one in weight)
+        first = group_ref[0] == 0
+        both = [jnp.where(first, mine, other), jnp.where(first, other, mine)]
+        weights = jnp.concatenate(both, axis=1)
+    else:
+        weights = weight[0]()[...].astype(F32)
+    rows, pixsq = weights.shape
     pix = int(round(pixsq**0.5))
     ch = unembed.shape[0] // pix
     groups = rows // (2 * GROUP)
-    w3 = weight_ref[...].astype(F32).reshape(groups, 2, GROUP, pixsq)
+    w3 = weights.reshape(groups, 2, GROUP, pixsq)
     for level in range(2):
         w_l = w3[:, level].reshape(groups * GROUP, pixsq).astype(BF16)
         store_spread(mix_ref, spread(w_l, False, pix), 0, level * pix * GROUP, pix)
@@ -376,6 +390,10 @@
 
 def early_kernel(pix, direct, loads, outs, scratch):
     *chunks, mix, scatter, embed = loads
+    if direct:
+        for i, one in enumerate(chunks):
+            outs[1][i] = one()[1]
+        chunks = [Loaded(one.ref.at[0]) for one in chunks]
     outs[0][...] = regrid_part(0, direct, joined(chunks), *scratch, mix, scatter, embed, pix)
 
 
@@ -424,8 +442,25 @@
     outs[0][...] = mm(normed, qkv()[...]).astype(BF16)
 
 
+def put_chunks(sent, chips):
+    rows = sent.shape[0] // (2 * len(chips))
+    for x in range(2 * len(chips)):
+        chips[x // 2][x % 2] = sent[x * rows : (x + 1) * rows]
+
+
+def pass_on_kernel(cap, loads, outs, scratch):
+    state = loads[0]()
+    kk = K
+    pd = state.shape[0] - 2 * kk
+    digits = state[pd:, :pd].astype(F32)
+    slot = (digits[:kk] * cap + digits[kk:]).astype(jnp.int32)
+    rows = 2 * cap
+    select = chosen((2 * NEAR * rows, pd), 0, lambda k: slot[k : k + 1, :], lambda c: c + 2 * NEAR, rows)
+    put_chunks(mm(select, state[:pd, :]).astype(BF16), outs)
+
+
 def second_kernel(layer, loads, outs, scratch):
-    packed, low, high, gain1, gain2, qkv, bias, left, right, proj, up, down, select = loads
+    packed, low, high, gain1, gain2, qkv, bias, left, right, proj, up, down, select, digits = loads
     half, d = low.ref.shape
     heads = bias.ref.shape[1] // (WIN * WIN)
     shift = half * (WIN // 2) // ROWS
@@ -476,9 +511,10 @@
     if len(outs) == 1:
         outs[0][...] = sent
         return
-    rows = sent.shape[0] // (2 * len(outs))
-    for x in range(2 * len(outs)):
-        outs[x // 2][x % 2] = sent[x * rows : (x + 1) * rows]
+    *chips, mirror = outs
+    put_chunks(sent, chips)
+    mirror[: 2 * half, :] = state
+    mirror[2 * half :, :] = digits()[...]
 
 
 def back_part(size, first, me_ref, chunks, mix, unembed, p_ref, slot_ref):
@@ -601,7 +637,7 @@
         turns = [*range(NEAR, chips), *range(NEAR - 1, 0, -1)]
 
         outgoing = call(pick_direct_kernel, [In(send_table), In(bands)],
-                        [sds((2, cap, width), BF16)] * chips, [vm((count, cap, width), BF16)], my, flops=1e10)
+                        [sds((2, cap, width), BF16)] * chips, [vm((count, cap, width), BF16)], [my], flops=1e+09)
         came = [outgoing[0]] + [None] * (chips - 1)
         for s in turns:
             came[s] = flip(outgoing[s], "tile", 2 * s)
@@ -611,17 +647,21 @@
 
     heads = rel_bias.shape[1]
     span = WIN * WIN
-    wsend = call(weights_kernel, [In(recv_table), In(regrid_weight)], [sds((2 * slots, pixsq), BF16)],
-                 flops=1e10, after=[outgoing[0] if direct else outgoing])
+    shared = lax.axis_size("groups") == 2 and pixsq % (2 * LANES) == 0
+    group = lax.axis_index("groups").astype(jnp.int32).reshape(1)
+    wsend = call(weights_kernel, [In(recv_table), In(regrid_weight)],
+                 [sds((2 * slots, pixsq // 2 if shared else pixsq), BF16)], (), [group],
+                 flops=1e+09, after=[outgoing[0] if direct else outgoing])
     wback = swap_pairs(wsend, "tile")
-    scatter_a, scatter_b, embed_pad, bias, select = call(
+    scatter_a, scatter_b, embed_pad, bias, select, digits = call(
         functools.partial(tables_kernel, cap, direct),
         [In(recv_table), In(embed_weight), In(rel_bias.transpose(1, 0, 2))],
         [sds((pd, slots // 2), BF16), sds((pd, 3 * slots // 2), BF16), sds((wide, d), BF16),
-         sds((rel_bias.shape[0], span, heads * span), F32), sds((2 * slots, pd), BF16)],
-        [vm((heads, 2 * LANES), F32)], my, flops=2e9, after=[wsend])
+         sds((rel_bias.shape[0], span, heads * span), F32), sds((slots if direct else 2 * slots, pd), BF16),
+         sds((2 * kk, d), BF16)],
+        [vm((heads, 2 * LANES), F32)], [my], flops=2e+08, after=[wsend])
     mix = call(functools.partial(mix_kernel, cap), [In(recv_table), In(regrid_weight)],
-               [sds((slots // GROUP, 2 * pix * GROUP, pix * GROUP), BF16)], (), my, flops=2e9, after=[embed_pad])
+               [sds((slots // GROUP, 2 * pix * GROUP, pix * GROUP), BF16)], (), [my], flops=2e+08, after=[embed_pad])
 
     def relay(arrays, after=()):
         shape = (len(arrays), *arrays[0].shape[1:])
@@ -631,14 +671,17 @@
         return [vm((rows, wide), F32), vm((2 * rows, wide), BF16)]
 
     if direct:
-        near = [at(x, 0) for x in came[:NEAR]]
+        near = [In(x) for x in came[:NEAR]]
     else:
         near, far = [at(incoming, slice(0, slots // 4))], [at(incoming, slice(slots // 4, slots))]
     total = call(functools.partial(early_kernel, pix, direct),
-                 [*near, In(mix), In(scatter_a), In(embed_pad)], [sds((pd, d), F32)],
-                 regrid_scratch(slots // 4), flops=2e9)
+                 [*near, In(mix), In(scatter_a), In(embed_pad)],
+                 [sds((pd, d), F32)] + [sds((NEAR, cap, width), BF16)] * direct,
+                 regrid_scratch(slots // 4), flops=2e+08)
     if direct:
-        for_partner = relay(came, [total])
+        total, near_pass = total
+        for_partner = call(relay_kernel, [*[at(near_pass, i) for i in range(NEAR)], *[at(x, 1) for x in came[NEAR:]]],
+                           [sds((chips, cap, width), BF16)])
         passed = flip(for_partner, "tile", 1)
         far = [at(passed, i) for i in range(NEAR)]
         far += [y for i in range(NEAR, chips) for y in (at(came[i], 0), at(passed, i))]
@@ -652,29 +695,35 @@
     low, high = call(
         functools.partial(first_kernel, pix, direct, 0),
         [*far, In(mix), In(scatter_b), In(embed_pad), In(total), *ins_a, *ins_b],
-        [sds((half, d), BF16)] * 2, regrid_scratch(3 * slots // 4), flops=4e9)
+        [sds((half, d), BF16)] * 2, regrid_scratch(3 * slots // 4), flops=4e+08)
     right = from_behind(low, "tile", -1)
     left = from_behind(high, "tile", 1)
+    wbacks = [wback]
+    if shared:
+        wbacks.append(flip(wback, "groups", 1))
     ins_a, ins_b = layer(1)
     packed = call(functools.partial(own_kernel, 1), [In(low), In(high), In(norm1_gain), at(qkv_weight, 1)],
-                  [sds((pd, 3 * d), BF16)], flops=2e8)
+                  [sds((pd, 3 * d), BF16)], flops=2e+07)
     rows = 2 * cap
     sent = call(
         functools.partial(second_kernel, 1),
-        [In(packed), In(low), In(high), *ins_a, In(left), In(right), *ins_b, In(select)],
-        [sds((2, rows, d), BF16)] * chips if direct else [sds((2 * slots, d), BF16)], flops=2e9)
+        [In(packed), In(low), In(high), *ins_a, In(left), In(right), *ins_b, In(select), In(digits)],
+        [sds((2, rows, d), BF16)] * NEAR + [sds((pd + 2 * kk, d), BF16)] if direct else [sds((2 * slots, d), BF16)], flops=2e+08)
     one_sent = sent[0] if direct else sent
     size = cap // GROUP if direct else None
     mix_back, unembed_pad, owner = call(
-        functools.partial(prep_back_kernel, size), [In(wback), In(unembed_weight.T), In(send_table)],
+        functools.partial(prep_back_kernel, size), [*[In(w) for w in wbacks], In(unembed_weight.T), In(send_table)],
         [sds((slots // GROUP, pix * GROUP, 2 * pix * GROUP), BF16), sds((wide, d), BF16),
-         sds((GROUP, slots), jnp.int32)], (), my, flops=2e9, after=[one_sent])
+         sds((GROUP, slots), jnp.int32)], (), [my, group], flops=2e+08, after=[one_sent])
 
     back_scratch = [vm((2 * per, wide), F32), vm((per, wide), F32)]
     if direct:
-        got = [sent[0]] + [None] * (chips - 1)
-        for s in turns:
-            got[s] = flip(sent[s], "tile", 2 * s)
+        *sent, mirror = sent
+        mirror = flip(mirror, "tile", 2 * NEAR)
+        got = [sent[0]] + [flip(sent[s], "tile", 2 * s) for s in range(1, NEAR)]
+        passed = call(functools.partial(pass_on_kernel, cap), [In(mirror)],
+                      [sds((2, rows, d), BF16)] * NEAR, flops=3e+07)
+        got += [passed[0]] + [flip(passed[s], "tile", 2 * s) for s in range(1, NEAR)]
         near_all = relay(got[:NEAR], [mix_back])
         near_pass = flip(near_all, "tile", 1)
         near = [y for i, x in enumerate(got[:NEAR]) for y in (at(x, 0), at(near_pass, i))]
@@ -682,12 +731,12 @@
         got = swap_pairs(sent, "tile").reshape(STAGES, 2 * per, d)
         near, far = [at(got, 0)], [at(got, 1)]
     prior = call(functools.partial(back_kernel, size, 0), [*near, In(unembed_pad), In(mix_back)],
-                 [sds((per, wide), BF16)], back_scratch, my, flops=2e9)
+                 [sds((per, wide), BF16)], back_scratch, [my], flops=2e+08)
     if direct:
         far_pass = flip(relay(got[NEAR:], [prior]), "tile", 1)
         far = [y for i, x in enumerate(got[NEAR:]) for y in (at(x, 0), at(far_pass, i))]
     return call(functools.partial(last_kernel, size, groups), [*far, In(unembed_pad), In(mix_back), In(prior), In(owner)],
-                [sds((pd, width), F32)], back_scratch, my, flops=3e9)
+                [sds((pd, width), F32)], back_scratch, [my], flops=3e+08)
 
 
 def solution(mesh):

time: 103 us -> 94.5 us (0.917); the launches traced: 102 us -> 94.3 us
  blocking collectives: 0 us -> 17 us
  local copies, waits for them, and re-layouts: 17.2 us -> 1.84 us
  starting transfers between devices: 36.6 us -> 26.9 us
  waiting for transfers between devices: 16.2 us -> 18.3 us
  Pallas kernels: 31.4 us -> 29.9 us
    all_to_all x0 -> x1, blocking collectives: none -> 17 us  [swap(): return lax.all_to_all(value, axis, split_axis=0, concat_axis=0, tiled=True)]
    unnamed x64 -> x28, local copies, waits for them, and re-layouts: 17.2 us -> 1.84 us
    all_to_all x1 -> x0, starting transfers between devices: 8.25 us -> none  [swap(): return lax.all_to_all(value, axis, split_axis=0, concat_axis=0, tiled=True)]
    ppermute x17 -> x18, waiting for transfers between devices: 10.3 us -> 16.9 us  [flip(): lax.ppermute(value, axis, [(source, source ^ bits) for source in range(co...]
    ppermute x2, waiting for transfers between devices: 5.87 us -> 1.43 us  [from_behind(): return lax.ppermute(value, axis, pairs)]
    ppermute x17 -> x18, starting transfers between devices: 24 us -> 22.4 us  [flip(): lax.ppermute(value, axis, [(source, source ^ bits) for source in range(co...]
    pallas_call x14 -> x15, Pallas kernels: 31.4 us -> 29.9 us  [call(): pl.pallas_call(run, out_shape=list(outs), in_specs=in_specs + [vmem] * le...]
  transfers between devices with their start and end apart: 20 -> 20, of which waited for: 6 -> 7; matrix products, arithmetic and copies ran while one was open for 0% -> 0% of each run, Pallas kernels for 25% -> 27%
where the time goes in v3:
time: 94.5 us; the launch traced here: 94.3 us
  Pallas kernels  29.9 us (32%)
  starting transfers between devices  26.9 us (28%)
  waiting for transfers between devices  18.3 us (19%)
  blocking collectives  17 us (18%)
  local copies, waits for them, and re-layouts  1.84 us (2%)
    pallas_call x15, Pallas kernels, call(): pl.pallas_call(run, out_shape=list(outs), in_specs=in_specs + [vmem] * le...  29.9 us
    ppermute x18, starting transfers between devices, flip(): lax.ppermute(value, axis, [(source, source ^ bits) for source in range(co...  22.4 us
    all_to_all x1, blocking collectives, swap(): return lax.all_to_all(value, axis, split_axis=0, concat_axis=0, tiled=True)  17 us
    ppermute x18, waiting for transfers between devices, flip(): lax.ppermute(value, axis, [(source, source ^ bits) for source in range(co...  16.9 us
    ppermute x2, starting transfers between devices, from_behind(): return lax.ppermute(value, axis, pairs)  4.49 us
  transfers between devices with their start and end apart: 20, of which 7 were waited for; matrix products, arithmetic and copies ran while one was open for 0% of the time, Pallas kernels for 27%

profile of v3, /device:TPU:0, one launch (start us, length us, event | category | flops | bytes accessed | tf_op | source)
XLA Modules:
  0.0 94.3 jit_solution(13746186625432643078)
XLA Ops:
  0.0 0.7 copy-done.11
  0.7 1.0 %copy-done.13 = bf16[192,1312]{1,0:T(8,128)(2,1)S(1)} copy-done((bf16[192,1312]{1,0:T(8,128)(2,1)S(1)}, bf16[192,1312]{1,0:T(8,128)(2,1)}, u32[]{:S(2)}) %copy-start.13) | copy-done | bytes 503832
  1.8 0.6 shard_map.127
  2.4 0.0 copy-start.4
  2.4 0.0 copy-start.8
  2.4 3.1 %collective-permute-start = (bf16[2,24,1312]{2,1,0:T(8,128)(2,1)S(1)}, bf16[2,24,1312]{2,1,0:T(8,128)(2,1)S(1)}, u32[]{:S(2)}, u32[]{:S(2)}) collective-permute-start(bf16[2,24,1312]{2,1,0:T(8,128)(2,1)S(1)} %get-tuple-element.36), channel_id=1, source_target_pairs={{0,2},{1,3},{2,0},{3,1},{4,6},{5,7},{6,4},{7,5},{8,10},{9,11},{10,... | collective-permute-start | bytes 377864 | tf_op jit(solution)/shard_map/ppermute | solution.py:601
  5.5 1.6 %collective-permute-start.1 = (bf16[2,24,1312]{2,1,0:T(8,128)(2,1)S(1)}, bf16[2,24,1312]{2,1,0:T(8,128)(2,1)S(1)}, u32[]{:S(2)}, u32[]{:S(2)}) collective-permute-start(bf16[2,24,1312]{2,1,0:T(8,128)(2,1)S(1)} %get-tuple-element.37), channel_id=1, source_target_pairs={{0,4},{1,5},{2,6},{3,7},{4,0},{5,1},{6,2},{7,3},{8,12},{9,13},{10,... | collective-permute-start | bytes 377864 | tf_op jit(solution)/shard_map/ppermute | solution.py:601
  7.0 3.0 %collective-permute-start.3 = (bf16[2,24,1312]{2,1,0:T(8,128)(2,1)S(1)}, bf16[2,24,1312]{2,1,0:T(8,128)(2,1)S(1)}, u32[]{:S(2)}, u32[]{:S(2)}) collective-permute-start(bf16[2,24,1312]{2,1,0:T(8,128)(2,1)S(1)} %get-tuple-element.42), channel_id=1, source_target_pairs={{0,8},{1,9},{2,10},{3,11},{4,12},{5,13},{6,14},{7,15},{8,0},{9,1},... | collective-permute-start | bytes 377864 | tf_op jit(solution)/shard_map/ppermute | solution.py:601
  10.0 1.3 %collective-permute-start.4 = (bf16[2,24,1312]{2,1,0:T(8,128)(2,1)S(1)}, bf16[2,24,1312]{2,1,0:T(8,128)(2,1)S(1)}, u32[]{:S(2)}, u32[]{:S(2)}) collective-permute-start(bf16[2,24,1312]{2,1,0:T(8,128)(2,1)S(1)} %get-tuple-element.43), channel_id=1, source_target_pairs={{0,10},{1,11},{2,8},{3,9},{4,14},{5,15},{6,12},{7,13},{8,2},{9,3},... | collective-permute-start | bytes 377864 | tf_op jit(solution)/shard_map/ppermute | solution.py:601
  11.3 3.6 %collective-permute-start.5 = (bf16[2,24,1312]{2,1,0:T(8,128)(2,1)S(1)}, bf16[2,24,1312]{2,1,0:T(8,128)(2,1)S(1)}, u32[]{:S(2)}, u32[]{:S(2)}) collective-permute-start(bf16[2,24,1312]{2,1,0:T(8,128)(2,1)S(1)} %get-tuple-element.44), channel_id=1, source_target_pairs={{0,12},{1,13},{2,14},{3,15},{4,8},{5,9},{6,10},{7,11},{8,4},{9,5},... | collective-permute-start | bytes 377864 | tf_op jit(solution)/shard_map/ppermute | solution.py:601
  14.9 1.6 %collective-permute-done.1.refs_2_ = bf16[2,24,1312]{2,1,0:T(8,128)(2,1)S(1)} collective-permute-done((bf16[2,24,1312]{2,1,0:T(8,128)(2,1)S(1)}, bf16[2,24,1312]{2,1,0:T(8,128)(2,1)S(1)}, u32[]{:S(2)}, u32[]{:S(2)}) %collective-permute-start.1) | collective-permute-done | bytes 125984 | tf_op jit(solution)/shard_map/ppermute | solution.py:601
  16.5 0.7 collective-permute-start.6
  17.3 0.4 shard_map.128.refs_4_
  17.7 2.2 %shard_map.129 = (bf16[192,192]{1,0:T(8,128)(2,1)S(1)}, bf16[192,576]{1,0:T(8,128)(2,1)S(1)}, bf16[2048,384]{1,0:T(8,128)(2,1)S(1)}, f32[2,64,768]{2,1,0:T(8,128...) custom-call(s32[1]{0:T(128)} %bitcast.refs_0_, s32[4,192]{1,0:T(4,128)S(1)} %copy-done.9, ...), custom_call_target="tpu_custom_call" | custom-call | flops 200000000 | bytes 1032288 | tf_op jit(solution)/shard_map/pallas_call | solution.py:75
  19.9 1.5 %shard_map.130.refs_4_.refs_12_ = bf16[48,256,128]{2,1,0:T(8,128)(2,1)S(1)} custom-call(s32[1]{0:T(128)} %bitcast.refs_0_, s32[4,192]{1,0:T(4,128)S(1)} %copy-done.9, bf16[192,1024]{1,0:T(8,128)(2,1)S(1)} %copy-done.6, bf16[2048,384]{1,0:T(8,128)(2,1)S(1)} %get-tuple-element.39.refs_3_.refs_6_.refs_14_), custom_call_target="tpu_custom_call" | custom-call | flops 200000000 | bytes 396288 | tf_op jit(solution)/shard_map/pallas_call | solution.py:75
  21.3 0.0 collective-permute-done.2.refs_3_
  21.3 0.0 copy-start.1
  21.3 0.0 copy-start.2
  21.4 2.6 %shard_map.131 = (f32[192,384]{1,0:T(8,128)S(1)}, bf16[4,24,1312]{2,1,0:T(8,128)(2,1)S(1)}) custom-call(bf16[2,24,1312]{2,1,0:T(8,128)(2,1)S(1)} %get-tuple-element.35.refs_3_.refs_0_, bf16[2,24,1312]{2,1,0:T(8,128)(2,1)S(1)} %collective-permute-done.refs_1_, bf16[2,24,1312]{2,1,0:T(8,128)(2,1)S(1)} %collective-permute-done.1.refs_2_, ...), custom_call_target="tpu_custom_call" | custom-call | flops 200000000 | bytes 5296128 | tf_op jit(solution)/shard_map/pallas_call | solution.py:75
  23.9 0.0 copy-start
  23.9 0.0 copy-start.3
  24.0 0.0 copy-start.7
  24.0 0.0 copy-start.10
  24.0 6.0 %collective-permute-done.4.refs_5_.refs_6_ = bf16[2,24,1312]{2,1,0:T(8,128)(2,1)S(1)} collective-permute-done((bf16[2,24,1312]{2,1,0:T(8,128)(2,1)S(1)}, bf16[2,24,1312]{2,1,0:T(8,128)(2,1)S(1)}, u32[]{:S(2)}, u32[]{:S(2)}) %collective-permute-start.4) | collective-permute-done | bytes 125984 | tf_op jit(solution)/shard_map/ppermute | solution.py:601
  30.0 0.1 collective-permute-start.7
  30.1 17.0 %all_to_all.11 = bf16[16,48,128]{2,1,0:T(8,128)(2,1)S(1)} all-to-all(bf16[16,48,128]{2,1,0:T(8,128)(2,1)S(1)} %bitcast.9), channel_id=1, replica_groups=mesh['groups'=2,'tile'=16] {'tile'}, dimensions={0} | all-to-all | bytes 393216 | tf_op jit(solution)/shard_map/all_to_all | solution.py:583
  47.1 1.5 %collective-permute-start.17 = (bf16[768,128]{1,0:T(8,128)(2,1)S(1)}, bf16[768,128]{1,0:T(8,128)(2,1)S(1)}, u32[]{:S(2)}, u32[]{:S(2)}) collective-permute-start(bf16[768,128]{1,0:T(8,128)(2,1)S(1)} %bitcast.7), channel_id=1, source_target_pairs={{0,16},{16,0},{1,17},{17,1},{2,18},{18,2},{3,19},{19,3},{4,20},{20... | collective-permute-start | bytes 589832 | tf_op jit(solution)/shard_map/ppermute | solution.py:601
  48.6 8.4 %shard_map.133 = (bf16[96,384]{1,0:T(8,128)(2,1)S(1)}, bf16[96,384]{1,0:T(8,128)(2,1)S(1)}) custom-call(bf16[8,24,1312]{2,1,0:T(8,128)(2,1)S(1)} %collective-permute-done.7.refs_0_.refs_1_.refs_2_.refs_3_.refs_5_.refs_7_.refs_9_.refs_11_, bf16[8,24,1312]{2,1,0:T(8,128)(2,1)S(1)} %collective-permute-done.7.refs_0_.refs_1_.refs_2_.refs_3_.refs_5_.refs_7_.refs_9_.refs_11_, ...), custom_call_target="tpu_custom_call" | custom-call | flops 400000000 | bytes 17246208 | tf_op jit(solution)/shard_map/pallas_call | solution.py:75
  57.1 0.1 collective-permute-start.8
  57.1 4.4 %collective-permute-start.9 = (bf16[96,384]{1,0:T(8,128)(2,1)S(1)}, bf16[96,384]{1,0:T(8,128)(2,1)S(1)}, u32[]{:S(2)}, u32[]{:S(2)}) collective-permute-start(bf16[96,384]{1,0:T(8,128)(2,1)S(1)} %get-tuple-element.49.refs_0_.refs_1_), channel_id=1, source_target_pairs={{0,15},{1,0},{2,1},{3,2},{4,3},{5,4},{6,5},{7,6},{8,7},{9,8},{10,9... | collective-permute-start | bytes 221192 | tf_op jit(solution)/shard_map/ppermute | solution.py:607
  61.6 0.6 shard_map.134.refs_0_
  62.2 1.4 %collective-permute-done.8.refs_7_ = bf16[96,384]{1,0:T(8,128)(2,1)S(1)} collective-permute-done((bf16[96,384]{1,0:T(8,128)(2,1)S(1)}, bf16[96,384]{1,0:T(8,128)(2,1)S(1)}, u32[]{:S(2)}, u32[]{:S(2)}) %collective-permute-start.8) | collective-permute-done | bytes 73760 | tf_op jit(solution)/shard_map/ppermute | solution.py:607
  63.6 4.8 %shard_map.135 = (bf16[2,48,384]{2,1,0:T(8,128)(2,1)S(1)}, bf16[2,48,384]{2,1,0:T(8,128)(2,1)S(1)}, bf16[2,48,384]{2,1,0:T(8,128)(2,1)S(1)}, bf16[2,48,384]{2,1,0:T(8,128)(2,1)S(1)}, bf16[200,384]{1,0:T(8,128)(2,1)S(1)}) custom-call(bf16[192,1152]{1,0:T(8,128)(2,1)S(1)} %shard_map.134.refs_0_, bf16[96,384]{1,0:T(8,128)(2,1)S(1)} %get-tuple-element.49.refs_0_.refs_1_, ...), custom_call_target="tpu_custom_call" | custom-call | flops 200000000 | bytes 8368128 | tf_op jit(solution)/shard_map/pallas_call | solution.py:75
  68.4 0.1 collective-permute-start.14
  68.5 0.1 collective-permute-start.15
  68.6 3.4 %collective-permute-start.16 = (bf16[2,48,384]{2,1,0:T(8,128)(2,1)S(1)}, bf16[2,48,384]{2,1,0:T(8,128)(2,1)S(1)}, u32[]{:S(2)}, u32[]{:S(2)}) collective-permute-start(bf16[2,48,384]{2,1,0:T(8,128)(2,1)S(1)} %get-tuple-element.61), channel_id=1, source_target_pairs={{0,6},{1,7},{2,4},{3,5},{4,2},{5,3},{6,0},{7,1},{8,14},{9,15},{10,... | collective-permute-start | bytes 221192 | tf_op jit(solution)/shard_map/ppermute | solution.py:601
  72.0 1.8 %shard_map.137 = (bf16[48,128,256]{2,1,0:T(8,128)(2,1)S(1)}, bf16[2048,384]{1,0:T(8,128)(2,1)S(1)}, s32[8,384]{1,0:T(8,128)S(1)}) custom-call(s32[1]{0:T(128)} %bitcast.refs_0_, s32[1]{0:T(128)} %bitcast.2.refs_0_.refs_1_, bf16[768,128]{1,0:T(8,128)(2,1)S(1)} %bitcast.8, bf16[768,128]{1,0:T(8,128)(2,1)S(1)} %collective-permute-done.17.refs_3_, ...), custom_call_target="tpu_custom_call" | custom-call | flops 200000000 | bytes 1402368 | tf_op jit(solution)/shard_map/pallas_call | solution.py:75
  73.8 1.3 %collective-permute-done.16.refs_3_.refs_7_ = bf16[2,48,384]{2,1,0:T(8,128)(2,1)S(1)} collective-permute-done((bf16[2,48,384]{2,1,0:T(8,128)(2,1)S(1)}, bf16[2,48,384]{2,1,0:T(8,128)(2,1)S(1)}, u32[]{:S(2)}, u32[]{:S(2)}) %collective-permute-start.16) | collective-permute-done | bytes 73760 | tf_op jit(solution)/shard_map/ppermute | solution.py:601
  75.1 0.4 collective-permute-start.18
  75.5 5.8 %collective-permute-done.10.refs_0_ = bf16[200,384]{1,0:T(8,128)(2,1)S(1)} collective-permute-done((bf16[200,384]{1,0:T(8,128)(2,1)S(1)}, bf16[200,384]{1,0:T(8,128)(2,1)S(1)}, u32[]{:S(2)}, u32[]{:S(2)}) %collective-permute-start.10) | collective-permute-done | bytes 153632 | tf_op jit(solution)/shard_map/ppermute | solution.py:601
  81.3 0.6 shard_map.136
  81.9 1.5 %collective-permute-start.11 = (bf16[2,48,384]{2,1,0:T(8,128)(2,1)S(1)}, bf16[2,48,384]{2,1,0:T(8,128)(2,1)S(1)}, u32[]{:S(2)}, u32[]{:S(2)}) collective-permute-start(bf16[2,48,384]{2,1,0:T(8,128)(2,1)S(1)} %get-tuple-element.55), channel_id=1, source_target_pairs={{0,2},{1,3},{2,0},{3,1},{4,6},{5,7},{6,4},{7,5},{8,10},{9,11},{10,... | collective-permute-start | bytes 221192 | tf_op jit(solution)/shard_map/ppermute | solution.py:601
  83.4 2.0 %collective-permute-start.13 = (bf16[2,48,384]{2,1,0:T(8,128)(2,1)S(1)}, bf16[2,48,384]{2,1,0:T(8,128)(2,1)S(1)}, u32[]{:S(2)}, u32[]{:S(2)}) collective-permute-start(bf16[2,48,384]{2,1,0:T(8,128)(2,1)S(1)} %get-tuple-element.57), channel_id=1, source_target_pairs={{0,6},{1,7},{2,4},{3,5},{4,2},{5,3},{6,0},{7,1},{8,14},{9,15},{10,... | collective-permute-start | bytes 221192 | tf_op jit(solution)/shard_map/ppermute | solution.py:601
  85.4 2.5 %shard_map.139.refs_4_.refs_11_ = bf16[192,2048]{1,0:T(8,128)(2,1)S(1)} custom-call(s32[1]{0:T(128)} %bitcast.refs_0_, bf16[2,48,384]{2,1,0:T(8,128)(2,1)S(1)} %get-tuple-element.58.refs_6_.refs_0_.refs_1_, bf16[4,48,384]{2,1,0:T(8,128)(2,1)S(1)} %collective-permute-done.18.refs_2_.refs_4_.refs_6_.refs_8_, ...), custom_call_target="tpu_custom_call" | custom-call | flops 200000000 | bytes 5603328 | tf_op jit(solution)/shard_map/pallas_call | solution.py:75
  87.9 0.9 collective-permute-done.13.refs_3_.refs_7_
  88.8 0.1 collective-permute-start.19
  88.9 1.4 %collective-permute-done.19.refs_2_.refs_4_.refs_6_.refs_8_ = bf16[4,48,384]{2,1,0:T(8,128)(2,1)S(1)} collective-permute-done((bf16[4,48,384]{2,1,0:T(8,128)(2,1)S(1)}, bf16[4,48,384]{2,1,0:T(8,128)(2,1)S(1)}, u32[]{:S(2)}, u32[]{:S(2)}) %collective-permute-start.19) | collective-permute-done | bytes 147488 | tf_op jit(solution)/shard_map/ppermute | solution.py:601
  90.2 4.1 %shard_map.141 = f32[192,1312]{1,0:T(8,128)} custom-call(s32[1]{0:T(128)} %bitcast.refs_0_, bf16[2,48,384]{2,1,0:T(8,128)(2,1)S(1)} %get-tuple-element.54.refs_0_.refs_1_, bf16[4,48,384]{2,1,0:T(8,128)(2,1)S(1)} %collective-permute-done.19.refs_2_.refs_4_.refs_6_.refs_8_, bf16[2,48,384]{2,1,0:T(8,128)(2,1)S(1)} %collective-permute-done.11.refs_1_.refs_3_, ...), custom_call_target="tpu_custom_call" | custom-call | flops 300000000 | bytes 6402048 | tf_op jit(solution)/shard_map/pallas_call | solution.py:75
  (36 shorter events, 0.1 us)
Async XLA Ops:
  0.0 17.3 %copy-start.9 = (s32[4,192]{1,0:T(4,128)S(1)}, s32[4,192]{1,0:T(4,128)}, u32[]{:S(2)}) copy-start(s32[4,192]{1,0:T(4,128)} %refs_1_.7) | copy-start | bytes 9220
  0.0 17.3 %copy-start.6 = (bf16[192,1024]{1,0:T(8,128)(2,1)S(1)}, bf16[192,1024]{1,0:T(8,128)(2,1)}, u32[]{:S(2)}) copy-start(bf16[192,1024]{1,0:T(8,128)(2,1)} %refs_2_.8) | copy-start | bytes 1179652
  0.0 0.7 copy-start.11
  0.7 1.0 %copy-start.13 = (bf16[192,1312]{1,0:T(8,128)(2,1)S(1)}, bf16[192,1312]{1,0:T(8,128)(2,1)}, u32[]{:S(2)}) copy-start(bf16[192,1312]{1,0:T(8,128)(2,1)} %refs_2_.5) | copy-start | bytes 1511428
  2.4 15.3 %copy-start.4 = (bf16[1312,384]{1,0:T(8,128)(2,1)S(1)}, bf16[1312,384]{1,0:T(8,128)(2,1)}, u32[]{:S(2)}) copy-start(bf16[1312,384]{1,0:T(8,128)(2,1)} %refs_2_.7) | copy-start | bytes 3022852
  2.4 15.3 %copy-start.8 = (f32[2,12,225]{2,0,1:T(2,128)S(1)}, f32[2,12,225]{2,0,1:T(2,128)}, u32[]{:S(2)}) copy-start(f32[2,12,225]{2,0,1:T(2,128)} %param.20) | copy-start | bytes 64804
  2.4 8.9 %collective-permute-start = (bf16[2,24,1312]{2,1,0:T(8,128)(2,1)S(1)}, bf16[2,24,1312]{2,1,0:T(8,128)(2,1)S(1)}, u32[]{:S(2)}, u32[]{:S(2)}) collective-permute-start(bf16[2,24,1312]{2,1,0:T(8,128)(2,1)S(1)} %get-tuple-element.36), channel_id=1, source_target_pairs={{0,2},{1,3},{2,0},{3,1},{4,6},{5,7},{6,4},{7,5},{8,10},{9,11},{10,... | collective-permute-start | bytes 377864 | tf_op jit(solution)/shard_map/ppermute | solution.py:601
  5.5 11.1 %collective-permute-start.1 = (bf16[2,24,1312]{2,1,0:T(8,128)(2,1)S(1)}, bf16[2,24,1312]{2,1,0:T(8,128)(2,1)S(1)}, u32[]{:S(2)}, u32[]{:S(2)}) collective-permute-start(bf16[2,24,1312]{2,1,0:T(8,128)(2,1)S(1)} %get-tuple-element.37), channel_id=1, source_target_pairs={{0,4},{1,5},{2,6},{3,7},{4,0},{5,1},{6,2},{7,3},{8,12},{9,13},{10,... | collective-permute-start | bytes 377864 | tf_op jit(solution)/shard_map/ppermute | solution.py:601
  7.0 14.3 %collective-permute-start.2 = (bf16[2,24,1312]{2,1,0:T(8,128)(2,1)S(1)}, bf16[2,24,1312]{2,1,0:T(8,128)(2,1)S(1)}, u32[]{:S(2)}, u32[]{:S(2)}) collective-permute-start(bf16[2,24,1312]{2,1,0:T(8,128)(2,1)S(1)} %get-tuple-element.38), channel_id=1, source_target_pairs={{0,6},{1,7},{2,4},{3,5},{4,2},{5,3},{6,0},{7,1},{8,14},{9,15},{10,... | collective-permute-start | bytes 377864 | tf_op jit(solution)/shard_map/ppermute | solution.py:601
  7.0 16.9 %collective-permute-start.3 = (bf16[2,24,1312]{2,1,0:T(8,128)(2,1)S(1)}, bf16[2,24,1312]{2,1,0:T(8,128)(2,1)S(1)}, u32[]{:S(2)}, u32[]{:S(2)}) collective-permute-start(bf16[2,24,1312]{2,1,0:T(8,128)(2,1)S(1)} %get-tuple-element.42), channel_id=1, source_target_pairs={{0,8},{1,9},{2,10},{3,11},{4,12},{5,13},{6,14},{7,15},{8,0},{9,1},... | collective-permute-start | bytes 377864 | tf_op jit(solution)/shard_map/ppermute | solution.py:601
  10.0 19.9 %collective-permute-start.4 = (bf16[2,24,1312]{2,1,0:T(8,128)(2,1)S(1)}, bf16[2,24,1312]{2,1,0:T(8,128)(2,1)S(1)}, u32[]{:S(2)}, u32[]{:S(2)}) collective-permute-start(bf16[2,24,1312]{2,1,0:T(8,128)(2,1)S(1)} %get-tuple-element.43), channel_id=1, source_target_pairs={{0,10},{1,11},{2,8},{3,9},{4,14},{5,15},{6,12},{7,13},{8,2},{9,3},... | collective-permute-start | bytes 377864 | tf_op jit(solution)/shard_map/ppermute | solution.py:601
  11.3 18.6 %collective-permute-start.5 = (bf16[2,24,1312]{2,1,0:T(8,128)(2,1)S(1)}, bf16[2,24,1312]{2,1,0:T(8,128)(2,1)S(1)}, u32[]{:S(2)}, u32[]{:S(2)}) collective-permute-start(bf16[2,24,1312]{2,1,0:T(8,128)(2,1)S(1)} %get-tuple-element.44), channel_id=1, source_target_pairs={{0,12},{1,13},{2,14},{3,15},{4,8},{5,9},{6,10},{7,11},{8,4},{9,5},... | collective-permute-start | bytes 377864 | tf_op jit(solution)/shard_map/ppermute | solution.py:601
  16.5 13.4 %collective-permute-start.6 = (bf16[2,24,1312]{2,1,0:T(8,128)(2,1)S(1)}, bf16[2,24,1312]{2,1,0:T(8,128)(2,1)S(1)}, u32[]{:S(2)}, u32[]{:S(2)}) collective-permute-start(bf16[2,24,1312]{2,1,0:T(8,128)(2,1)S(1)} %get-tuple-element.45), channel_id=1, source_target_pairs={{0,14},{1,15},{2,12},{3,13},{4,10},{5,11},{6,8},{7,9},{8,6},{9,7},... | collective-permute-start | bytes 377864 | tf_op jit(solution)/shard_map/ppermute | solution.py:601
  21.3 27.3 %copy-start.1 = (bf16[2,384,1536]{2,1,0:T(8,128)(2,1)S(1)}, bf16[2,384,1536]{2,1,0:T(8,128)(2,1)}, u32[]{:S(2)}) copy-start(bf16[2,384,1536]{2,1,0:T(8,128)(2,1)} %refs_10_.1) | copy-start | bytes 7077892
  21.3 27.3 %copy-start.2 = (bf16[2,1536,384]{2,1,0:T(8,128)(2,1)S(1)}, bf16[2,1536,384]{2,1,0:T(8,128)(2,1)}, u32[]{:S(2)}) copy-start(bf16[2,1536,384]{2,1,0:T(8,128)(2,1)} %refs_11_.1) | copy-start | bytes 7077892
  23.9 24.7 %copy-start = (bf16[2,384,1152]{2,1,0:T(8,128)(2,1)S(1)}, bf16[2,384,1152]{2,1,0:T(8,128)(2,1)}, u32[]{:S(2)}) copy-start(bf16[2,384,1152]{2,1,0:T(8,128)(2,1)} %refs_5_.2) | copy-start | bytes 5308420
  23.9 24.7 %copy-start.3 = (bf16[2,384,384]{2,1,0:T(8,128)(2,1)S(1)}, bf16[2,384,384]{2,1,0:T(8,128)(2,1)}, u32[]{:S(2)}) copy-start(bf16[2,384,384]{2,1,0:T(8,128)(2,1)} %refs_9_.1) | copy-start | bytes 1769476
  24.0 24.7 %copy-start.7 = (f32[2,384]{1,0:T(2,128)S(1)}, f32[2,384]{1,0:T(2,128)}, u32[]{:S(2)}) copy-start(f32[2,384]{1,0:T(2,128)} %refs_3_.3) | copy-start | bytes 9220
  24.0 24.7 %copy-start.10 = (f32[2,384]{1,0:T(2,128)S(1)}, f32[2,384]{1,0:T(2,128)}, u32[]{:S(2)}) copy-start(f32[2,384]{1,0:T(2,128)} %refs_4_.1) | copy-start | bytes 9220
  30.0 18.6 %collective-permute-start.7 = (bf16[8,24,1312]{2,1,0:T(8,128)(2,1)S(1)}, bf16[8,24,1312]{2,1,0:T(8,128)(2,1)S(1)}, u32[]{:S(2)}, u32[]{:S(2)}) collective-permute-start(bf16[8,24,1312]{2,1,0:T(8,128)(2,1)S(1)} %shard_map.132), channel_id=1, source_target_pairs={{0,1},{1,0},{2,3},{3,2},{4,5},{5,4},{6,7},{7,6},{8,9},{9,8},{10,11... | collective-permute-start | bytes 1511432 | tf_op jit(solution)/shard_map/ppermute | solution.py:601
  47.1 24.9 %collective-permute-start.17 = (bf16[768,128]{1,0:T(8,128)(2,1)S(1)}, bf16[768,128]{1,0:T(8,128)(2,1)S(1)}, u32[]{:S(2)}, u32[]{:S(2)}) collective-permute-start(bf16[768,128]{1,0:T(8,128)(2,1)S(1)} %bitcast.7), channel_id=1, source_target_pairs={{0,16},{16,0},{1,17},{17,1},{2,18},{18,2},{3,19},{19,3},{4,20},{20... | collective-permute-start | bytes 589832 | tf_op jit(solution)/shard_map/ppermute | solution.py:601
  57.1 6.5 %collective-permute-start.8 = (bf16[96,384]{1,0:T(8,128)(2,1)S(1)}, bf16[96,384]{1,0:T(8,128)(2,1)S(1)}, u32[]{:S(2)}, u32[]{:S(2)}) collective-permute-start(bf16[96,384]{1,0:T(8,128)(2,1)S(1)} %get-tuple-element.50.refs_1_.refs_2_), channel_id=1, source_target_pairs={{0,1},{1,2},{2,3},{3,4},{4,5},{5,6},{6,7},{7,8},{8,9},{9,10},{10,1... | collective-permute-start | bytes 221192 | tf_op jit(solution)/shard_map/ppermute | solution.py:607
  57.1 6.5 %collective-permute-start.9 = (bf16[96,384]{1,0:T(8,128)(2,1)S(1)}, bf16[96,384]{1,0:T(8,128)(2,1)S(1)}, u32[]{:S(2)}, u32[]{:S(2)}) collective-permute-start(bf16[96,384]{1,0:T(8,128)(2,1)S(1)} %get-tuple-element.49.refs_0_.refs_1_), channel_id=1, source_target_pairs={{0,15},{1,0},{2,1},{3,2},{4,3},{5,4},{6,5},{7,6},{8,7},{9,8},{10,9... | collective-permute-start | bytes 221192 | tf_op jit(solution)/shard_map/ppermute | solution.py:607
  63.6 8.4 %copy-start.5 = (bf16[384,1312]{0,1:T(8,128)(2,1)S(1)}, bf16[384,1312]{0,1:T(8,128)(2,1)}, u32[]{:S(2)}) copy-start(bf16[384,1312]{0,1:T(8,128)(2,1)} %param.25) | copy-start | bytes 3022852
  63.6 8.4 %copy-start.12 = (s32[1,384]{1,0:T(1,128)S(1)}, s32[1,384]{1,0:T(1,128)}, u32[]{:S(2)}) copy-start(s32[1,384]{1,0:T(1,128)} %refs_5_.3) | copy-start | bytes 4612
  68.4 5.4 %collective-permute-start.14 = (bf16[2,48,384]{2,1,0:T(8,128)(2,1)S(1)}, bf16[2,48,384]{2,1,0:T(8,128)(2,1)S(1)}, u32[]{:S(2)}, u32[]{:S(2)}) collective-permute-start(bf16[2,48,384]{2,1,0:T(8,128)(2,1)S(1)} %get-tuple-element.59), channel_id=1, source_target_pairs={{0,2},{1,3},{2,0},{3,1},{4,6},{5,7},{6,4},{7,5},{8,10},{9,11},{10,... | collective-permute-start | bytes 221192 | tf_op jit(solution)/shard_map/ppermute | solution.py:601
  68.5 5.3 %collective-permute-start.15 = (bf16[2,48,384]{2,1,0:T(8,128)(2,1)S(1)}, bf16[2,48,384]{2,1,0:T(8,128)(2,1)S(1)}, u32[]{:S(2)}, u32[]{:S(2)}) collective-permute-start(bf16[2,48,384]{2,1,0:T(8,128)(2,1)S(1)} %get-tuple-element.60), channel_id=1, source_target_pairs={{0,4},{1,5},{2,6},{3,7},{4,0},{5,1},{6,2},{7,3},{8,12},{9,13},{10,... | collective-permute-start | bytes 221192 | tf_op jit(solution)/shard_map/ppermute | solution.py:601
  68.6 6.5 %collective-permute-start.16 = (bf16[2,48,384]{2,1,0:T(8,128)(2,1)S(1)}, bf16[2,48,384]{2,1,0:T(8,128)(2,1)S(1)}, u32[]{:S(2)}, u32[]{:S(2)}) collective-permute-start(bf16[2,48,384]{2,1,0:T(8,128)(2,1)S(1)} %get-tuple-element.61), channel_id=1, source_target_pairs={{0,6},{1,7},{2,4},{3,5},{4,2},{5,3},{6,0},{7,1},{8,14},{9,15},{10,... | collective-permute-start | bytes 221192 | tf_op jit(solution)/shard_map/ppermute | solution.py:601
  72.0 9.3 %collective-permute-start.10 = (bf16[200,384]{1,0:T(8,128)(2,1)S(1)}, bf16[200,384]{1,0:T(8,128)(2,1)S(1)}, u32[]{:S(2)}, u32[]{:S(2)}) collective-permute-start(bf16[200,384]{1,0:T(8,128)(2,1)S(1)} %get-tuple-element.53), channel_id=1, source_target_pairs={{0,8},{1,9},{2,10},{3,11},{4,12},{5,13},{6,14},{7,15},{8,0},{9,1},... | collective-permute-start | bytes 460808 | tf_op jit(solution)/shard_map/ppermute | solution.py:601
  75.1 10.3 %collective-permute-start.18 = (bf16[4,48,384]{2,1,0:T(8,128)(2,1)S(1)}, bf16[4,48,384]{2,1,0:T(8,128)(2,1)S(1)}, u32[]{:S(2)}, u32[]{:S(2)}) collective-permute-start(bf16[4,48,384]{2,1,0:T(8,128)(2,1)S(1)} %shard_map.138), channel_id=1, source_target_pairs={{0,1},{1,0},{2,3},{3,2},{4,5},{5,4},{6,7},{7,6},{8,9},{9,8},{10,11... | collective-permute-start | bytes 442376 | tf_op jit(solution)/shard_map/ppermute | solution.py:601
  81.9 6.0 %collective-permute-start.11 = (bf16[2,48,384]{2,1,0:T(8,128)(2,1)S(1)}, bf16[2,48,384]{2,1,0:T(8,128)(2,1)S(1)}, u32[]{:S(2)}, u32[]{:S(2)}) collective-permute-start(bf16[2,48,384]{2,1,0:T(8,128)(2,1)S(1)} %get-tuple-element.55), channel_id=1, source_target_pairs={{0,2},{1,3},{2,0},{3,1},{4,6},{5,7},{6,4},{7,5},{8,10},{9,11},{10,... | collective-permute-start | bytes 221192 | tf_op jit(solution)/shard_map/ppermute | solution.py:601
  83.4 4.5 %collective-permute-start.12 = (bf16[2,48,384]{2,1,0:T(8,128)(2,1)S(1)}, bf16[2,48,384]{2,1,0:T(8,128)(2,1)S(1)}, u32[]{:S(2)}, u32[]{:S(2)}) collective-permute-start(bf16[2,48,384]{2,1,0:T(8,128)(2,1)S(1)} %get-tuple-element.56), channel_id=1, source_target_pairs={{0,4},{1,5},{2,6},{3,7},{4,0},{5,1},{6,2},{7,3},{8,12},{9,13},{10,... | collective-permute-start | bytes 221192 | tf_op jit(solution)/shard_map/ppermute | solution.py:601
  83.4 5.4 %collective-permute-start.13 = (bf16[2,48,384]{2,1,0:T(8,128)(2,1)S(1)}, bf16[2,48,384]{2,1,0:T(8,128)(2,1)S(1)}, u32[]{:S(2)}, u32[]{:S(2)}) collective-permute-start(bf16[2,48,384]{2,1,0:T(8,128)(2,1)S(1)} %get-tuple-element.57), channel_id=1, source_target_pairs={{0,6},{1,7},{2,4},{3,5},{4,2},{5,3},{6,0},{7,1},{8,14},{9,15},{10,... | collective-permute-start | bytes 221192 | tf_op jit(solution)/shard_map/ppermute | solution.py:601
  88.8 1.4 %collective-permute-start.19 = (bf16[4,48,384]{2,1,0:T(8,128)(2,1)S(1)}, bf16[4,48,384]{2,1,0:T(8,128)(2,1)S(1)}, u32[]{:S(2)}, u32[]{:S(2)}) collective-permute-start(bf16[4,48,384]{2,1,0:T(8,128)(2,1)S(1)} %shard_map.140), channel_id=1, source_target_pairs={{0,1},{1,0},{2,3},{3,2},{4,5},{5,4},{6,7},{7,6},{8,9},{9,8},{10,11... | collective-permute-start | bytes 442376 | tf_op jit(solution)/shard_map/ppermute | solution.py:601

commit v4 on v2

--- a/solution.py
+++ b/solution.py
@@ -292,8 +292,15 @@
 
 
 def head_mask(heads, span, d):
-    head_of = iota((heads * span, d), 0) // span == iota((heads * span, d), 1) // (d // heads)
-    return head_of.astype(F32).astype(BF16)
+    size = d // heads
+    shape = (LANES // size * span, LANES)
+    return (iota(shape, 0) // span == iota(shape, 1) // size).astype(F32).astype(BF16)
+
+
+def by_group(weights, values):
+    rows = values[0].shape[0]
+    parts = [mm(weights[:, g * rows : (g + 1) * rows], v) for g, v in enumerate(values)]
+    return jnp.concatenate(parts, axis=1)
 
 
 def softmax_parts(scores, side):
@@ -309,13 +316,18 @@
 
 def attend_rows(query, key, value, bias, heads, mask, blocked):
     d = query.shape[1]
-    key_all = jnp.concatenate([key] * heads, axis=0) * mask
-    value_all = jnp.concatenate([value] * heads, axis=0) * mask
-    scores = mm_nt(query, key_all) * (d // heads) ** (-0.5) + bias
+    times = mask.shape[0] // key.shape[0]
+    scores, values = [], []
+    for g in range(d // LANES):
+        lanes = slice(g * LANES, (g + 1) * LANES)
+        expand = lambda v: jnp.concatenate([v[:, lanes]] * times, axis=0) * mask
+        scores.append(mm_nt(query[:, lanes], expand(key)))
+        values.append(expand(value))
+    scores = jnp.concatenate(scores, axis=1) * (d // heads) ** (-0.5) + bias
     if blocked is not None:
         scores = jnp.where(blocked, -1e30, scores)
     weights = softmax_parts(scores, key.shape[0]).astype(BF16)
-    return mm(weights, value_all), weights
+    return by_group(weights, values), weights
 
 
 def feed_forward(residual, gain2, up, down):
@@ -403,7 +415,7 @@
         out, wts = attend_rows(rows(query), rows(key), rows(value), bias_all, heads, mask, None)
         mixed[w], mixed[win_rows + w] = out[:part_rows], out[part_rows:]
         weights[w], weights[win_rows + w] = wts[:part_rows], wts[part_rows:]
-    total = mm(jnp.concatenate(weights, axis=0), mask)
+    total = by_group(jnp.concatenate(weights, axis=0), [mask] * (d // LANES))
     mixed = (jnp.concatenate(mixed, axis=0) / total).astype(BF16)
     attended = mm(mixed, proj()[...]).astype(BF16)
     residual = state + attended.astype(F32)
@@ -466,7 +478,7 @@
             out, wts = attend_rows(q, k, v, b, heads, mask, blocked)
             outs_m[side].append(out)
             outs_w[side].append(wts)
-    total = mm(jnp.concatenate(outs_w[0] + outs_w[1], axis=0), mask)
+    total = by_group(jnp.concatenate(outs_w[0] + outs_w[1], axis=0), [mask] * (d // LANES))
     mixed = (jnp.concatenate(outs_m[0] + outs_m[1], axis=0) / total).astype(BF16)
     attended = mm(mixed, proj()[...]).astype(BF16)
     residual = own + attended.astype(F32)

time: 103 us -> 101 us (0.981)
  Pallas kernels: 31.4 us -> 29.6 us
    pallas_call x14, Pallas kernels: 31.4 us -> 29.6 us  [call(): pl.pallas_call(run, out_shape=list(outs), in_specs=in_specs + [vmem] * le...]
  transfers between devices with their start and end apart: 20 -> 20, of which waited for: 6 -> 6; matrix products, arithmetic and copies ran while one was open for 0% -> 0% of each run, Pallas kernels for 25% -> 24%
where the time goes in v4:
time: 101 us; the launch traced here: 100 us
  starting transfers between devices  36.6 us (36%)
  Pallas kernels  29.6 us (29%)
  local copies, waits for them, and re-layouts  17.2 us (17%)
  waiting for transfers between devices  16.2 us (16%)
    pallas_call x14, Pallas kernels, call(): pl.pallas_call(run, out_shape=list(outs), in_specs=in_specs + [vmem] * le...  29.6 us
    ppermute x17, starting transfers between devices, flip(): lax.ppermute(value, axis, [(source, source ^ bits) for source in range(co...  24 us
    unnamed x64, local copies, waits for them, and re-layouts  17.2 us
    ppermute x17, waiting for transfers between devices, flip(): lax.ppermute(value, axis, [(source, source ^ bits) for source in range(co...  10.3 us
    all_to_all x1, starting transfers between devices, swap(): return lax.all_to_all(value, axis, split_axis=0, concat_axis=0, tiled=True)  8.25 us
    ppermute x2, waiting for transfers between devices, from_behind(): return lax.ppermute(value, axis, pairs)  5.87 us
    ppermute x2, starting transfers between devices, from_behind(): return lax.ppermute(value, axis, pairs)  4.37 us
  transfers between devices with their start and end apart: 20, of which 6 were waited for; matrix products, arithmetic and copies ran while one was open for 0% of the time, Pallas kernels for 24%

profile of v4, /device:TPU:0, one launch (start us, length us, event | category | flops | bytes accessed | tf_op | source)
XLA Modules:
  0.0 100.0 jit_solution(18410132620348911690)
XLA Ops:
  0.0 1.0 %copy-done.26 = bf16[192,1312]{1,0:T(8,128)(2,1)S(1)} copy-done((bf16[192,1312]{1,0:T(8,128)(2,1)S(1)}, bf16[192,1312]{1,0:T(8,128)(2,1)}, u32[]{:S(2)}) %copy-start.26) | copy-done | bytes 503832
  1.1 0.7 copy-done.30
  1.7 0.6 shard_map.127
  2.3 3.1 %collective-permute-start = (bf16[2,24,1312]{2,1,0:T(8,128)(2,1)S(1)}, bf16[2,24,1312]{2,1,0:T(8,128)(2,1)S(1)}, u32[]{:S(2)}, u32[]{:S(2)}) collective-permute-start(bf16[2,24,1312]{2,1,0:T(8,128)(2,1)S(1)} %get-tuple-element.32), channel_id=1, source_target_pairs={{0,2},{1,3},{2,0},{3,1},{4,6},{5,7},{6,4},{7,5},{8,10},{9,11},{10,... | collective-permute-start | bytes 377864 | tf_op jit(solution)/shard_map/ppermute | solution.py:577
  5.4 1.6 %collective-permute-start.1 = (bf16[2,24,1312]{2,1,0:T(8,128)(2,1)S(1)}, bf16[2,24,1312]{2,1,0:T(8,128)(2,1)S(1)}, u32[]{:S(2)}, u32[]{:S(2)}) collective-permute-start(bf16[2,24,1312]{2,1,0:T(8,128)(2,1)S(1)} %get-tuple-element.33), channel_id=1, source_target_pairs={{0,4},{1,5},{2,6},{3,7},{4,0},{5,1},{6,2},{7,3},{8,12},{9,13},{10,... | collective-permute-start | bytes 377864 | tf_op jit(solution)/shard_map/ppermute | solution.py:577
  7.0 3.0 %collective-permute-start.3 = (bf16[2,24,1312]{2,1,0:T(8,128)(2,1)S(1)}, bf16[2,24,1312]{2,1,0:T(8,128)(2,1)S(1)}, u32[]{:S(2)}, u32[]{:S(2)}) collective-permute-start(bf16[2,24,1312]{2,1,0:T(8,128)(2,1)S(1)} %get-tuple-element.35), channel_id=1, source_target_pairs={{0,8},{1,9},{2,10},{3,11},{4,12},{5,13},{6,14},{7,15},{8,0},{9,1},... | collective-permute-start | bytes 377864 | tf_op jit(solution)/shard_map/ppermute | solution.py:577
  9.9 1.3 %collective-permute-start.4 = (bf16[2,24,1312]{2,1,0:T(8,128)(2,1)S(1)}, bf16[2,24,1312]{2,1,0:T(8,128)(2,1)S(1)}, u32[]{:S(2)}, u32[]{:S(2)}) collective-permute-start(bf16[2,24,1312]{2,1,0:T(8,128)(2,1)S(1)} %get-tuple-element.36), channel_id=1, source_target_pairs={{0,10},{1,11},{2,8},{3,9},{4,14},{5,15},{6,12},{7,13},{8,2},{9,3},... | collective-permute-start | bytes 377864 | tf_op jit(solution)/shard_map/ppermute | solution.py:577
  11.2 0.4 shard_map.128.refs_4_
  11.6 0.8 copy-done.24
  12.4 2.4 %shard_map.129 = (bf16[192,192]{1,0:T(8,128)(2,1)S(1)}, bf16[192,576]{1,0:T(8,128)(2,1)S(1)}, bf16[2048,384]{1,0:T(8,128)(2,1)S(1)}, f32[2,64,768]{2,1,0:T(8,128)S(1)}, bf16[768,192]{1,0:T(8,128)(2,1)S(1)}) custom-call(s32[1]{0:T(128)} %bitcast.refs_0_, s32[4,192]{1,0:T(4,128)S(1)} %copy-done.29, bf16[1312,384]{1,0:T(8,128)(2,1)S(1)} %copy-done.24, ...), custom_call_target="tpu_custom_call" | custom-call | flops 2000000000 | bytes 1032288 | tf_op jit(solution)/shard_map/pallas_call | solution.py:74
  14.9 0.7 copy-done.17
  15.6 0.7 copy-done.20
  16.3 1.4 %shard_map.130.refs_4_.refs_12_ = bf16[48,256,128]{2,1,0:T(8,128)(2,1)S(1)} custom-call(s32[1]{0:T(128)} %bitcast.refs_0_, s32[4,192]{1,0:T(4,128)S(1)} %copy-done.29, bf16[192,1024]{1,0:T(8,128)(2,1)S(1)} %copy-done.27, bf16[2048,384]{1,0:T(8,128)(2,1)S(1)} %get-tuple-element.39.refs_3_.refs_6_.refs_14_), custom_call_target="tpu_custom_call" | custom-call | flops 2000000000 | bytes 396288 | tf_op jit(solution)/shard_map/pallas_call | solution.py:74
  17.8 3.7 %collective-permute-start.5 = (bf16[2,24,1312]{2,1,0:T(8,128)(2,1)S(1)}, bf16[2,24,1312]{2,1,0:T(8,128)(2,1)S(1)}, u32[]{:S(2)}, u32[]{:S(2)}) collective-permute-start(bf16[2,24,1312]{2,1,0:T(8,128)(2,1)S(1)} %get-tuple-element.37), channel_id=1, source_target_pairs={{0,12},{1,13},{2,14},{3,15},{4,8},{5,9},{6,10},{7,11},{8,4},{9,5},... | collective-permute-start | bytes 377864 | tf_op jit(solution)/shard_map/ppermute | solution.py:577
  21.5 2.6 %shard_map.131.refs_8_.refs_15_ = f32[192,384]{1,0:T(8,128)S(1)} custom-call(bf16[2,24,1312]{2,1,0:T(8,128)(2,1)S(1)} %get-tuple-element.31.refs_2_.refs_0_, bf16[2,24,1312]{2,1,0:T(8,128)(2,1)S(1)} %collective-permute-done.refs_1_, bf16[2,24,1312]{2,1,0:T(8,128)(2,1)S(1)} %collective-permute-done.1.refs_2_, ...), custom_call_target="tpu_custom_call" | custom-call | flops 2000000000 | bytes 5296128 | tf_op jit(solution)/shard_map/pallas_call | solution.py:74
  24.1 5.7 %collective-permute-done.4.refs_5_.refs_6_ = bf16[2,24,1312]{2,1,0:T(8,128)(2,1)S(1)} collective-permute-done((bf16[2,24,1312]{2,1,0:T(8,128)(2,1)S(1)}, bf16[2,24,1312]{2,1,0:T(8,128)(2,1)S(1)}, u32[]{:S(2)}, u32[]{:S(2)}) %collective-permute-start.4) | collective-permute-done | bytes 125984 | tf_op jit(solution)/shard_map/ppermute | solution.py:577
  29.9 0.9 shard_map.132
  30.8 0.7 copy-done.9
  31.5 8.2 %all-to-all-start = ((bf16[16,48,256]{2,1,0:T(8,128)(2,1)}), bf16[16,48,256]{2,1,0:T(8,128)(2,1)}, u32[]{:S(2)}, u32[]{:S(2)}) async-start(bf16[16,48,256]{2,1,0:T(8,128)(2,1)} %bitcast.5), calls=%async_computation | async-start | bytes 786432 | tf_op jit(solution)/shard_map/all_to_all | solution.py:559
  39.8 1.7 %copy-done.1 = bf16[2,384,1536]{2,1,0:T(8,128)(2,1)S(1)} copy-done((bf16[2,384,1536]{2,1,0:T(8,128)(2,1)S(1)}, bf16[2,384,1536]{2,1,0:T(8,128)(2,1)}, u32[]{:S(2)}) %copy-start.1) | copy-done | bytes 2359320
  41.5 1.7 %copy-done.3 = bf16[2,1536,384]{2,1,0:T(8,128)(2,1)S(1)} copy-done((bf16[2,1536,384]{2,1,0:T(8,128)(2,1)S(1)}, bf16[2,1536,384]{2,1,0:T(8,128)(2,1)}, u32[]{:S(2)}) %copy-start.3) | copy-done | bytes 2359320
  43.2 1.9 %copy-done.5 = bf16[48,256,128]{2,1,0:T(8,128)(2,1)S(1)} copy-done((bf16[48,256,128]{2,1,0:T(8,128)(2,1)S(1)}, bf16[48,256,128]{2,1,0:T(8,128)(2,1)}, u32[]{:S(2)}) %copy-start.5) | copy-done | bytes 3145752
  45.1 1.4 %copy-done.8 = bf16[2048,384]{1,0:T(8,128)(2,1)S(1)} copy-done((bf16[2048,384]{1,0:T(8,128)(2,1)S(1)}, bf16[2048,384]{1,0:T(8,128)(2,1)}, u32[]{:S(2)}) %copy-start.8) | copy-done | bytes 1572888
  46.5 1.0 copy-done.10
  47.4 0.9 copy-done.12
  48.3 0.9 copy-done.14
  49.2 0.9 copy-done.16
  50.2 0.9 copy-done.21
  51.1 7.8 %shard_map.133 = (bf16[96,384]{1,0:T(8,128)(2,1)S(1)}, bf16[96,384]{1,0:T(8,128)(2,1)S(1)}) custom-call(bf16[8,24,1312]{2,1,0:T(8,128)(2,1)S(1)} %collective-permute-done.7.refs_0_.refs_1_.refs_2_.refs_3_.refs_5_.refs_7_.refs_9_.refs_11_, bf16[8,24,1312]{2,1,0:T(8,128)(2,1)S(1)} %collective-permute-done.7.refs_0_.refs_1_.refs_2_.refs_3_.refs_5_.refs_7_.refs_9_.refs_11_, ...), custom_call_target="tpu_custom_call" | custom-call | flops 4000000000 | bytes 17246208 | tf_op jit(solution)/shard_map/pallas_call | solution.py:74
  58.9 4.4 %collective-permute-start.9 = (bf16[96,384]{1,0:T(8,128)(2,1)S(1)}, bf16[96,384]{1,0:T(8,128)(2,1)S(1)}, u32[]{:S(2)}, u32[]{:S(2)}) collective-permute-start(bf16[96,384]{1,0:T(8,128)(2,1)S(1)} %get-tuple-element.43.refs_0_.refs_1_), channel_id=1, source_target_pairs={{0,15},{1,0},{2,1},{3,2},{4,3},{5,4},{6,5},{7,6},{8,7},{9,8},{10,9... | collective-permute-start | bytes 221192 | tf_op jit(solution)/shard_map/ppermute | solution.py:583
  63.3 0.6 shard_map.134.refs_0_
  63.9 1.4 %collective-permute-done.9.refs_8_ = bf16[96,384]{1,0:T(8,128)(2,1)S(1)} collective-permute-done((bf16[96,384]{1,0:T(8,128)(2,1)S(1)}, bf16[96,384]{1,0:T(8,128)(2,1)S(1)}, u32[]{:S(2)}, u32[]{:S(2)}) %collective-permute-start.9) | collective-permute-done | bytes 73760 | tf_op jit(solution)/shard_map/ppermute | solution.py:583
  65.2 4.5 %collective-permute-done.8.refs_7_ = bf16[96,384]{1,0:T(8,128)(2,1)S(1)} collective-permute-done((bf16[96,384]{1,0:T(8,128)(2,1)S(1)}, bf16[96,384]{1,0:T(8,128)(2,1)S(1)}, u32[]{:S(2)}, u32[]{:S(2)}) %collective-permute-start.8) | collective-permute-done | bytes 73760 | tf_op jit(solution)/shard_map/ppermute | solution.py:583
  69.7 3.8 %shard_map.135 = (bf16[2,48,384]{2,1,0:T(8,128)(2,1)S(1)}, bf16[2,48,384]{2,1,0:T(8,128)(2,1)S(1)}, bf16[2,48,384]{2,1,0:T(8,128)(2,1)S(1)}, bf16[2,48,384]{2,1,...) custom-call(bf16[192,1152]{1,0:T(8,128)(2,1)S(1)} %shard_map.134.ref, ...), custom_call_target="tpu_custom_call" | custom-call | flops 2000000000 | bytes 8509440 | tf_op jit(solution)/shard_map/pallas_call | solution.py:74
  73.5 0.1 collective-permute-start.14
  73.7 3.4 %collective-permute-start.16 = (bf16[2,48,384]{2,1,0:T(8,128)(2,1)S(1)}, bf16[2,48,384]{2,1,0:T(8,128)(2,1)S(1)}, u32[]{:S(2)}, u32[]{:S(2)}) collective-permute-start(bf16[2,48,384]{2,1,0:T(8,128)(2,1)S(1)} %get-tuple-element.53), channel_id=1, source_target_pairs={{0,6},{1,7},{2,4},{3,5},{4,2},{5,3},{6,0},{7,1},{8,14},{9,15},{10,... | collective-permute-start | bytes 221192 | tf_op jit(solution)/shard_map/ppermute | solution.py:577
  77.1 1.2 %copy-done.25 = bf16[384,1312]{0,1:T(8,128)(2,1)S(1)} copy-done((bf16[384,1312]{0,1:T(8,128)(2,1)S(1)}, bf16[384,1312]{0,1:T(8,128)(2,1)}, u32[]{:S(2)}) %copy-start.25) | copy-done | bytes 1007640
  78.3 2.8 %shard_map.136 = (bf16[48,128,256]{2,1,0:T(8,128)(2,1)S(1)}, bf16[2048,384]{1,0:T(8,128)(2,1)S(1)}, s32[8,384]{1,0:T(8,128)S(1)}) custom-call(s32[1]{0:T(128)} %bitcast.refs_0_, bf16[768,256]{1,0:T(8,128)(2,1)} %bitcast.3.refs_1_, bf16[1312,384]{1,0:T(8,128)(2,1)S(1)} %bitcast.6, s32[1,384]{1,0:T(1,128)S(1)} %copy-done.31, ...), custom_call_target="tpu_custom_call" | custom-call | flops 2000000000 | bytes 1402368 | tf_op jit(solution)/shard_map/pallas_call | solution.py:74
  81.1 0.1 collective-permute-start.17
  81.2 0.1 collective-permute-start.10
  81.3 2.4 %collective-permute-start.11 = (bf16[2,48,384]{2,1,0:T(8,128)(2,1)S(1)}, bf16[2,48,384]{2,1,0:T(8,128)(2,1)S(1)}, u32[]{:S(2)}, u32[]{:S(2)}) collective-permute-start(bf16[2,48,384]{2,1,0:T(8,128)(2,1)S(1)} %get-tuple-element.47), channel_id=1, source_target_pairs={{0,10},{1,11},{2,8},{3,9},{4,14},{5,15},{6,12},{7,13},{8,2},{9,3},... | collective-permute-start | bytes 221192 | tf_op jit(solution)/shard_map/ppermute | solution.py:577
  83.7 1.2 %collective-permute-start.12 = (bf16[2,48,384]{2,1,0:T(8,128)(2,1)S(1)}, bf16[2,48,384]{2,1,0:T(8,128)(2,1)S(1)}, u32[]{:S(2)}, u32[]{:S(2)}) collective-permute-start(bf16[2,48,384]{2,1,0:T(8,128)(2,1)S(1)} %get-tuple-element.48), channel_id=1, source_target_pairs={{0,12},{1,13},{2,14},{3,15},{4,8},{5,9},{6,10},{7,11},{8,4},{9,5},... | collective-permute-start | bytes 221192 | tf_op jit(solution)/shard_map/ppermute | solution.py:577
  84.9 4.0 %collective-permute-start.13 = (bf16[2,48,384]{2,1,0:T(8,128)(2,1)S(1)}, bf16[2,48,384]{2,1,0:T(8,128)(2,1)S(1)}, u32[]{:S(2)}, u32[]{:S(2)}) collective-permute-start(bf16[2,48,384]{2,1,0:T(8,128)(2,1)S(1)} %get-tuple-element.49), channel_id=1, source_target_pairs={{0,14},{1,15},{2,12},{3,13},{4,10},{5,11},{6,8},{7,9},{8,6},{9,7},... | collective-permute-start | bytes 221192 | tf_op jit(solution)/shard_map/ppermute | solution.py:577
  88.9 2.4 %shard_map.138.refs_4_.refs_11_ = bf16[192,2048]{1,0:T(8,128)(2,1)S(1)} custom-call(s32[1]{0:T(128)} %bitcast.refs_0_, bf16[2,48,384]{2,1,0:T(8,128)(2,1)S(1)} %get-tuple-element.50.refs_4_.refs_0_.refs_1_, bf16[4,48,384]{2,1,0:T(8,128)(2,1)S(1)} %collective-permute-done.17.refs_2_.refs_4_.refs_6_.refs_8_, ...), custom_call_target="tpu_custom_call" | custom-call | flops 2000000000 | bytes 5603328 | tf_op jit(solution)/shard_map/pallas_call | solution.py:74
  91.4 1.2 %collective-permute-done.10.refs_0_.refs_1_ = bf16[2,48,384]{2,1,0:T(8,128)(2,1)S(1)} collective-permute-done((bf16[2,48,384]{2,1,0:T(8,128)(2,1)S(1)}, bf16[2,48,384]{2,1,0:T(8,128)(2,1)S(1)}, u32[]{:S(2)}, u32[]{:S(2)}) %collective-permute-start.10) | collective-permute-done | bytes 73760 | tf_op jit(solution)/shard_map/ppermute | solution.py:577
  92.6 1.9 %collective-permute-done.11.refs_1_.refs_3_ = bf16[2,48,384]{2,1,0:T(8,128)(2,1)S(1)} collective-permute-done((bf16[2,48,384]{2,1,0:T(8,128)(2,1)S(1)}, bf16[2,48,384]{2,1,0:T(8,128)(2,1)S(1)}, u32[]{:S(2)}, u32[]{:S(2)}) %collective-permute-start.11) | collective-permute-done | bytes 73760 | tf_op jit(solution)/shard_map/ppermute | solution.py:577
  94.6 1.4 %collective-permute-done.18.refs_2_.refs_4_.refs_6_.refs_8_ = bf16[4,48,384]{2,1,0:T(8,128)(2,1)S(1)} collective-permute-done((bf16[4,48,384]{2,1,0:T(8,128)(2,1)S(1)}, bf16[4,48,384]{2,1,0:T(8,128)(2,1)S(1)}, u32[]{:S(2)}, u32[]{:S(2)}) %collective-permute-start.18) | collective-permute-done | bytes 147488 | tf_op jit(solution)/shard_map/ppermute | solution.py:577
  96.0 4.0 %shard_map.140 = f32[192,1312]{1,0:T(8,128)} custom-call(s32[1]{0:T(128)} %bitcast.refs_0_, bf16[2,48,384]{2,1,0:T(8,128)(2,1)S(1)} %collective-permute-done.10.refs_0_.refs_1_, bf16[4,48,384]{2,1,0:T(8,128)(2,1)S(1)} %collective-permute-done.18.refs_2_.refs_4_.refs_6_.refs_8_, bf16[2,48,384]{2,1,0:T(8,128)(2,1)S(1)} %collective-permute-done.11.refs_1_.refs_3_, ...), custom_call_target="tpu_custom_call" | custom-call | flops 3000000000 | bytes 6402048 | tf_op jit(solution)/shard_map/pallas_call | solution.py:74
  (70 shorter events, 0.3 us)
Async XLA Ops:
  0.0 1.0 %copy-start.26 = (bf16[192,1312]{1,0:T(8,128)(2,1)S(1)}, bf16[192,1312]{1,0:T(8,128)(2,1)}, u32[]{:S(2)}) copy-start(bf16[192,1312]{1,0:T(8,128)(2,1)} %refs_2_.4) | copy-start | bytes 1511428
  1.7 9.5 %copy-start.27 = (bf16[192,1024]{1,0:T(8,128)(2,1)S(1)}, bf16[192,1024]{1,0:T(8,128)(2,1)}, u32[]{:S(2)}) copy-start(bf16[192,1024]{1,0:T(8,128)(2,1)} %refs_2_.6) | copy-start | bytes 1179652
  1.7 9.5 %copy-start.29 = (s32[4,192]{1,0:T(4,128)S(1)}, s32[4,192]{1,0:T(4,128)}, u32[]{:S(2)}) copy-start(s32[4,192]{1,0:T(4,128)} %refs_1_.7) | copy-start | bytes 9220
  2.3 15.5 %collective-permute-start = (bf16[2,24,1312]{2,1,0:T(8,128)(2,1)S(1)}, bf16[2,24,1312]{2,1,0:T(8,128)(2,1)S(1)}, u32[]{:S(2)}, u32[]{:S(2)}) collective-permute-start(bf16[2,24,1312]{2,1,0:T(8,128)(2,1)S(1)} %get-tuple-element.32), channel_id=1, source_target_pairs={{0,2},{1,3},{2,0},{3,1},{4,6},{5,7},{6,4},{7,5},{8,10},{9,11},{10,... | collective-permute-start | bytes 377864 | tf_op jit(solution)/shard_map/ppermute | solution.py:577
  5.4 16.1 %collective-permute-start.1 = (bf16[2,24,1312]{2,1,0:T(8,128)(2,1)S(1)}, bf16[2,24,1312]{2,1,0:T(8,128)(2,1)S(1)}, u32[]{:S(2)}, u32[]{:S(2)}) collective-permute-start(bf16[2,24,1312]{2,1,0:T(8,128)(2,1)S(1)} %get-tuple-element.33), channel_id=1, source_target_pairs={{0,4},{1,5},{2,6},{3,7},{4,0},{5,1},{6,2},{7,3},{8,12},{9,13},{10,... | collective-permute-start | bytes 377864 | tf_op jit(solution)/shard_map/ppermute | solution.py:577
  7.0 14.5 %collective-permute-start.2 = (bf16[2,24,1312]{2,1,0:T(8,128)(2,1)S(1)}, bf16[2,24,1312]{2,1,0:T(8,128)(2,1)S(1)}, u32[]{:S(2)}, u32[]{:S(2)}) collective-permute-start(bf16[2,24,1312]{2,1,0:T(8,128)(2,1)S(1)} %get-tuple-element.34), channel_id=1, source_target_pairs={{0,6},{1,7},{2,4},{3,5},{4,2},{5,3},{6,0},{7,1},{8,14},{9,15},{10,... | collective-permute-start | bytes 377864 | tf_op jit(solution)/shard_map/ppermute | solution.py:577
  7.0 17.2 %collective-permute-start.3 = (bf16[2,24,1312]{2,1,0:T(8,128)(2,1)S(1)}, bf16[2,24,1312]{2,1,0:T(8,128)(2,1)S(1)}, u32[]{:S(2)}, u32[]{:S(2)}) collective-permute-start(bf16[2,24,1312]{2,1,0:T(8,128)(2,1)S(1)} %get-tuple-element.35), channel_id=1, source_target_pairs={{0,8},{1,9},{2,10},{3,11},{4,12},{5,13},{6,14},{7,15},{8,0},{9,1},... | collective-permute-start | bytes 377864 | tf_op jit(solution)/shard_map/ppermute | solution.py:577
  9.9 19.9 %collective-permute-start.4 = (bf16[2,24,1312]{2,1,0:T(8,128)(2,1)S(1)}, bf16[2,24,1312]{2,1,0:T(8,128)(2,1)S(1)}, u32[]{:S(2)}, u32[]{:S(2)}) collective-permute-start(bf16[2,24,1312]{2,1,0:T(8,128)(2,1)S(1)} %get-tuple-element.36), channel_id=1, source_target_pairs={{0,10},{1,11},{2,8},{3,9},{4,14},{5,15},{6,12},{7,13},{8,2},{9,3},... | collective-permute-start | bytes 377864 | tf_op jit(solution)/shard_map/ppermute | solution.py:577
  11.2 1.2 %copy-start.24 = (bf16[1312,384]{1,0:T(8,128)(2,1)S(1)}, bf16[1312,384]{1,0:T(8,128)(2,1)}, u32[]{:S(2)}) copy-start(bf16[1312,384]{1,0:T(8,128)(2,1)} %refs_2_.5) | copy-start | bytes 3022852
  11.2 1.2 %copy-start.28 = (f32[2,12,225]{2,0,1:T(2,128)S(1)}, f32[2,12,225]{2,0,1:T(2,128)}, u32[]{:S(2)}) copy-start(f32[2,12,225]{2,0,1:T(2,128)} %param.20) | copy-start | bytes 64804
  11.6 3.3 %copy-start.19 = (bf16[768,256]{1,0:T(8,128)(2,1)}, bf16[768,256]{1,0:T(8,128)(2,1)S(1)}, u32[]{:S(2)}) copy-start(bf16[768,256]{1,0:T(8,128)(2,1)S(1)} %shard_map.128.refs_4_) | copy-start | bytes 1179652
  16.3 5.2 %copy-start.7 = (bf16[2048,384]{1,0:T(8,128)(2,1)}, bf16[2048,384]{1,0:T(8,128)(2,1)S(1)}, u32[]{:S(2)}) copy-start(bf16[2048,384]{1,0:T(8,128)(2,1)S(1)} %get-tuple-element.39.refs_3_.refs_6_.refs_14_) | copy-start | bytes 4718596
  17.8 6.3 %copy-start.4 = (bf16[48,256,128]{2,1,0:T(8,128)(2,1)}, bf16[48,256,128]{2,1,0:T(8,128)(2,1)S(1)}, u32[]{:S(2)}) copy-start(bf16[48,256,128]{2,1,0:T(8,128)(2,1)S(1)} %shard_map.130.refs_4_.refs_12_) | copy-start | bytes 9437188
  17.8 12.1 %collective-permute-start.5 = (bf16[2,24,1312]{2,1,0:T(8,128)(2,1)S(1)}, bf16[2,24,1312]{2,1,0:T(8,128)(2,1)S(1)}, u32[]{:S(2)}, u32[]{:S(2)}) collective-permute-start(bf16[2,24,1312]{2,1,0:T(8,128)(2,1)S(1)} %get-tuple-element.37), channel_id=1, source_target_pairs={{0,12},{1,13},{2,14},{3,15},{4,8},{5,9},{6,10},{7,11},{8,4},{9,5},... | collective-permute-start | bytes 377864 | tf_op jit(solution)/shard_map/ppermute | solution.py:577
  21.5 8.4 %collective-permute-start.6 = (bf16[2,24,1312]{2,1,0:T(8,128)(2,1)S(1)}, bf16[2,24,1312]{2,1,0:T(8,128)(2,1)S(1)}, u32[]{:S(2)}, u32[]{:S(2)}) collective-permute-start(bf16[2,24,1312]{2,1,0:T(8,128)(2,1)S(1)} %get-tuple-element.38), channel_id=1, source_target_pairs={{0,14},{1,15},{2,12},{3,13},{4,10},{5,11},{6,8},{7,9},{8,6},{9,7},... | collective-permute-start | bytes 377864 | tf_op jit(solution)/shard_map/ppermute | solution.py:577
  24.1 15.7 %copy-start = (bf16[2,384,1152]{2,1,0:T(8,128)(2,1)S(1)}, bf16[2,384,1152]{2,1,0:T(8,128)(2,1)}, u32[]{:S(2)}) copy-start(bf16[2,384,1152]{2,1,0:T(8,128)(2,1)} %refs_5_.1) | copy-start | bytes 5308420
  24.1 15.7 %copy-start.6 = (bf16[2,384,384]{2,1,0:T(8,128)(2,1)S(1)}, bf16[2,384,384]{2,1,0:T(8,128)(2,1)}, u32[]{:S(2)}) copy-start(bf16[2,384,384]{2,1,0:T(8,128)(2,1)} %refs_9_.1) | copy-start | bytes 1769476
  24.1 15.7 %copy-start.22 = (f32[2,384]{1,0:T(2,128)S(1)}, f32[2,384]{1,0:T(2,128)}, u32[]{:S(2)}) copy-start(f32[2,384]{1,0:T(2,128)} %refs_3_.4) | copy-start | bytes 9220
  24.1 15.7 %copy-start.23 = (f32[2,384]{1,0:T(2,128)S(1)}, f32[2,384]{1,0:T(2,128)}, u32[]{:S(2)}) copy-start(f32[2,384]{1,0:T(2,128)} %refs_4_.1) | copy-start | bytes 9220
  29.9 0.9 copy-start.11
  29.9 1.7 %copy-start.13 = (bf16[2,24,1312]{2,1,0:T(8,128)(2,1)}, bf16[2,24,1312]{2,1,0:T(8,128)(2,1)S(1)}, u32[]{:S(2)}) copy-start(bf16[2,24,1312]{2,1,0:T(8,128)(2,1)S(1)} %collective-permute-done.5.refs_6_.refs_8_) | copy-start | bytes 377860
  29.9 1.6 %copy-start.15 = (bf16[2,24,1312]{2,1,0:T(8,128)(2,1)}, bf16[2,24,1312]{2,1,0:T(8,128)(2,1)S(1)}, u32[]{:S(2)}) copy-start(bf16[2,24,1312]{2,1,0:T(8,128)(2,1)S(1)} %collective-permute-done.6.refs_7_.refs_10_) | copy-start | bytes 377860
  31.5 8.3 %collective-permute-start.7 = (bf16[8,24,1312]{2,1,0:T(8,128)(2,1)}, bf16[8,24,1312]{2,1,0:T(8,128)(2,1)S(1)}, u32[]{:S(2)}, u32[]{:S(2)}) collective-permute-start(bf16[8,24,1312]{2,1,0:T(8,128)(2,1)} %shard_map.132), channel_id=1, source_target_pairs={{0,1},{1,0},{2,3},{3,2},{4,5},{5,4},{6,7},{7,6},{8,9},{9,8},{10,11... | collective-permute-start | bytes 1511432 | tf_op jit(solution)/shard_map/ppermute | solution.py:577
  31.5 45.5 %all-to-all-start = ((bf16[16,48,256]{2,1,0:T(8,128)(2,1)}), bf16[16,48,256]{2,1,0:T(8,128)(2,1)}, u32[]{:S(2)}, u32[]{:S(2)}) async-start(bf16[16,48,256]{2,1,0:T(8,128)(2,1)} %bitcast.5), calls=%async_computation | async-start | bytes 786432 | tf_op jit(solution)/shard_map/all_to_all | solution.py:559
  39.8 1.7 %copy-start.1 = (bf16[2,384,1536]{2,1,0:T(8,128)(2,1)S(1)}, bf16[2,384,1536]{2,1,0:T(8,128)(2,1)}, u32[]{:S(2)}) copy-start(bf16[2,384,1536]{2,1,0:T(8,128)(2,1)} %refs_10_.1) | copy-start | bytes 7077892
  41.5 1.7 %copy-start.3 = (bf16[2,1536,384]{2,1,0:T(8,128)(2,1)S(1)}, bf16[2,1536,384]{2,1,0:T(8,128)(2,1)}, u32[]{:S(2)}) copy-start(bf16[2,1536,384]{2,1,0:T(8,128)(2,1)} %refs_11_.1) | copy-start | bytes 7077892
  43.2 1.9 %copy-start.5 = (bf16[48,256,128]{2,1,0:T(8,128)(2,1)S(1)}, bf16[48,256,128]{2,1,0:T(8,128)(2,1)}, u32[]{:S(2)}) copy-start(bf16[48,256,128]{2,1,0:T(8,128)(2,1)} %copy-done.4) | copy-start | bytes 9437188
  45.1 1.4 %copy-start.8 = (bf16[2048,384]{1,0:T(8,128)(2,1)S(1)}, bf16[2048,384]{1,0:T(8,128)(2,1)}, u32[]{:S(2)}) copy-start(bf16[2048,384]{1,0:T(8,128)(2,1)} %copy-done.7) | copy-start | bytes 4718596
  46.5 1.0 copy-start.10
  47.4 0.9 copy-start.12
  48.3 0.9 copy-start.14
  49.2 0.9 copy-start.16
  50.2 0.9 copy-start.21
  51.1 18.6 %copy-start.18 = (bf16[768,192]{1,0:T(8,128)(2,1)S(1)}, bf16[768,192]{1,0:T(8,128)(2,1)}, u32[]{:S(2)}) copy-start(bf16[768,192]{1,0:T(8,128)(2,1)} %copy-done.17) | copy-start | bytes 884740
  58.9 10.9 %copy-start.2 = (bf16[2,384,1536]{2,1,0:T(8,128)(2,1)S(1)}, bf16[2,384,1536]{2,1,0:T(8,128)(2,1)}, u32[]{:S(2)}) copy-start(bf16[2,384,1536]{2,1,0:T(8,128)(2,1)} %refs_10_.1) | copy-start | bytes 7077892
  58.9 6.3 %collective-permute-start.9 = (bf16[96,384]{1,0:T(8,128)(2,1)S(1)}, bf16[96,384]{1,0:T(8,128)(2,1)S(1)}, u32[]{:S(2)}, u32[]{:S(2)}) collective-permute-start(bf16[96,384]{1,0:T(8,128)(2,1)S(1)} %get-tuple-element.43.refs_0_.refs_1_), channel_id=1, source_target_pairs={{0,15},{1,0},{2,1},{3,2},{4,3},{5,4},{6,5},{7,6},{8,7},{9,8},{10,9... | collective-permute-start | bytes 221192 | tf_op jit(solution)/shard_map/ppermute | solution.py:583
  63.3 6.5 %collective-permute-start.8 = (bf16[96,384]{1,0:T(8,128)(2,1)S(1)}, bf16[96,384]{1,0:T(8,128)(2,1)S(1)}, u32[]{:S(2)}, u32[]{:S(2)}) collective-permute-start(bf16[96,384]{1,0:T(8,128)(2,1)S(1)} %get-tuple-element.44.refs_1_.refs_2_), channel_id=1, source_target_pairs={{0,1},{1,2},{2,3},{3,4},{4,5},{5,6},{6,7},{7,8},{8,9},{9,10},{10,1... | collective-permute-start | bytes 221192 | tf_op jit(solution)/shard_map/ppermute | solution.py:583
  69.7 7.3 %copy-start.31 = (s32[1,384]{1,0:T(1,128)S(1)}, s32[1,384]{1,0:T(1,128)}, u32[]{:S(2)}) copy-start(s32[1,384]{1,0:T(1,128)} %refs_3_.5) | copy-start | bytes 4612
  73.5 7.6 %collective-permute-start.14 = (bf16[2,48,384]{2,1,0:T(8,128)(2,1)S(1)}, bf16[2,48,384]{2,1,0:T(8,128)(2,1)S(1)}, u32[]{:S(2)}, u32[]{:S(2)}) collective-permute-start(bf16[2,48,384]{2,1,0:T(8,128)(2,1)S(1)} %get-tuple-element.51), channel_id=1, source_target_pairs={{0,2},{1,3},{2,0},{3,1},{4,6},{5,7},{6,4},{7,5},{8,10},{9,11},{10,... | collective-permute-start | bytes 221192 | tf_op jit(solution)/shard_map/ppermute | solution.py:577
  73.6 7.5 %collective-permute-start.15 = (bf16[2,48,384]{2,1,0:T(8,128)(2,1)S(1)}, bf16[2,48,384]{2,1,0:T(8,128)(2,1)S(1)}, u32[]{:S(2)}, u32[]{:S(2)}) collective-permute-start(bf16[2,48,384]{2,1,0:T(8,128)(2,1)S(1)} %get-tuple-element.52), channel_id=1, source_target_pairs={{0,4},{1,5},{2,6},{3,7},{4,0},{5,1},{6,2},{7,3},{8,12},{9,13},{10,... | collective-permute-start | bytes 221192 | tf_op jit(solution)/shard_map/ppermute | solution.py:577
  73.7 7.4 %collective-permute-start.16 = (bf16[2,48,384]{2,1,0:T(8,128)(2,1)S(1)}, bf16[2,48,384]{2,1,0:T(8,128)(2,1)S(1)}, u32[]{:S(2)}, u32[]{:S(2)}) collective-permute-start(bf16[2,48,384]{2,1,0:T(8,128)(2,1)S(1)} %get-tuple-element.53), channel_id=1, source_target_pairs={{0,6},{1,7},{2,4},{3,5},{4,2},{5,3},{6,0},{7,1},{8,14},{9,15},{10,... | collective-permute-start | bytes 221192 | tf_op jit(solution)/shard_map/ppermute | solution.py:577
  77.1 1.2 %copy-start.25 = (bf16[384,1312]{0,1:T(8,128)(2,1)S(1)}, bf16[384,1312]{0,1:T(8,128)(2,1)}, u32[]{:S(2)}) copy-start(bf16[384,1312]{0,1:T(8,128)(2,1)} %param.25) | copy-start | bytes 3022852
  81.1 7.8 %collective-permute-start.17 = (bf16[4,48,384]{2,1,0:T(8,128)(2,1)S(1)}, bf16[4,48,384]{2,1,0:T(8,128)(2,1)S(1)}, u32[]{:S(2)}, u32[]{:S(2)}) collective-permute-start(bf16[4,48,384]{2,1,0:T(8,128)(2,1)S(1)} %shard_map.137), channel_id=1, source_target_pairs={{0,1},{1,0},{2,3},{3,2},{4,5},{5,4},{6,7},{7,6},{8,9},{9,8},{10,11... | collective-permute-start | bytes 442376 | tf_op jit(solution)/shard_map/ppermute | solution.py:577
  81.2 11.4 %collective-permute-start.10 = (bf16[2,48,384]{2,1,0:T(8,128)(2,1)S(1)}, bf16[2,48,384]{2,1,0:T(8,128)(2,1)S(1)}, u32[]{:S(2)}, u32[]{:S(2)}) collective-permute-start(bf16[2,48,384]{2,1,0:T(8,128)(2,1)S(1)} %get-tuple-element.46), channel_id=1, source_target_pairs={{0,8},{1,9},{2,10},{3,11},{4,12},{5,13},{6,14},{7,15},{8,0},{9,1},... | collective-permute-start | bytes 221192 | tf_op jit(solution)/shard_map/ppermute | solution.py:577
  81.3 13.2 %collective-permute-start.11 = (bf16[2,48,384]{2,1,0:T(8,128)(2,1)S(1)}, bf16[2,48,384]{2,1,0:T(8,128)(2,1)S(1)}, u32[]{:S(2)}, u32[]{:S(2)}) collective-permute-start(bf16[2,48,384]{2,1,0:T(8,128)(2,1)S(1)} %get-tuple-element.47), channel_id=1, source_target_pairs={{0,10},{1,11},{2,8},{3,9},{4,14},{5,15},{6,12},{7,13},{8,2},{9,3},... | collective-permute-start | bytes 221192 | tf_op jit(solution)/shard_map/ppermute | solution.py:577
  83.7 10.8 %collective-permute-start.12 = (bf16[2,48,384]{2,1,0:T(8,128)(2,1)S(1)}, bf16[2,48,384]{2,1,0:T(8,128)(2,1)S(1)}, u32[]{:S(2)}, u32[]{:S(2)}) collective-permute-start(bf16[2,48,384]{2,1,0:T(8,128)(2,1)S(1)} %get-tuple-element.48), channel_id=1, source_target_pairs={{0,12},{1,13},{2,14},{3,15},{4,8},{5,9},{6,10},{7,11},{8,4},{9,5},... | collective-permute-start | bytes 221192 | tf_op jit(solution)/shard_map/ppermute | solution.py:577
  84.9 9.6 %collective-permute-start.13 = (bf16[2,48,384]{2,1,0:T(8,128)(2,1)S(1)}, bf16[2,48,384]{2,1,0:T(8,128)(2,1)S(1)}, u32[]{:S(2)}, u32[]{:S(2)}) collective-permute-start(bf16[2,48,384]{2,1,0:T(8,128)(2,1)S(1)} %get-tuple-element.49), channel_id=1, source_target_pairs={{0,14},{1,15},{2,12},{3,13},{4,10},{5,11},{6,8},{7,9},{8,6},{9,7},... | collective-permute-start | bytes 221192 | tf_op jit(solution)/shard_map/ppermute | solution.py:577
  94.5 1.4 %collective-permute-start.18 = (bf16[4,48,384]{2,1,0:T(8,128)(2,1)S(1)}, bf16[4,48,384]{2,1,0:T(8,128)(2,1)S(1)}, u32[]{:S(2)}, u32[]{:S(2)}) collective-permute-start(bf16[4,48,384]{2,1,0:T(8,128)(2,1)S(1)} %shard_map.139), channel_id=1, source_target_pairs={{0,1},{1,0},{2,3},{3,2},{4,5},{5,4},{6,7},{7,6},{8,9},{9,8},{10,11... | collective-permute-start | bytes 442376 | tf_op jit(solution)/shard_map/ppermute | solution.py:577
  (4 other events, 2.8 us)

commit v5 on v4

--- a/solution.py
+++ b/solution.py
@@ -377,13 +377,11 @@
 
     lax.fori_loop(0, slots // GROUP, group, 0, unroll=4)
     scatter_ref, embed_ref = scatter(), embed()
-    total = None
+    pixels = []
     for j in range(0, pix, 2):
         cols = slice(j * LANES, (j + 2) * LANES)
-        pixels = mm(scatter_ref[...], c_ref[:, cols])
-        term = mm(pixels.astype(BF16), embed_ref[cols, :])
-        total = term if total is None else total + term
-    return total
+        pixels.append(mm(scatter_ref[...], c_ref[:, cols]).astype(BF16))
+    return mm(jnp.concatenate(pixels, axis=1), embed_ref[...])
 
 
 def early_kernel(pix, direct, loads, outs, scratch):

time: 101 us -> 100 us (0.990)
  Pallas kernels: 29.6 us -> 27.8 us
    pallas_call x14, Pallas kernels: 29.6 us -> 27.8 us  [call(): pl.pallas_call(run, out_shape=list(outs), in_specs=in_specs + [vmem] * le...]
  transfers between devices with their start and end apart: 20 -> 20, of which waited for: 6 -> 6; matrix products, arithmetic and copies ran while one was open for 0% -> 0% of each run, Pallas kernels for 24% -> 23%
where the time goes in v5:
time: 100 us; the launch traced here: 98.9 us
  starting transfers between devices  36.6 us (37%)
  Pallas kernels  27.8 us (28%)
  local copies, waits for them, and re-layouts  17.2 us (17%)
  waiting for transfers between devices  16.9 us (17%)
    pallas_call x14, Pallas kernels, call(): pl.pallas_call(run, out_shape=list(outs), in_specs=in_specs + [vmem] * le...  27.8 us
    ppermute x17, starting transfers between devices, flip(): lax.ppermute(value, axis, [(source, source ^ bits) for source in range(co...  24 us
    unnamed x64, local copies, waits for them, and re-layouts  17.2 us
    ppermute x17, waiting for transfers between devices, flip(): lax.ppermute(value, axis, [(source, source ^ bits) for source in range(co...  11 us
    all_to_all x1, starting transfers between devices, swap(): return lax.all_to_all(value, axis, split_axis=0, concat_axis=0, tiled=True)  8.25 us
    ppermute x2, waiting for transfers between devices, from_behind(): return lax.ppermute(value, axis, pairs)  5.87 us
    ppermute x2, starting transfers between devices, from_behind(): return lax.ppermute(value, axis, pairs)  4.36 us
  transfers between devices with their start and end apart: 20, of which 6 were waited for; matrix products, arithmetic and copies ran while one was open for 0% of the time, Pallas kernels for 23%

profile of v5, /device:TPU:0, one launch (start us, length us, event | category | flops | bytes accessed | tf_op | source)
XLA Modules:
  0.0 98.9 jit_solution(2755954759745752289)
XLA Ops:
  0.0 1.0 %copy-done.26 = bf16[192,1312]{1,0:T(8,128)(2,1)S(1)} copy-done((bf16[192,1312]{1,0:T(8,128)(2,1)S(1)}, bf16[192,1312]{1,0:T(8,128)(2,1)}, u32[]{:S(2)}) %copy-start.26) | copy-done | bytes 503832
  1.1 0.7 copy-done.30
  1.7 0.6 shard_map.127
  2.3 3.1 %collective-permute-start = (bf16[2,24,1312]{2,1,0:T(8,128)(2,1)S(1)}, bf16[2,24,1312]{2,1,0:T(8,128)(2,1)S(1)}, u32[]{:S(2)}, u32[]{:S(2)}) collective-permute-start(bf16[2,24,1312]{2,1,0:T(8,128)(2,1)S(1)} %get-tuple-element.32), channel_id=1, source_target_pairs={{0,2},{1,3},{2,0},{3,1},{4,6},{5,7},{6,4},{7,5},{8,10},{9,11},{10,... | collective-permute-start | bytes 377864 | tf_op jit(solution)/shard_map/ppermute | solution.py:575
  5.4 1.6 %collective-permute-start.1 = (bf16[2,24,1312]{2,1,0:T(8,128)(2,1)S(1)}, bf16[2,24,1312]{2,1,0:T(8,128)(2,1)S(1)}, u32[]{:S(2)}, u32[]{:S(2)}) collective-permute-start(bf16[2,24,1312]{2,1,0:T(8,128)(2,1)S(1)} %get-tuple-element.33), channel_id=1, source_target_pairs={{0,4},{1,5},{2,6},{3,7},{4,0},{5,1},{6,2},{7,3},{8,12},{9,13},{10,... | collective-permute-start | bytes 377864 | tf_op jit(solution)/shard_map/ppermute | solution.py:575
  7.0 3.0 %collective-permute-start.3 = (bf16[2,24,1312]{2,1,0:T(8,128)(2,1)S(1)}, bf16[2,24,1312]{2,1,0:T(8,128)(2,1)S(1)}, u32[]{:S(2)}, u32[]{:S(2)}) collective-permute-start(bf16[2,24,1312]{2,1,0:T(8,128)(2,1)S(1)} %get-tuple-element.35), channel_id=1, source_target_pairs={{0,8},{1,9},{2,10},{3,11},{4,12},{5,13},{6,14},{7,15},{8,0},{9,1},... | collective-permute-start | bytes 377864 | tf_op jit(solution)/shard_map/ppermute | solution.py:575
  9.9 1.3 %collective-permute-start.4 = (bf16[2,24,1312]{2,1,0:T(8,128)(2,1)S(1)}, bf16[2,24,1312]{2,1,0:T(8,128)(2,1)S(1)}, u32[]{:S(2)}, u32[]{:S(2)}) collective-permute-start(bf16[2,24,1312]{2,1,0:T(8,128)(2,1)S(1)} %get-tuple-element.36), channel_id=1, source_target_pairs={{0,10},{1,11},{2,8},{3,9},{4,14},{5,15},{6,12},{7,13},{8,2},{9,3},... | collective-permute-start | bytes 377864 | tf_op jit(solution)/shard_map/ppermute | solution.py:575
  11.2 0.4 shard_map.128.refs_4_
  11.6 0.8 copy-done.24
  12.4 2.4 %shard_map.129 = (bf16[192,192]{1,0:T(8,128)(2,1)S(1)}, bf16[192,576]{1,0:T(8,128)(2,1)S(1)}, bf16[2048,384]{1,0:T(8,128)(2,1)S(1)}, f32[2,64,768]{2,1,0:T(8,128)S(1)}, bf16[768,192]{1,0:T(8,128)(2,1)S(1)}) custom-call(s32[1]{0:T(128)} %bitcast.refs_0_, s32[4,192]{1,0:T(4,128)S(1)} %copy-done.29, bf16[1312,384]{1,0:T(8,128)(2,1)S(1)} %copy-done.24, ...), custom_call_target="tpu_custom_call" | custom-call | flops 2000000000 | bytes 1032288 | tf_op jit(solution)/shard_map/pallas_call | solution.py:74
  14.9 0.7 copy-done.17
  15.6 0.7 copy-done.20
  16.3 1.4 %shard_map.130.refs_4_.refs_12_ = bf16[48,256,128]{2,1,0:T(8,128)(2,1)S(1)} custom-call(s32[1]{0:T(128)} %bitcast.refs_0_, s32[4,192]{1,0:T(4,128)S(1)} %copy-done.29, bf16[192,1024]{1,0:T(8,128)(2,1)S(1)} %copy-done.27, bf16[2048,384]{1,0:T(8,128)(2,1)S(1)} %get-tuple-element.39.refs_3_.refs_6_.refs_14_), custom_call_target="tpu_custom_call" | custom-call | flops 2000000000 | bytes 396288 | tf_op jit(solution)/shard_map/pallas_call | solution.py:74
  17.8 3.7 %collective-permute-start.5 = (bf16[2,24,1312]{2,1,0:T(8,128)(2,1)S(1)}, bf16[2,24,1312]{2,1,0:T(8,128)(2,1)S(1)}, u32[]{:S(2)}, u32[]{:S(2)}) collective-permute-start(bf16[2,24,1312]{2,1,0:T(8,128)(2,1)S(1)} %get-tuple-element.37), channel_id=1, source_target_pairs={{0,12},{1,13},{2,14},{3,15},{4,8},{5,9},{6,10},{7,11},{8,4},{9,5},... | collective-permute-start | bytes 377864 | tf_op jit(solution)/shard_map/ppermute | solution.py:575
  21.5 1.8 %shard_map.131.refs_8_.refs_15_ = f32[192,384]{1,0:T(8,128)S(1)} custom-call(bf16[2,24,1312]{2,1,0:T(8,128)(2,1)S(1)} %get-tuple-element.31.refs_2_.refs_0_, bf16[2,24,1312]{2,1,0:T(8,128)(2,1)S(1)} %collective-permute-done.refs_1_, bf16[2,24,1312]{2,1,0:T(8,128)(2,1)S(1)} %collective-permute-done.1.refs_2_, ...), custom_call_target="tpu_custom_call" | custom-call | flops 2000000000 | bytes 5296128 | tf_op jit(solution)/shard_map/pallas_call | solution.py:74
  23.4 6.5 %collective-permute-done.4.refs_5_.refs_6_ = bf16[2,24,1312]{2,1,0:T(8,128)(2,1)S(1)} collective-permute-done((bf16[2,24,1312]{2,1,0:T(8,128)(2,1)S(1)}, bf16[2,24,1312]{2,1,0:T(8,128)(2,1)S(1)}, u32[]{:S(2)}, u32[]{:S(2)}) %collective-permute-start.4) | collective-permute-done | bytes 125984 | tf_op jit(solution)/shard_map/ppermute | solution.py:575
  29.9 0.9 shard_map.132
  30.8 0.7 copy-done.9
  31.5 8.2 %all-to-all-start = ((bf16[16,48,256]{2,1,0:T(8,128)(2,1)}), bf16[16,48,256]{2,1,0:T(8,128)(2,1)}, u32[]{:S(2)}, u32[]{:S(2)}) async-start(bf16[16,48,256]{2,1,0:T(8,128)(2,1)} %bitcast.5), calls=%async_computation | async-start | bytes 786432 | tf_op jit(solution)/shard_map/all_to_all | solution.py:557
  39.8 1.7 %copy-done.1 = bf16[2,384,1536]{2,1,0:T(8,128)(2,1)S(1)} copy-done((bf16[2,384,1536]{2,1,0:T(8,128)(2,1)S(1)}, bf16[2,384,1536]{2,1,0:T(8,128)(2,1)}, u32[]{:S(2)}) %copy-start.1) | copy-done | bytes 2359320
  41.5 1.7 %copy-done.3 = bf16[2,1536,384]{2,1,0:T(8,128)(2,1)S(1)} copy-done((bf16[2,1536,384]{2,1,0:T(8,128)(2,1)S(1)}, bf16[2,1536,384]{2,1,0:T(8,128)(2,1)}, u32[]{:S(2)}) %copy-start.3) | copy-done | bytes 2359320
  43.2 1.9 %copy-done.5 = bf16[48,256,128]{2,1,0:T(8,128)(2,1)S(1)} copy-done((bf16[48,256,128]{2,1,0:T(8,128)(2,1)S(1)}, bf16[48,256,128]{2,1,0:T(8,128)(2,1)}, u32[]{:S(2)}) %copy-start.5) | copy-done | bytes 3145752
  45.1 1.4 %copy-done.8 = bf16[2048,384]{1,0:T(8,128)(2,1)S(1)} copy-done((bf16[2048,384]{1,0:T(8,128)(2,1)S(1)}, bf16[2048,384]{1,0:T(8,128)(2,1)}, u32[]{:S(2)}) %copy-start.8) | copy-done | bytes 1572888
  46.5 1.0 copy-done.10
  47.4 0.9 copy-done.12
  48.3 0.9 copy-done.14
  49.2 0.9 copy-done.16
  50.2 0.9 copy-done.21
  51.1 6.7 %shard_map.133 = (bf16[96,384]{1,0:T(8,128)(2,1)S(1)}, bf16[96,384]{1,0:T(8,128)(2,1)S(1)}) custom-call(bf16[8,24,1312]{2,1,0:T(8,128)(2,1)S(1)} %collective-permute-done.7.refs_0_.refs_1_.refs_2_.refs_3_.refs_5_.refs_7_.refs_9_.refs_11_, bf16[8,24,1312]{2,1,0:T(8,128)(2,1)S(1)} %collective-permute-done.7.refs_0_.refs_1_.refs_2_.refs_3_.refs_5_.refs_7_.refs_9_.refs_11_, ...), custom_call_target="tpu_custom_call" | custom-call | flops 4000000000 | bytes 17246208 | tf_op jit(solution)/shard_map/pallas_call | solution.py:74
  57.8 4.4 %collective-permute-start.9 = (bf16[96,384]{1,0:T(8,128)(2,1)S(1)}, bf16[96,384]{1,0:T(8,128)(2,1)S(1)}, u32[]{:S(2)}, u32[]{:S(2)}) collective-permute-start(bf16[96,384]{1,0:T(8,128)(2,1)S(1)} %get-tuple-element.43.refs_0_.refs_1_), channel_id=1, source_target_pairs={{0,15},{1,0},{2,1},{3,2},{4,3},{5,4},{6,5},{7,6},{8,7},{9,8},{10,9... | collective-permute-start | bytes 221192 | tf_op jit(solution)/shard_map/ppermute | solution.py:581
  62.2 0.6 shard_map.134.refs_0_
  62.8 1.4 %collective-permute-done.9.refs_8_ = bf16[96,384]{1,0:T(8,128)(2,1)S(1)} collective-permute-done((bf16[96,384]{1,0:T(8,128)(2,1)S(1)}, bf16[96,384]{1,0:T(8,128)(2,1)S(1)}, u32[]{:S(2)}, u32[]{:S(2)}) %collective-permute-start.9) | collective-permute-done | bytes 73760 | tf_op jit(solution)/shard_map/ppermute | solution.py:581
  64.2 4.5 %collective-permute-done.8.refs_7_ = bf16[96,384]{1,0:T(8,128)(2,1)S(1)} collective-permute-done((bf16[96,384]{1,0:T(8,128)(2,1)S(1)}, bf16[96,384]{1,0:T(8,128)(2,1)S(1)}, u32[]{:S(2)}, u32[]{:S(2)}) %collective-permute-start.8) | collective-permute-done | bytes 73760 | tf_op jit(solution)/shard_map/ppermute | solution.py:581
  68.7 3.8 %shard_map.135 = (bf16[2,48,384]{2,1,0:T(8,128)(2,1)S(1)}, bf16[2,48,384]{2,1,0:T(8,128)(2,1)S(1)}, bf16[2,48,384]{2,1,0:T(8,128)(2,1)S(1)}, bf16[2,48,384]{2,1,...) custom-call(bf16[192,1152]{1,0:T(8,128)(2,1)S(1)} %shard_map.134.ref, ...), custom_call_target="tpu_custom_call" | custom-call | flops 2000000000 | bytes 8509440 | tf_op jit(solution)/shard_map/pallas_call | solution.py:74
  72.4 0.1 collective-permute-start.14
  72.5 0.1 collective-permute-start.15
  72.6 3.4 %collective-permute-start.16 = (bf16[2,48,384]{2,1,0:T(8,128)(2,1)S(1)}, bf16[2,48,384]{2,1,0:T(8,128)(2,1)S(1)}, u32[]{:S(2)}, u32[]{:S(2)}) collective-permute-start(bf16[2,48,384]{2,1,0:T(8,128)(2,1)S(1)} %get-tuple-element.53), channel_id=1, source_target_pairs={{0,6},{1,7},{2,4},{3,5},{4,2},{5,3},{6,0},{7,1},{8,14},{9,15},{10,... | collective-permute-start | bytes 221192 | tf_op jit(solution)/shard_map/ppermute | solution.py:575
  76.0 1.2 %copy-done.25 = bf16[384,1312]{0,1:T(8,128)(2,1)S(1)} copy-done((bf16[384,1312]{0,1:T(8,128)(2,1)S(1)}, bf16[384,1312]{0,1:T(8,128)(2,1)}, u32[]{:S(2)}) %copy-start.25) | copy-done | bytes 1007640
  77.2 2.8 %shard_map.136 = (bf16[48,128,256]{2,1,0:T(8,128)(2,1)S(1)}, bf16[2048,384]{1,0:T(8,128)(2,1)S(1)}, s32[8,384]{1,0:T(8,128)S(1)}) custom-call(s32[1]{0:T(128)} %bitcast.refs_0_, bf16[768,256]{1,0:T(8,128)(2,1)} %bitcast.3.refs_1_, bf16[1312,384]{1,0:T(8,128)(2,1)S(1)} %bitcast.6, s32[1,384]{1,0:T(1,128)S(1)} %copy-done.31, ...), custom_call_target="tpu_custom_call" | custom-call | flops 2000000000 | bytes 1402368 | tf_op jit(solution)/shard_map/pallas_call | solution.py:74
  80.0 0.1 collective-permute-start.17
  80.2 2.4 %collective-permute-start.11 = (bf16[2,48,384]{2,1,0:T(8,128)(2,1)S(1)}, bf16[2,48,384]{2,1,0:T(8,128)(2,1)S(1)}, u32[]{:S(2)}, u32[]{:S(2)}) collective-permute-start(bf16[2,48,384]{2,1,0:T(8,128)(2,1)S(1)} %get-tuple-element.47), channel_id=1, source_target_pairs={{0,10},{1,11},{2,8},{3,9},{4,14},{5,15},{6,12},{7,13},{8,2},{9,3},... | collective-permute-start | bytes 221192 | tf_op jit(solution)/shard_map/ppermute | solution.py:575
  82.6 1.2 %collective-permute-start.12 = (bf16[2,48,384]{2,1,0:T(8,128)(2,1)S(1)}, bf16[2,48,384]{2,1,0:T(8,128)(2,1)S(1)}, u32[]{:S(2)}, u32[]{:S(2)}) collective-permute-start(bf16[2,48,384]{2,1,0:T(8,128)(2,1)S(1)} %get-tuple-element.48), channel_id=1, source_target_pairs={{0,12},{1,13},{2,14},{3,15},{4,8},{5,9},{6,10},{7,11},{8,4},{9,5},... | collective-permute-start | bytes 221192 | tf_op jit(solution)/shard_map/ppermute | solution.py:575
  83.8 4.0 %collective-permute-start.13 = (bf16[2,48,384]{2,1,0:T(8,128)(2,1)S(1)}, bf16[2,48,384]{2,1,0:T(8,128)(2,1)S(1)}, u32[]{:S(2)}, u32[]{:S(2)}) collective-permute-start(bf16[2,48,384]{2,1,0:T(8,128)(2,1)S(1)} %get-tuple-element.49), channel_id=1, source_target_pairs={{0,14},{1,15},{2,12},{3,13},{4,10},{5,11},{6,8},{7,9},{8,6},{9,7},... | collective-permute-start | bytes 221192 | tf_op jit(solution)/shard_map/ppermute | solution.py:575
  87.8 2.4 %shard_map.138.refs_4_.refs_11_ = bf16[192,2048]{1,0:T(8,128)(2,1)S(1)} custom-call(s32[1]{0:T(128)} %bitcast.refs_0_, bf16[2,48,384]{2,1,0:T(8,128)(2,1)S(1)} %get-tuple-element.50.refs_4_.refs_0_.refs_1_, bf16[4,48,384]{2,1,0:T(8,128)(2,1)S(1)} %collective-permute-done.17.refs_2_.refs_4_.refs_6_.refs_8_, ...), custom_call_target="tpu_custom_call" | custom-call | flops 2000000000 | bytes 5603328 | tf_op jit(solution)/shard_map/pallas_call | solution.py:74
  90.3 1.2 %collective-permute-done.10.refs_0_.refs_1_ = bf16[2,48,384]{2,1,0:T(8,128)(2,1)S(1)} collective-permute-done((bf16[2,48,384]{2,1,0:T(8,128)(2,1)S(1)}, bf16[2,48,384]{2,1,0:T(8,128)(2,1)S(1)}, u32[]{:S(2)}, u32[]{:S(2)}) %collective-permute-start.10) | collective-permute-done | bytes 73760 | tf_op jit(solution)/shard_map/ppermute | solution.py:575
  91.5 1.9 %collective-permute-done.11.refs_1_.refs_3_ = bf16[2,48,384]{2,1,0:T(8,128)(2,1)S(1)} collective-permute-done((bf16[2,48,384]{2,1,0:T(8,128)(2,1)S(1)}, bf16[2,48,384]{2,1,0:T(8,128)(2,1)S(1)}, u32[]{:S(2)}, u32[]{:S(2)}) %collective-permute-start.11) | collective-permute-done | bytes 73760 | tf_op jit(solution)/shard_map/ppermute | solution.py:575
  93.5 1.4 %collective-permute-done.18.refs_2_.refs_4_.refs_6_.refs_8_ = bf16[4,48,384]{2,1,0:T(8,128)(2,1)S(1)} collective-permute-done((bf16[4,48,384]{2,1,0:T(8,128)(2,1)S(1)}, bf16[4,48,384]{2,1,0:T(8,128)(2,1)S(1)}, u32[]{:S(2)}, u32[]{:S(2)}) %collective-permute-start.18) | collective-permute-done | bytes 147488 | tf_op jit(solution)/shard_map/ppermute | solution.py:575
  94.9 4.0 %shard_map.140 = f32[192,1312]{1,0:T(8,128)} custom-call(s32[1]{0:T(128)} %bitcast.refs_0_, bf16[2,48,384]{2,1,0:T(8,128)(2,1)S(1)} %collective-permute-done.10.refs_0_.refs_1_, bf16[4,48,384]{2,1,0:T(8,128)(2,1)S(1)} %collective-permute-done.18.refs_2_.refs_4_.refs_6_.refs_8_, bf16[2,48,384]{2,1,0:T(8,128)(2,1)S(1)} %collective-permute-done.11.refs_1_.refs_3_, ...), custom_call_target="tpu_custom_call" | custom-call | flops 3000000000 | bytes 6402048 | tf_op jit(solution)/shard_map/pallas_call | solution.py:74
  (70 shorter events, 0.3 us)
Async XLA Ops:
  0.0 1.0 %copy-start.26 = (bf16[192,1312]{1,0:T(8,128)(2,1)S(1)}, bf16[192,1312]{1,0:T(8,128)(2,1)}, u32[]{:S(2)}) copy-start(bf16[192,1312]{1,0:T(8,128)(2,1)} %refs_2_.4) | copy-start | bytes 1511428
  1.7 9.5 %copy-start.27 = (bf16[192,1024]{1,0:T(8,128)(2,1)S(1)}, bf16[192,1024]{1,0:T(8,128)(2,1)}, u32[]{:S(2)}) copy-start(bf16[192,1024]{1,0:T(8,128)(2,1)} %refs_2_.6) | copy-start | bytes 1179652
  1.7 9.5 %copy-start.29 = (s32[4,192]{1,0:T(4,128)S(1)}, s32[4,192]{1,0:T(4,128)}, u32[]{:S(2)}) copy-start(s32[4,192]{1,0:T(4,128)} %refs_1_.7) | copy-start | bytes 9220
  2.3 15.5 %collective-permute-start = (bf16[2,24,1312]{2,1,0:T(8,128)(2,1)S(1)}, bf16[2,24,1312]{2,1,0:T(8,128)(2,1)S(1)}, u32[]{:S(2)}, u32[]{:S(2)}) collective-permute-start(bf16[2,24,1312]{2,1,0:T(8,128)(2,1)S(1)} %get-tuple-element.32), channel_id=1, source_target_pairs={{0,2},{1,3},{2,0},{3,1},{4,6},{5,7},{6,4},{7,5},{8,10},{9,11},{10,... | collective-permute-start | bytes 377864 | tf_op jit(solution)/shard_map/ppermute | solution.py:575
  5.4 16.1 %collective-permute-start.1 = (bf16[2,24,1312]{2,1,0:T(8,128)(2,1)S(1)}, bf16[2,24,1312]{2,1,0:T(8,128)(2,1)S(1)}, u32[]{:S(2)}, u32[]{:S(2)}) collective-permute-start(bf16[2,24,1312]{2,1,0:T(8,128)(2,1)S(1)} %get-tuple-element.33), channel_id=1, source_target_pairs={{0,4},{1,5},{2,6},{3,7},{4,0},{5,1},{6,2},{7,3},{8,12},{9,13},{10,... | collective-permute-start | bytes 377864 | tf_op jit(solution)/shard_map/ppermute | solution.py:575
  7.0 14.5 %collective-permute-start.2 = (bf16[2,24,1312]{2,1,0:T(8,128)(2,1)S(1)}, bf16[2,24,1312]{2,1,0:T(8,128)(2,1)S(1)}, u32[]{:S(2)}, u32[]{:S(2)}) collective-permute-start(bf16[2,24,1312]{2,1,0:T(8,128)(2,1)S(1)} %get-tuple-element.34), channel_id=1, source_target_pairs={{0,6},{1,7},{2,4},{3,5},{4,2},{5,3},{6,0},{7,1},{8,14},{9,15},{10,... | collective-permute-start | bytes 377864 | tf_op jit(solution)/shard_map/ppermute | solution.py:575
  7.0 16.4 %collective-permute-start.3 = (bf16[2,24,1312]{2,1,0:T(8,128)(2,1)S(1)}, bf16[2,24,1312]{2,1,0:T(8,128)(2,1)S(1)}, u32[]{:S(2)}, u32[]{:S(2)}) collective-permute-start(bf16[2,24,1312]{2,1,0:T(8,128)(2,1)S(1)} %get-tuple-element.35), channel_id=1, source_target_pairs={{0,8},{1,9},{2,10},{3,11},{4,12},{5,13},{6,14},{7,15},{8,0},{9,1},... | collective-permute-start | bytes 377864 | tf_op jit(solution)/shard_map/ppermute | solution.py:575
  9.9 19.9 %collective-permute-start.4 = (bf16[2,24,1312]{2,1,0:T(8,128)(2,1)S(1)}, bf16[2,24,1312]{2,1,0:T(8,128)(2,1)S(1)}, u32[]{:S(2)}, u32[]{:S(2)}) collective-permute-start(bf16[2,24,1312]{2,1,0:T(8,128)(2,1)S(1)} %get-tuple-element.36), channel_id=1, source_target_pairs={{0,10},{1,11},{2,8},{3,9},{4,14},{5,15},{6,12},{7,13},{8,2},{9,3},... | collective-permute-start | bytes 377864 | tf_op jit(solution)/shard_map/ppermute | solution.py:575
  11.2 1.2 %copy-start.24 = (bf16[1312,384]{1,0:T(8,128)(2,1)S(1)}, bf16[1312,384]{1,0:T(8,128)(2,1)}, u32[]{:S(2)}) copy-start(bf16[1312,384]{1,0:T(8,128)(2,1)} %refs_2_.5) | copy-start | bytes 3022852
  11.2 1.2 %copy-start.28 = (f32[2,12,225]{2,0,1:T(2,128)S(1)}, f32[2,12,225]{2,0,1:T(2,128)}, u32[]{:S(2)}) copy-start(f32[2,12,225]{2,0,1:T(2,128)} %param.20) | copy-start | bytes 64804
  11.6 3.3 %copy-start.19 = (bf16[768,256]{1,0:T(8,128)(2,1)}, bf16[768,256]{1,0:T(8,128)(2,1)S(1)}, u32[]{:S(2)}) copy-start(bf16[768,256]{1,0:T(8,128)(2,1)S(1)} %shard_map.128.refs_4_) | copy-start | bytes 1179652
  16.3 5.2 %copy-start.7 = (bf16[2048,384]{1,0:T(8,128)(2,1)}, bf16[2048,384]{1,0:T(8,128)(2,1)S(1)}, u32[]{:S(2)}) copy-start(bf16[2048,384]{1,0:T(8,128)(2,1)S(1)} %get-tuple-element.39.refs_3_.refs_6_.refs_14_) | copy-start | bytes 4718596
  17.8 5.6 %copy-start.4 = (bf16[48,256,128]{2,1,0:T(8,128)(2,1)}, bf16[48,256,128]{2,1,0:T(8,128)(2,1)S(1)}, u32[]{:S(2)}) copy-start(bf16[48,256,128]{2,1,0:T(8,128)(2,1)S(1)} %shard_map.130.refs_4_.refs_12_) | copy-start | bytes 9437188
  17.8 12.1 %collective-permute-start.5 = (bf16[2,24,1312]{2,1,0:T(8,128)(2,1)S(1)}, bf16[2,24,1312]{2,1,0:T(8,128)(2,1)S(1)}, u32[]{:S(2)}, u32[]{:S(2)}) collective-permute-start(bf16[2,24,1312]{2,1,0:T(8,128)(2,1)S(1)} %get-tuple-element.37), channel_id=1, source_target_pairs={{0,12},{1,13},{2,14},{3,15},{4,8},{5,9},{6,10},{7,11},{8,4},{9,5},... | collective-permute-start | bytes 377864 | tf_op jit(solution)/shard_map/ppermute | solution.py:575
  21.5 8.4 %collective-permute-start.6 = (bf16[2,24,1312]{2,1,0:T(8,128)(2,1)S(1)}, bf16[2,24,1312]{2,1,0:T(8,128)(2,1)S(1)}, u32[]{:S(2)}, u32[]{:S(2)}) collective-permute-start(bf16[2,24,1312]{2,1,0:T(8,128)(2,1)S(1)} %get-tuple-element.38), channel_id=1, source_target_pairs={{0,14},{1,15},{2,12},{3,13},{4,10},{5,11},{6,8},{7,9},{8,6},{9,7},... | collective-permute-start | bytes 377864 | tf_op jit(solution)/shard_map/ppermute | solution.py:575
  23.3 16.5 %copy-start = (bf16[2,384,1152]{2,1,0:T(8,128)(2,1)S(1)}, bf16[2,384,1152]{2,1,0:T(8,128)(2,1)}, u32[]{:S(2)}) copy-start(bf16[2,384,1152]{2,1,0:T(8,128)(2,1)} %refs_5_.1) | copy-start | bytes 5308420
  23.4 16.4 %copy-start.6 = (bf16[2,384,384]{2,1,0:T(8,128)(2,1)S(1)}, bf16[2,384,384]{2,1,0:T(8,128)(2,1)}, u32[]{:S(2)}) copy-start(bf16[2,384,384]{2,1,0:T(8,128)(2,1)} %refs_9_.1) | copy-start | bytes 1769476
  23.4 16.4 %copy-start.22 = (f32[2,384]{1,0:T(2,128)S(1)}, f32[2,384]{1,0:T(2,128)}, u32[]{:S(2)}) copy-start(f32[2,384]{1,0:T(2,128)} %refs_3_.4) | copy-start | bytes 9220
  23.4 16.4 %copy-start.23 = (f32[2,384]{1,0:T(2,128)S(1)}, f32[2,384]{1,0:T(2,128)}, u32[]{:S(2)}) copy-start(f32[2,384]{1,0:T(2,128)} %refs_4_.1) | copy-start | bytes 9220
  29.9 0.9 copy-start.11
  29.9 1.7 %copy-start.13 = (bf16[2,24,1312]{2,1,0:T(8,128)(2,1)}, bf16[2,24,1312]{2,1,0:T(8,128)(2,1)S(1)}, u32[]{:S(2)}) copy-start(bf16[2,24,1312]{2,1,0:T(8,128)(2,1)S(1)} %collective-permute-done.5.refs_6_.refs_8_) | copy-start | bytes 377860
  29.9 1.6 %copy-start.15 = (bf16[2,24,1312]{2,1,0:T(8,128)(2,1)}, bf16[2,24,1312]{2,1,0:T(8,128)(2,1)S(1)}, u32[]{:S(2)}) copy-start(bf16[2,24,1312]{2,1,0:T(8,128)(2,1)S(1)} %collective-permute-done.6.refs_7_.refs_10_) | copy-start | bytes 377860
  31.5 8.3 %collective-permute-start.7 = (bf16[8,24,1312]{2,1,0:T(8,128)(2,1)}, bf16[8,24,1312]{2,1,0:T(8,128)(2,1)S(1)}, u32[]{:S(2)}, u32[]{:S(2)}) collective-permute-start(bf16[8,24,1312]{2,1,0:T(8,128)(2,1)} %shard_map.132), channel_id=1, source_target_pairs={{0,1},{1,0},{2,3},{3,2},{4,5},{5,4},{6,7},{7,6},{8,9},{9,8},{10,11... | collective-permute-start | bytes 1511432 | tf_op jit(solution)/shard_map/ppermute | solution.py:575
  31.5 44.5 %all-to-all-start = ((bf16[16,48,256]{2,1,0:T(8,128)(2,1)}), bf16[16,48,256]{2,1,0:T(8,128)(2,1)}, u32[]{:S(2)}, u32[]{:S(2)}) async-start(bf16[16,48,256]{2,1,0:T(8,128)(2,1)} %bitcast.5), calls=%async_computation | async-start | bytes 786432 | tf_op jit(solution)/shard_map/all_to_all | solution.py:557
  39.8 1.7 %copy-start.1 = (bf16[2,384,1536]{2,1,0:T(8,128)(2,1)S(1)}, bf16[2,384,1536]{2,1,0:T(8,128)(2,1)}, u32[]{:S(2)}) copy-start(bf16[2,384,1536]{2,1,0:T(8,128)(2,1)} %refs_10_.1) | copy-start | bytes 7077892
  41.5 1.7 %copy-start.3 = (bf16[2,1536,384]{2,1,0:T(8,128)(2,1)S(1)}, bf16[2,1536,384]{2,1,0:T(8,128)(2,1)}, u32[]{:S(2)}) copy-start(bf16[2,1536,384]{2,1,0:T(8,128)(2,1)} %refs_11_.1) | copy-start | bytes 7077892
  43.2 1.9 %copy-start.5 = (bf16[48,256,128]{2,1,0:T(8,128)(2,1)S(1)}, bf16[48,256,128]{2,1,0:T(8,128)(2,1)}, u32[]{:S(2)}) copy-start(bf16[48,256,128]{2,1,0:T(8,128)(2,1)} %copy-done.4) | copy-start | bytes 9437188
  45.1 1.4 %copy-start.8 = (bf16[2048,384]{1,0:T(8,128)(2,1)S(1)}, bf16[2048,384]{1,0:T(8,128)(2,1)}, u32[]{:S(2)}) copy-start(bf16[2048,384]{1,0:T(8,128)(2,1)} %copy-done.7) | copy-start | bytes 4718596
  46.5 1.0 copy-start.10
  47.4 0.9 copy-start.12
  48.3 0.9 copy-start.14
  49.2 0.9 copy-start.16
  50.2 0.9 copy-start.21
  51.1 17.6 %copy-start.18 = (bf16[768,192]{1,0:T(8,128)(2,1)S(1)}, bf16[768,192]{1,0:T(8,128)(2,1)}, u32[]{:S(2)}) copy-start(bf16[768,192]{1,0:T(8,128)(2,1)} %copy-done.17) | copy-start | bytes 884740
  57.8 10.9 %copy-start.2 = (bf16[2,384,1536]{2,1,0:T(8,128)(2,1)S(1)}, bf16[2,384,1536]{2,1,0:T(8,128)(2,1)}, u32[]{:S(2)}) copy-start(bf16[2,384,1536]{2,1,0:T(8,128)(2,1)} %refs_10_.1) | copy-start | bytes 7077892
  57.8 6.3 %collective-permute-start.9 = (bf16[96,384]{1,0:T(8,128)(2,1)S(1)}, bf16[96,384]{1,0:T(8,128)(2,1)S(1)}, u32[]{:S(2)}, u32[]{:S(2)}) collective-permute-start(bf16[96,384]{1,0:T(8,128)(2,1)S(1)} %get-tuple-element.43.refs_0_.refs_1_), channel_id=1, source_target_pairs={{0,15},{1,0},{2,1},{3,2},{4,3},{5,4},{6,5},{7,6},{8,7},{9,8},{10,9... | collective-permute-start | bytes 221192 | tf_op jit(solution)/shard_map/ppermute | solution.py:581
  62.2 6.5 %collective-permute-start.8 = (bf16[96,384]{1,0:T(8,128)(2,1)S(1)}, bf16[96,384]{1,0:T(8,128)(2,1)S(1)}, u32[]{:S(2)}, u32[]{:S(2)}) collective-permute-start(bf16[96,384]{1,0:T(8,128)(2,1)S(1)} %get-tuple-element.44.refs_1_.refs_2_), channel_id=1, source_target_pairs={{0,1},{1,2},{2,3},{3,4},{4,5},{5,6},{6,7},{7,8},{8,9},{9,10},{10,1... | collective-permute-start | bytes 221192 | tf_op jit(solution)/shard_map/ppermute | solution.py:581
  68.7 7.3 %copy-start.31 = (s32[1,384]{1,0:T(1,128)S(1)}, s32[1,384]{1,0:T(1,128)}, u32[]{:S(2)}) copy-start(s32[1,384]{1,0:T(1,128)} %refs_3_.5) | copy-start | bytes 4612
  72.4 7.6 %collective-permute-start.14 = (bf16[2,48,384]{2,1,0:T(8,128)(2,1)S(1)}, bf16[2,48,384]{2,1,0:T(8,128)(2,1)S(1)}, u32[]{:S(2)}, u32[]{:S(2)}) collective-permute-start(bf16[2,48,384]{2,1,0:T(8,128)(2,1)S(1)} %get-tuple-element.51), channel_id=1, source_target_pairs={{0,2},{1,3},{2,0},{3,1},{4,6},{5,7},{6,4},{7,5},{8,10},{9,11},{10,... | collective-permute-start | bytes 221192 | tf_op jit(solution)/shard_map/ppermute | solution.py:575
  72.5 7.5 %collective-permute-start.15 = (bf16[2,48,384]{2,1,0:T(8,128)(2,1)S(1)}, bf16[2,48,384]{2,1,0:T(8,128)(2,1)S(1)}, u32[]{:S(2)}, u32[]{:S(2)}) collective-permute-start(bf16[2,48,384]{2,1,0:T(8,128)(2,1)S(1)} %get-tuple-element.52), channel_id=1, source_target_pairs={{0,4},{1,5},{2,6},{3,7},{4,0},{5,1},{6,2},{7,3},{8,12},{9,13},{10,... | collective-permute-start | bytes 221192 | tf_op jit(solution)/shard_map/ppermute | solution.py:575
  72.6 7.4 %collective-permute-start.16 = (bf16[2,48,384]{2,1,0:T(8,128)(2,1)S(1)}, bf16[2,48,384]{2,1,0:T(8,128)(2,1)S(1)}, u32[]{:S(2)}, u32[]{:S(2)}) collective-permute-start(bf16[2,48,384]{2,1,0:T(8,128)(2,1)S(1)} %get-tuple-element.53), channel_id=1, source_target_pairs={{0,6},{1,7},{2,4},{3,5},{4,2},{5,3},{6,0},{7,1},{8,14},{9,15},{10,... | collective-permute-start | bytes 221192 | tf_op jit(solution)/shard_map/ppermute | solution.py:575
  76.0 1.2 %copy-start.25 = (bf16[384,1312]{0,1:T(8,128)(2,1)S(1)}, bf16[384,1312]{0,1:T(8,128)(2,1)}, u32[]{:S(2)}) copy-start(bf16[384,1312]{0,1:T(8,128)(2,1)} %param.25) | copy-start | bytes 3022852
  80.0 7.8 %collective-permute-start.17 = (bf16[4,48,384]{2,1,0:T(8,128)(2,1)S(1)}, bf16[4,48,384]{2,1,0:T(8,128)(2,1)S(1)}, u32[]{:S(2)}, u32[]{:S(2)}) collective-permute-start(bf16[4,48,384]{2,1,0:T(8,128)(2,1)S(1)} %shard_map.137), channel_id=1, source_target_pairs={{0,1},{1,0},{2,3},{3,2},{4,5},{5,4},{6,7},{7,6},{8,9},{9,8},{10,11... | collective-permute-start | bytes 442376 | tf_op jit(solution)/shard_map/ppermute | solution.py:575
  80.1 11.4 %collective-permute-start.10 = (bf16[2,48,384]{2,1,0:T(8,128)(2,1)S(1)}, bf16[2,48,384]{2,1,0:T(8,128)(2,1)S(1)}, u32[]{:S(2)}, u32[]{:S(2)}) collective-permute-start(bf16[2,48,384]{2,1,0:T(8,128)(2,1)S(1)} %get-tuple-element.46), channel_id=1, source_target_pairs={{0,8},{1,9},{2,10},{3,11},{4,12},{5,13},{6,14},{7,15},{8,0},{9,1},... | collective-permute-start | bytes 221192 | tf_op jit(solution)/shard_map/ppermute | solution.py:575
  80.2 13.2 %collective-permute-start.11 = (bf16[2,48,384]{2,1,0:T(8,128)(2,1)S(1)}, bf16[2,48,384]{2,1,0:T(8,128)(2,1)S(1)}, u32[]{:S(2)}, u32[]{:S(2)}) collective-permute-start(bf16[2,48,384]{2,1,0:T(8,128)(2,1)S(1)} %get-tuple-element.47), channel_id=1, source_target_pairs={{0,10},{1,11},{2,8},{3,9},{4,14},{5,15},{6,12},{7,13},{8,2},{9,3},... | collective-permute-start | bytes 221192 | tf_op jit(solution)/shard_map/ppermute | solution.py:575
  82.6 10.8 %collective-permute-start.12 = (bf16[2,48,384]{2,1,0:T(8,128)(2,1)S(1)}, bf16[2,48,384]{2,1,0:T(8,128)(2,1)S(1)}, u32[]{:S(2)}, u32[]{:S(2)}) collective-permute-start(bf16[2,48,384]{2,1,0:T(8,128)(2,1)S(1)} %get-tuple-element.48), channel_id=1, source_target_pairs={{0,12},{1,13},{2,14},{3,15},{4,8},{5,9},{6,10},{7,11},{8,4},{9,5},... | collective-permute-start | bytes 221192 | tf_op jit(solution)/shard_map/ppermute | solution.py:575
  83.8 9.6 %collective-permute-start.13 = (bf16[2,48,384]{2,1,0:T(8,128)(2,1)S(1)}, bf16[2,48,384]{2,1,0:T(8,128)(2,1)S(1)}, u32[]{:S(2)}, u32[]{:S(2)}) collective-permute-start(bf16[2,48,384]{2,1,0:T(8,128)(2,1)S(1)} %get-tuple-element.49), channel_id=1, source_target_pairs={{0,14},{1,15},{2,12},{3,13},{4,10},{5,11},{6,8},{7,9},{8,6},{9,7},... | collective-permute-start | bytes 221192 | tf_op jit(solution)/shard_map/ppermute | solution.py:575
  93.5 1.4 %collective-permute-start.18 = (bf16[4,48,384]{2,1,0:T(8,128)(2,1)S(1)}, bf16[4,48,384]{2,1,0:T(8,128)(2,1)S(1)}, u32[]{:S(2)}, u32[]{:S(2)}) collective-permute-start(bf16[4,48,384]{2,1,0:T(8,128)(2,1)S(1)} %shard_map.139), channel_id=1, source_target_pairs={{0,1},{1,0},{2,3},{3,2},{4,5},{5,4},{6,7},{7,6},{8,9},{9,8},{10,11... | collective-permute-start | bytes 442376 | tf_op jit(solution)/shard_map/ppermute | solution.py:575
  (4 other events, 2.8 us)

commit v6 on v5

--- a/solution.py
+++ b/solution.py
@@ -270,6 +270,15 @@
             down = pltpu.roll(owner, gap, 1)
             swapped = jnp.where((chunk >> bit) & 1 == 0, up, down)
             owner = jnp.where((me_ref[0] >> bit) & 1 == 1, swapped, owner)
+        r, c = iota((owner.shape[1], owner.shape[1]), 0), iota((owner.shape[1], owner.shape[1]), 1)
+        chunk = over(c, cap)
+        late = chunk - 2 * NEAR
+        late = 2 * NEAR + jnp.where(late < NEAR, 2 * late, 2 * late - 2 * NEAR + 1)
+        source = jnp.where(chunk < 2 * NEAR, chunk, late) * cap + c - chunk * cap
+        move = (r == source).astype(F32).astype(BF16)
+        low = owner % (2 * LANES // 4)
+        owner = [mm(v.astype(F32).astype(BF16), move) for v in (owner - low, low)]
+        owner = (owner[0] + owner[1]).astype(jnp.int32)
     owner_ref[...] = owner
     rows, pixsq = weight_ref.shape
     pix = int(round(pixsq**0.5))
@@ -375,7 +384,7 @@
             c_ref[to, i * LANES : (i + 1) * LANES] = both
         return carry
 
-    lax.fori_loop(0, slots // GROUP, group, 0, unroll=4)
+    lax.fori_loop(0, slots // GROUP, group, 0, unroll=12)
     scatter_ref, embed_ref = scatter(), embed()
     pixels = []
     for j in range(0, pix, 2):
@@ -491,6 +500,10 @@
         outs[x // 2][x % 2] = sent[x * rows : (x + 1) * rows]
 
 
+def return_chunk(stage, i):
+    return i if stage == 0 else 2 * NEAR + 2 * i + stage - 1
+
+
 def back_part(size, first, me_ref, chunks, mix, unembed, p_ref, slot_ref):
     rows = jnp.concatenate([one()[...].reshape(-1, one.ref.shape[-1]) for one in chunks], axis=0)
     unembed_ref = unembed()
@@ -505,15 +518,15 @@
         data = jnp.concatenate([lay_tiles(got[:GROUP], pix), lay_tiles(got[GROUP:], pix)], axis=0)
         where = first + g
         if size is not None:
-            chunk = lax.div(where, size)
-            where = (chunk ^ me_ref[0]) * size + where - chunk * size
+            chunk = lax.div(g, size)
+            where = (return_chunk(first, chunk) ^ me_ref[0]) * size + g - chunk * size
         out = mm(mix_ref[where], data.astype(BF16))
         to = pl.ds(pl.multiple_of(g * GROUP, GROUP), GROUP)
         for i in range(pix):
             slot_ref[to, i * LANES : (i + 1) * LANES] = out[i * GROUP : (i + 1) * GROUP]
         return carry
 
-    lax.fori_loop(0, rows.shape[0] // (2 * GROUP), group, 0, unroll=4)
+    lax.fori_loop(0, rows.shape[0] // (2 * GROUP), group, 0, unroll=12)
 
 
 def back_kernel(size, first, me_ref, loads, outs, scratch):
@@ -524,6 +537,8 @@
 
 def last_kernel(size, first, me_ref, loads, outs, scratch):
     *chunks, unembed, mix, prior, send = loads
+    if size is not None:
+        *chunks, own_far = chunks
     back_part(size, first, me_ref, chunks, mix, unembed, *scratch)
     slot_ref, out_ref = scratch[1], outs[0]
     pix = unembed.ref.shape[0] // LANES
@@ -535,7 +550,8 @@
     tiles = [None] * (-(-total // LANES))
     for j in range(0, pix, 2):
         cols = slice(j * LANES, (j + 2) * LANES)
-        slots = jnp.concatenate([prior_ref[:, cols], slot_ref[:, cols].astype(BF16)], axis=0)
+        slots = [prior_ref[:, cols]] + ([own_far()[:, cols]] if size is not None else [])
+        slots = jnp.concatenate([*slots, slot_ref[:, cols].astype(BF16)], axis=0)
         both = mm(onehot, slots)
         for jj in (j, j + 1):
             val = both[:, (jj - j) * LANES : (jj - j + 1) * LANES]
@@ -694,9 +710,15 @@
     prior = call(functools.partial(back_kernel, size, 0), [*near, In(unembed_pad), In(mix_back)],
                  [sds((per, wide), BF16)], back_scratch, my, flops=2e9)
     if direct:
-        far_pass = flip(relay(got[NEAR:], [prior]), "tile", 1)
-        far = [y for i, x in enumerate(got[NEAR:]) for y in (at(x, 0), at(far_pass, i))]
-    return call(functools.partial(last_kernel, size, groups), [*far, In(unembed_pad), In(mix_back), In(prior), In(owner)],
+        far_all = relay(got[NEAR:], [prior])
+        far_pass = flip(far_all, "tile", 1)
+        own_far = call(functools.partial(back_kernel, size, 1), [*[at(x, 0) for x in got[NEAR:]], In(unembed_pad), In(mix_back)],
+                       [sds((per // 2, wide), BF16)], [vm((per, wide), F32), vm((per // 2, wide), F32)], my, flops=1e9, after=[far_all])
+        far = [at(far_pass, i) for i in range(NEAR)]
+    if direct:
+        back_scratch = [vm((per, wide), F32), vm((per // 2, wide), F32)]
+        far.append(In(own_far))
+    return call(functools.partial(last_kernel, size, 2 if direct else groups), [*far, In(unembed_pad), In(mix_back), In(prior), In(owner)],
                 [sds((pd, width), F32)], back_scratch, my, flops=3e9)
 
 

time: 100 us -> 98.2 us (0.982)
  Pallas kernels: 27.8 us -> 25.8 us
    pallas_call x14 -> x15, Pallas kernels: 27.8 us -> 25.8 us  [call(): pl.pallas_call(run, out_shape=list(outs), in_specs=in_specs + [vmem] * le...]
  transfers between devices with their start and end apart: 20 -> 20, of which waited for: 6 -> 6; matrix products, arithmetic and copies ran while one was open for 0% -> 0% of each run, Pallas kernels for 23% -> 22%
where the time goes in v6:
time: 98.2 us; the launch traced here: 97.1 us
  starting transfers between devices  36.6 us (37%)
  Pallas kernels  25.8 us (26%)
  local copies, waits for them, and re-layouts  17.2 us (18%)
  waiting for transfers between devices  17.1 us (17%)
    pallas_call x15, Pallas kernels, call(): pl.pallas_call(run, out_shape=list(outs), in_specs=in_specs + [vmem] * le...  25.8 us
    ppermute x17, starting transfers between devices, flip(): lax.ppermute(value, axis, [(source, source ^ bits) for source in range(co...  24 us
    unnamed x64, local copies, waits for them, and re-layouts  17.2 us
    ppermute x17, waiting for transfers between devices, flip(): lax.ppermute(value, axis, [(source, source ^ bits) for source in range(co...  11.2 us
    all_to_all x1, starting transfers between devices, swap(): return lax.all_to_all(value, axis, split_axis=0, concat_axis=0, tiled=True)  8.25 us
    ppermute x2, waiting for transfers between devices, from_behind(): return lax.ppermute(value, axis, pairs)  5.87 us
    ppermute x2, starting transfers between devices, from_behind(): return lax.ppermute(value, axis, pairs)  4.36 us
  transfers between devices with their start and end apart: 20, of which 6 were waited for; matrix products, arithmetic and copies ran while one was open for 0% of the time, Pallas kernels for 22%

profile of v6, /device:TPU:0, one launch (start us, length us, event | category | flops | bytes accessed | tf_op | source)
XLA Modules:
  0.0 97.1 jit_solution(10982002457210289637)
XLA Ops:
  0.0 1.0 %copy-done.26 = bf16[192,1312]{1,0:T(8,128)(2,1)S(1)} copy-done((bf16[192,1312]{1,0:T(8,128)(2,1)S(1)}, bf16[192,1312]{1,0:T(8,128)(2,1)}, u32[]{:S(2)}) %copy-start.26) | copy-done | bytes 503832
  1.1 0.7 copy-done.30
  1.7 0.6 shard_map.127
  2.3 3.1 %collective-permute-start = (bf16[2,24,1312]{2,1,0:T(8,128)(2,1)S(1)}, bf16[2,24,1312]{2,1,0:T(8,128)(2,1)S(1)}, u32[]{:S(2)}, u32[]{:S(2)}) collective-permute-start(bf16[2,24,1312]{2,1,0:T(8,128)(2,1)S(1)} %get-tuple-element.32), channel_id=1, source_target_pairs={{0,2},{1,3},{2,0},{3,1},{4,6},{5,7},{6,4},{7,5},{8,10},{9,11},{10,... | collective-permute-start | bytes 377864 | tf_op jit(solution)/shard_map/ppermute | solution.py:591
  5.4 1.6 %collective-permute-start.1 = (bf16[2,24,1312]{2,1,0:T(8,128)(2,1)S(1)}, bf16[2,24,1312]{2,1,0:T(8,128)(2,1)S(1)}, u32[]{:S(2)}, u32[]{:S(2)}) collective-permute-start(bf16[2,24,1312]{2,1,0:T(8,128)(2,1)S(1)} %get-tuple-element.33), channel_id=1, source_target_pairs={{0,4},{1,5},{2,6},{3,7},{4,0},{5,1},{6,2},{7,3},{8,12},{9,13},{10,... | collective-permute-start | bytes 377864 | tf_op jit(solution)/shard_map/ppermute | solution.py:591
  7.0 3.0 %collective-permute-start.3 = (bf16[2,24,1312]{2,1,0:T(8,128)(2,1)S(1)}, bf16[2,24,1312]{2,1,0:T(8,128)(2,1)S(1)}, u32[]{:S(2)}, u32[]{:S(2)}) collective-permute-start(bf16[2,24,1312]{2,1,0:T(8,128)(2,1)S(1)} %get-tuple-element.35), channel_id=1, source_target_pairs={{0,8},{1,9},{2,10},{3,11},{4,12},{5,13},{6,14},{7,15},{8,0},{9,1},... | collective-permute-start | bytes 377864 | tf_op jit(solution)/shard_map/ppermute | solution.py:591
  9.9 1.3 %collective-permute-start.4 = (bf16[2,24,1312]{2,1,0:T(8,128)(2,1)S(1)}, bf16[2,24,1312]{2,1,0:T(8,128)(2,1)S(1)}, u32[]{:S(2)}, u32[]{:S(2)}) collective-permute-start(bf16[2,24,1312]{2,1,0:T(8,128)(2,1)S(1)} %get-tuple-element.36), channel_id=1, source_target_pairs={{0,10},{1,11},{2,8},{3,9},{4,14},{5,15},{6,12},{7,13},{8,2},{9,3},... | collective-permute-start | bytes 377864 | tf_op jit(solution)/shard_map/ppermute | solution.py:591
  11.2 0.4 shard_map.128.refs_4_
  11.6 0.8 copy-done.24
  12.4 2.4 %shard_map.129 = (bf16[192,192]{1,0:T(8,128)(2,1)S(1)}, bf16[192,576]{1,0:T(8,128)(2,1)S(1)}, bf16[2048,384]{1,0:T(8,128)(2,1)S(1)}, f32[2,64,768]{2,1,0:T(8,128)S(1)}, bf16[768,192]{1,0:T(8,128)(2,1)S(1)}) custom-call(s32[1]{0:T(128)} %bitcast.refs_0_, s32[4,192]{1,0:T(4,128)S(1)} %copy-done.29, bf16[1312,384]{1,0:T(8,128)(2,1)S(1)} %copy-done.24, ...), custom_call_target="tpu_custom_call" | custom-call | flops 2000000000 | bytes 1032288 | tf_op jit(solution)/shard_map/pallas_call | solution.py:74
  14.9 0.7 copy-done.17
  15.6 0.7 copy-done.20
  16.3 1.4 %shard_map.130.refs_4_.refs_12_ = bf16[48,256,128]{2,1,0:T(8,128)(2,1)S(1)} custom-call(s32[1]{0:T(128)} %bitcast.refs_0_, s32[4,192]{1,0:T(4,128)S(1)} %copy-done.29, bf16[192,1024]{1,0:T(8,128)(2,1)S(1)} %copy-done.27, bf16[2048,384]{1,0:T(8,128)(2,1)S(1)} %get-tuple-element.39.refs_3_.refs_6_.refs_14_), custom_call_target="tpu_custom_call" | custom-call | flops 2000000000 | bytes 396288 | tf_op jit(solution)/shard_map/pallas_call | solution.py:74
  17.8 3.7 %collective-permute-start.5 = (bf16[2,24,1312]{2,1,0:T(8,128)(2,1)S(1)}, bf16[2,24,1312]{2,1,0:T(8,128)(2,1)S(1)}, u32[]{:S(2)}, u32[]{:S(2)}) collective-permute-start(bf16[2,24,1312]{2,1,0:T(8,128)(2,1)S(1)} %get-tuple-element.37), channel_id=1, source_target_pairs={{0,12},{1,13},{2,14},{3,15},{4,8},{5,9},{6,10},{7,11},{8,4},{9,5},... | collective-permute-start | bytes 377864 | tf_op jit(solution)/shard_map/ppermute | solution.py:591
  21.5 1.4 %shard_map.131.refs_8_.refs_15_ = f32[192,384]{1,0:T(8,128)S(1)} custom-call(bf16[2,24,1312]{2,1,0:T(8,128)(2,1)S(1)} %get-tuple-element.31.refs_2_.refs_0_, bf16[2,24,1312]{2,1,0:T(8,128)(2,1)S(1)} %collective-permute-done.refs_1_, bf16[2,24,1312]{2,1,0:T(8,128)(2,1)S(1)} %collective-permute-done.1.refs_2_, ...), custom_call_target="tpu_custom_call" | custom-call | flops 2000000000 | bytes 5296128 | tf_op jit(solution)/shard_map/pallas_call | solution.py:74
  23.0 6.9 %collective-permute-done.4.refs_5_.refs_6_ = bf16[2,24,1312]{2,1,0:T(8,128)(2,1)S(1)} collective-permute-done((bf16[2,24,1312]{2,1,0:T(8,128)(2,1)S(1)}, bf16[2,24,1312]{2,1,0:T(8,128)(2,1)S(1)}, u32[]{:S(2)}, u32[]{:S(2)}) %collective-permute-start.4) | collective-permute-done | bytes 125984 | tf_op jit(solution)/shard_map/ppermute | solution.py:591
  29.9 0.9 shard_map.132
  30.8 0.7 copy-done.9
  31.5 8.2 %all-to-all-start = ((bf16[16,48,256]{2,1,0:T(8,128)(2,1)}), bf16[16,48,256]{2,1,0:T(8,128)(2,1)}, u32[]{:S(2)}, u32[]{:S(2)}) async-start(bf16[16,48,256]{2,1,0:T(8,128)(2,1)} %bitcast.5), calls=%async_computation | async-start | bytes 786432 | tf_op jit(solution)/shard_map/all_to_all | solution.py:573
  39.8 1.7 %copy-done.1 = bf16[2,384,1536]{2,1,0:T(8,128)(2,1)S(1)} copy-done((bf16[2,384,1536]{2,1,0:T(8,128)(2,1)S(1)}, bf16[2,384,1536]{2,1,0:T(8,128)(2,1)}, u32[]{:S(2)}) %copy-start.1) | copy-done | bytes 2359320
  41.5 1.7 %copy-done.3 = bf16[2,1536,384]{2,1,0:T(8,128)(2,1)S(1)} copy-done((bf16[2,1536,384]{2,1,0:T(8,128)(2,1)S(1)}, bf16[2,1536,384]{2,1,0:T(8,128)(2,1)}, u32[]{:S(2)}) %copy-start.3) | copy-done | bytes 2359320
  43.2 1.9 %copy-done.5 = bf16[48,256,128]{2,1,0:T(8,128)(2,1)S(1)} copy-done((bf16[48,256,128]{2,1,0:T(8,128)(2,1)S(1)}, bf16[48,256,128]{2,1,0:T(8,128)(2,1)}, u32[]{:S(2)}) %copy-start.5) | copy-done | bytes 3145752
  45.1 1.4 %copy-done.8 = bf16[2048,384]{1,0:T(8,128)(2,1)S(1)} copy-done((bf16[2048,384]{1,0:T(8,128)(2,1)S(1)}, bf16[2048,384]{1,0:T(8,128)(2,1)}, u32[]{:S(2)}) %copy-start.8) | copy-done | bytes 1572888
  46.5 1.0 copy-done.10
  47.4 0.9 copy-done.12
  48.3 0.9 copy-done.14
  49.2 0.9 copy-done.16
  50.2 0.9 copy-done.21
  51.1 5.9 %shard_map.133 = (bf16[96,384]{1,0:T(8,128)(2,1)S(1)}, bf16[96,384]{1,0:T(8,128)(2,1)S(1)}) custom-call(bf16[8,24,1312]{2,1,0:T(8,128)(2,1)S(1)} %collective-permute-done.7.refs_0_.refs_1_.refs_2_.refs_3_.refs_5_.refs_7_.refs_9_.refs_11_, bf16[8,24,1312]{2,1,0:T(8,128)(2,1)S(1)} %collective-permute-done.7.refs_0_.refs_1_.refs_2_.refs_3_.refs_5_.refs_7_.refs_9_.refs_11_, ...), custom_call_target="tpu_custom_call" | custom-call | flops 4000000000 | bytes 17246208 | tf_op jit(solution)/shard_map/pallas_call | solution.py:74
  57.0 4.4 %collective-permute-start.9 = (bf16[96,384]{1,0:T(8,128)(2,1)S(1)}, bf16[96,384]{1,0:T(8,128)(2,1)S(1)}, u32[]{:S(2)}, u32[]{:S(2)}) collective-permute-start(bf16[96,384]{1,0:T(8,128)(2,1)S(1)} %get-tuple-element.43.refs_0_.refs_1_), channel_id=1, source_target_pairs={{0,15},{1,0},{2,1},{3,2},{4,3},{5,4},{6,5},{7,6},{8,7},{9,8},{10,9... | collective-permute-start | bytes 221192 | tf_op jit(solution)/shard_map/ppermute | solution.py:597
  61.4 0.6 shard_map.134.refs_0_
  62.0 1.4 %collective-permute-done.9.refs_8_ = bf16[96,384]{1,0:T(8,128)(2,1)S(1)} collective-permute-done((bf16[96,384]{1,0:T(8,128)(2,1)S(1)}, bf16[96,384]{1,0:T(8,128)(2,1)S(1)}, u32[]{:S(2)}, u32[]{:S(2)}) %collective-permute-start.9) | collective-permute-done | bytes 73760 | tf_op jit(solution)/shard_map/ppermute | solution.py:597
  63.4 4.5 %collective-permute-done.8.refs_7_ = bf16[96,384]{1,0:T(8,128)(2,1)S(1)} collective-permute-done((bf16[96,384]{1,0:T(8,128)(2,1)S(1)}, bf16[96,384]{1,0:T(8,128)(2,1)S(1)}, u32[]{:S(2)}, u32[]{:S(2)}) %collective-permute-start.8) | collective-permute-done | bytes 73760 | tf_op jit(solution)/shard_map/ppermute | solution.py:597
  67.9 3.8 %shard_map.135 = (bf16[2,48,384]{2,1,0:T(8,128)(2,1)S(1)}, bf16[2,48,384]{2,1,0:T(8,128)(2,1)S(1)}, bf16[2,48,384]{2,1,0:T(8,128)(2,1)S(1)}, bf16[2,48,384]{2,1,...) custom-call(bf16[192,1152]{1,0:T(8,128)(2,1)S(1)} %shard_map.134.ref, ...), custom_call_target="tpu_custom_call" | custom-call | flops 2000000000 | bytes 8509440 | tf_op jit(solution)/shard_map/pallas_call | solution.py:74
  71.7 0.1 collective-permute-start.15
  71.8 3.4 %collective-permute-start.16 = (bf16[2,48,384]{2,1,0:T(8,128)(2,1)S(1)}, bf16[2,48,384]{2,1,0:T(8,128)(2,1)S(1)}, u32[]{:S(2)}, u32[]{:S(2)}) collective-permute-start(bf16[2,48,384]{2,1,0:T(8,128)(2,1)S(1)} %get-tuple-element.53), channel_id=1, source_target_pairs={{0,6},{1,7},{2,4},{3,5},{4,2},{5,3},{6,0},{7,1},{8,14},{9,15},{10,... | collective-permute-start | bytes 221192 | tf_op jit(solution)/shard_map/ppermute | solution.py:591
  75.2 1.2 %copy-done.25 = bf16[384,1312]{0,1:T(8,128)(2,1)S(1)} copy-done((bf16[384,1312]{0,1:T(8,128)(2,1)S(1)}, bf16[384,1312]{0,1:T(8,128)(2,1)}, u32[]{:S(2)}) %copy-start.25) | copy-done | bytes 1007640
  76.4 3.0 %shard_map.136 = (bf16[48,128,256]{2,1,0:T(8,128)(2,1)S(1)}, bf16[2048,384]{1,0:T(8,128)(2,1)S(1)}, s32[8,384]{1,0:T(8,128)S(1)}) custom-call(s32[1]{0:T(128)} %bitcast.refs_0_, bf16[768,256]{1,0:T(8,128)(2,1)} %bitcast.3.refs_1_, bf16[1312,384]{1,0:T(8,128)(2,1)S(1)} %bitcast.6, s32[1,384]{1,0:T(1,128)S(1)} %copy-done.31, ...), custom_call_target="tpu_custom_call" | custom-call | flops 2000000000 | bytes 1402368 | tf_op jit(solution)/shard_map/pallas_call | solution.py:74
  79.5 0.1 collective-permute-start.17
  79.6 2.4 %collective-permute-start.11 = (bf16[2,48,384]{2,1,0:T(8,128)(2,1)S(1)}, bf16[2,48,384]{2,1,0:T(8,128)(2,1)S(1)}, u32[]{:S(2)}, u32[]{:S(2)}) collective-permute-start(bf16[2,48,384]{2,1,0:T(8,128)(2,1)S(1)} %get-tuple-element.47), channel_id=1, source_target_pairs={{0,10},{1,11},{2,8},{3,9},{4,14},{5,15},{6,12},{7,13},{8,2},{9,3},... | collective-permute-start | bytes 221192 | tf_op jit(solution)/shard_map/ppermute | solution.py:591
  82.1 1.0 %collective-permute-start.12 = (bf16[2,48,384]{2,1,0:T(8,128)(2,1)S(1)}, bf16[2,48,384]{2,1,0:T(8,128)(2,1)S(1)}, u32[]{:S(2)}, u32[]{:S(2)}) collective-permute-start(bf16[2,48,384]{2,1,0:T(8,128)(2,1)S(1)} %get-tuple-element.48), channel_id=1, source_target_pairs={{0,12},{1,13},{2,14},{3,15},{4,8},{5,9},{6,10},{7,11},{8,4},{9,5},... | collective-permute-start | bytes 221192 | tf_op jit(solution)/shard_map/ppermute | solution.py:591
  83.1 4.2 %collective-permute-start.13 = (bf16[2,48,384]{2,1,0:T(8,128)(2,1)S(1)}, bf16[2,48,384]{2,1,0:T(8,128)(2,1)S(1)}, u32[]{:S(2)}, u32[]{:S(2)}) collective-permute-start(bf16[2,48,384]{2,1,0:T(8,128)(2,1)S(1)} %get-tuple-element.49), channel_id=1, source_target_pairs={{0,14},{1,15},{2,12},{3,13},{4,10},{5,11},{6,8},{7,9},{8,6},{9,7},... | collective-permute-start | bytes 221192 | tf_op jit(solution)/shard_map/ppermute | solution.py:591
  87.3 1.8 %shard_map.138.refs_4_.refs_8_ = bf16[192,2048]{1,0:T(8,128)(2,1)S(1)} custom-call(s32[1]{0:T(128)} %bitcast.refs_0_, bf16[2,48,384]{2,1,0:T(8,128)(2,1)S(1)} %get-tuple-element.50.refs_4_.refs_0_.refs_1_, bf16[4,48,384]{2,1,0:T(8,128)(2,1)S(1)} %collective-permute-done.17.refs_2_.refs_4_.refs_6_.refs_8_, ...), custom_call_target="tpu_custom_call" | custom-call | flops 2000000000 | bytes 5603328 | tf_op jit(solution)/shard_map/pallas_call | solution.py:74
  89.1 1.8 %collective-permute-done.10.refs_0_.refs_1_ = bf16[2,48,384]{2,1,0:T(8,128)(2,1)S(1)} collective-permute-done((bf16[2,48,384]{2,1,0:T(8,128)(2,1)S(1)}, bf16[2,48,384]{2,1,0:T(8,128)(2,1)S(1)}, u32[]{:S(2)}, u32[]{:S(2)}) %collective-permute-start.10) | collective-permute-done | bytes 73760 | tf_op jit(solution)/shard_map/ppermute | solution.py:591
  90.9 2.1 %collective-permute-done.11.refs_1_.refs_2_ = bf16[2,48,384]{2,1,0:T(8,128)(2,1)S(1)} collective-permute-done((bf16[2,48,384]{2,1,0:T(8,128)(2,1)S(1)}, bf16[2,48,384]{2,1,0:T(8,128)(2,1)S(1)}, u32[]{:S(2)}, u32[]{:S(2)}) %collective-permute-start.11) | collective-permute-done | bytes 73760 | tf_op jit(solution)/shard_map/ppermute | solution.py:591
  93.2 1.0 %shard_map.140.refs_5_ = bf16[96,2048]{1,0:T(8,128)(2,1)S(1)} custom-call(s32[1]{0:T(128)} %bitcast.refs_0_, bf16[2,48,384]{2,1,0:T(8,128)(2,1)S(1)} %collective-permute-done.10.refs_0_.refs_1_, bf16[2,48,384]{2,1,0:T(8,128)(2,1)S(1)} %collective-permute-done.11.refs_1_.refs_2_, bf16[2,48,384]{2,1,0:T(8,128)(2,1)S(1)} %collective-permute-done.12.refs_2_.refs_3_, ...), custom_call_target="tpu_custom_call" | custom-call | flops 1000000000 | bytes 5013504 | tf_op jit(solution)/shard_map/pallas_call | solution.py:74
  94.2 0.3 collective-permute-done.18.refs_1_.refs_2_.refs_3_.refs_4_
  94.6 2.6 %shard_map.141 = f32[192,1312]{1,0:T(8,128)} custom-call(s32[1]{0:T(128)} %bitcast.refs_0_, bf16[4,48,384]{2,1,0:T(8,128)(2,1)S(1)} %collective-permute-done.18.refs_1_.refs_2_.refs_3_.refs_4_, bf16[4,48,384]{2,1,0:T(8,128)(2,1)S(1)} %collective-permute-done.18.refs_1_.refs_2_.refs_3_.refs_4_, ...), custom_call_target="tpu_custom_call" | custom-call | flops 3000000000 | bytes 6500352 | tf_op jit(solution)/shard_map/pallas_call | solution.py:74
  (71 shorter events, 0.4 us)
Async XLA Ops:
  0.0 1.0 %copy-start.26 = (bf16[192,1312]{1,0:T(8,128)(2,1)S(1)}, bf16[192,1312]{1,0:T(8,128)(2,1)}, u32[]{:S(2)}) copy-start(bf16[192,1312]{1,0:T(8,128)(2,1)} %refs_2_.4) | copy-start | bytes 1511428
  1.7 9.5 %copy-start.27 = (bf16[192,1024]{1,0:T(8,128)(2,1)S(1)}, bf16[192,1024]{1,0:T(8,128)(2,1)}, u32[]{:S(2)}) copy-start(bf16[192,1024]{1,0:T(8,128)(2,1)} %refs_2_.6) | copy-start | bytes 1179652
  1.7 9.5 %copy-start.29 = (s32[4,192]{1,0:T(4,128)S(1)}, s32[4,192]{1,0:T(4,128)}, u32[]{:S(2)}) copy-start(s32[4,192]{1,0:T(4,128)} %refs_1_.7) | copy-start | bytes 9220
  2.3 15.5 %collective-permute-start = (bf16[2,24,1312]{2,1,0:T(8,128)(2,1)S(1)}, bf16[2,24,1312]{2,1,0:T(8,128)(2,1)S(1)}, u32[]{:S(2)}, u32[]{:S(2)}) collective-permute-start(bf16[2,24,1312]{2,1,0:T(8,128)(2,1)S(1)} %get-tuple-element.32), channel_id=1, source_target_pairs={{0,2},{1,3},{2,0},{3,1},{4,6},{5,7},{6,4},{7,5},{8,10},{9,11},{10,... | collective-permute-start | bytes 377864 | tf_op jit(solution)/shard_map/ppermute | solution.py:591
  5.4 16.1 %collective-permute-start.1 = (bf16[2,24,1312]{2,1,0:T(8,128)(2,1)S(1)}, bf16[2,24,1312]{2,1,0:T(8,128)(2,1)S(1)}, u32[]{:S(2)}, u32[]{:S(2)}) collective-permute-start(bf16[2,24,1312]{2,1,0:T(8,128)(2,1)S(1)} %get-tuple-element.33), channel_id=1, source_target_pairs={{0,4},{1,5},{2,6},{3,7},{4,0},{5,1},{6,2},{7,3},{8,12},{9,13},{10,... | collective-permute-start | bytes 377864 | tf_op jit(solution)/shard_map/ppermute | solution.py:591
  7.0 14.5 %collective-permute-start.2 = (bf16[2,24,1312]{2,1,0:T(8,128)(2,1)S(1)}, bf16[2,24,1312]{2,1,0:T(8,128)(2,1)S(1)}, u32[]{:S(2)}, u32[]{:S(2)}) collective-permute-start(bf16[2,24,1312]{2,1,0:T(8,128)(2,1)S(1)} %get-tuple-element.34), channel_id=1, source_target_pairs={{0,6},{1,7},{2,4},{3,5},{4,2},{5,3},{6,0},{7,1},{8,14},{9,15},{10,... | collective-permute-start | bytes 377864 | tf_op jit(solution)/shard_map/ppermute | solution.py:591
  7.0 16.0 %collective-permute-start.3 = (bf16[2,24,1312]{2,1,0:T(8,128)(2,1)S(1)}, bf16[2,24,1312]{2,1,0:T(8,128)(2,1)S(1)}, u32[]{:S(2)}, u32[]{:S(2)}) collective-permute-start(bf16[2,24,1312]{2,1,0:T(8,128)(2,1)S(1)} %get-tuple-element.35), channel_id=1, source_target_pairs={{0,8},{1,9},{2,10},{3,11},{4,12},{5,13},{6,14},{7,15},{8,0},{9,1},... | collective-permute-start | bytes 377864 | tf_op jit(solution)/shard_map/ppermute | solution.py:591
  9.9 19.9 %collective-permute-start.4 = (bf16[2,24,1312]{2,1,0:T(8,128)(2,1)S(1)}, bf16[2,24,1312]{2,1,0:T(8,128)(2,1)S(1)}, u32[]{:S(2)}, u32[]{:S(2)}) collective-permute-start(bf16[2,24,1312]{2,1,0:T(8,128)(2,1)S(1)} %get-tuple-element.36), channel_id=1, source_target_pairs={{0,10},{1,11},{2,8},{3,9},{4,14},{5,15},{6,12},{7,13},{8,2},{9,3},... | collective-permute-start | bytes 377864 | tf_op jit(solution)/shard_map/ppermute | solution.py:591
  11.2 1.2 %copy-start.24 = (bf16[1312,384]{1,0:T(8,128)(2,1)S(1)}, bf16[1312,384]{1,0:T(8,128)(2,1)}, u32[]{:S(2)}) copy-start(bf16[1312,384]{1,0:T(8,128)(2,1)} %refs_2_.5) | copy-start | bytes 3022852
  11.2 1.2 %copy-start.28 = (f32[2,12,225]{2,0,1:T(2,128)S(1)}, f32[2,12,225]{2,0,1:T(2,128)}, u32[]{:S(2)}) copy-start(f32[2,12,225]{2,0,1:T(2,128)} %param.20) | copy-start | bytes 64804
  11.6 3.3 %copy-start.19 = (bf16[768,256]{1,0:T(8,128)(2,1)}, bf16[768,256]{1,0:T(8,128)(2,1)S(1)}, u32[]{:S(2)}) copy-start(bf16[768,256]{1,0:T(8,128)(2,1)S(1)} %shard_map.128.refs_4_) | copy-start | bytes 1179652
  16.3 5.2 %copy-start.7 = (bf16[2048,384]{1,0:T(8,128)(2,1)}, bf16[2048,384]{1,0:T(8,128)(2,1)S(1)}, u32[]{:S(2)}) copy-start(bf16[2048,384]{1,0:T(8,128)(2,1)S(1)} %get-tuple-element.39.refs_3_.refs_6_.refs_14_) | copy-start | bytes 4718596
  17.8 5.2 %copy-start.4 = (bf16[48,256,128]{2,1,0:T(8,128)(2,1)}, bf16[48,256,128]{2,1,0:T(8,128)(2,1)S(1)}, u32[]{:S(2)}) copy-start(bf16[48,256,128]{2,1,0:T(8,128)(2,1)S(1)} %shard_map.130.refs_4_.refs_12_) | copy-start | bytes 9437188
  17.8 12.1 %collective-permute-start.5 = (bf16[2,24,1312]{2,1,0:T(8,128)(2,1)S(1)}, bf16[2,24,1312]{2,1,0:T(8,128)(2,1)S(1)}, u32[]{:S(2)}, u32[]{:S(2)}) collective-permute-start(bf16[2,24,1312]{2,1,0:T(8,128)(2,1)S(1)} %get-tuple-element.37), channel_id=1, source_target_pairs={{0,12},{1,13},{2,14},{3,15},{4,8},{5,9},{6,10},{7,11},{8,4},{9,5},... | collective-permute-start | bytes 377864 | tf_op jit(solution)/shard_map/ppermute | solution.py:591
  21.5 8.4 %collective-permute-start.6 = (bf16[2,24,1312]{2,1,0:T(8,128)(2,1)S(1)}, bf16[2,24,1312]{2,1,0:T(8,128)(2,1)S(1)}, u32[]{:S(2)}, u32[]{:S(2)}) collective-permute-start(bf16[2,24,1312]{2,1,0:T(8,128)(2,1)S(1)} %get-tuple-element.38), channel_id=1, source_target_pairs={{0,14},{1,15},{2,12},{3,13},{4,10},{5,11},{6,8},{7,9},{8,6},{9,7},... | collective-permute-start | bytes 377864 | tf_op jit(solution)/shard_map/ppermute | solution.py:591
  22.9 16.9 %copy-start = (bf16[2,384,1152]{2,1,0:T(8,128)(2,1)S(1)}, bf16[2,384,1152]{2,1,0:T(8,128)(2,1)}, u32[]{:S(2)}) copy-start(bf16[2,384,1152]{2,1,0:T(8,128)(2,1)} %refs_5_.1) | copy-start | bytes 5308420
  23.0 16.9 %copy-start.6 = (bf16[2,384,384]{2,1,0:T(8,128)(2,1)S(1)}, bf16[2,384,384]{2,1,0:T(8,128)(2,1)}, u32[]{:S(2)}) copy-start(bf16[2,384,384]{2,1,0:T(8,128)(2,1)} %refs_9_.1) | copy-start | bytes 1769476
  23.0 16.9 %copy-start.22 = (f32[2,384]{1,0:T(2,128)S(1)}, f32[2,384]{1,0:T(2,128)}, u32[]{:S(2)}) copy-start(f32[2,384]{1,0:T(2,128)} %refs_3_.4) | copy-start | bytes 9220
  23.0 16.9 %copy-start.23 = (f32[2,384]{1,0:T(2,128)S(1)}, f32[2,384]{1,0:T(2,128)}, u32[]{:S(2)}) copy-start(f32[2,384]{1,0:T(2,128)} %refs_4_.1) | copy-start | bytes 9220
  29.9 0.9 copy-start.11
  29.9 1.7 %copy-start.13 = (bf16[2,24,1312]{2,1,0:T(8,128)(2,1)}, bf16[2,24,1312]{2,1,0:T(8,128)(2,1)S(1)}, u32[]{:S(2)}) copy-start(bf16[2,24,1312]{2,1,0:T(8,128)(2,1)S(1)} %collective-permute-done.5.refs_6_.refs_8_) | copy-start | bytes 377860
  29.9 1.6 %copy-start.15 = (bf16[2,24,1312]{2,1,0:T(8,128)(2,1)}, bf16[2,24,1312]{2,1,0:T(8,128)(2,1)S(1)}, u32[]{:S(2)}) copy-start(bf16[2,24,1312]{2,1,0:T(8,128)(2,1)S(1)} %collective-permute-done.6.refs_7_.refs_10_) | copy-start | bytes 377860
  31.5 8.3 %collective-permute-start.7 = (bf16[8,24,1312]{2,1,0:T(8,128)(2,1)}, bf16[8,24,1312]{2,1,0:T(8,128)(2,1)S(1)}, u32[]{:S(2)}, u32[]{:S(2)}) collective-permute-start(bf16[8,24,1312]{2,1,0:T(8,128)(2,1)} %shard_map.132), channel_id=1, source_target_pairs={{0,1},{1,0},{2,3},{3,2},{4,5},{5,4},{6,7},{7,6},{8,9},{9,8},{10,11... | collective-permute-start | bytes 1511432 | tf_op jit(solution)/shard_map/ppermute | solution.py:591
  31.5 43.7 %all-to-all-start = ((bf16[16,48,256]{2,1,0:T(8,128)(2,1)}), bf16[16,48,256]{2,1,0:T(8,128)(2,1)}, u32[]{:S(2)}, u32[]{:S(2)}) async-start(bf16[16,48,256]{2,1,0:T(8,128)(2,1)} %bitcast.5), calls=%async_computation | async-start | bytes 786432 | tf_op jit(solution)/shard_map/all_to_all | solution.py:573
  39.8 1.7 %copy-start.1 = (bf16[2,384,1536]{2,1,0:T(8,128)(2,1)S(1)}, bf16[2,384,1536]{2,1,0:T(8,128)(2,1)}, u32[]{:S(2)}) copy-start(bf16[2,384,1536]{2,1,0:T(8,128)(2,1)} %refs_10_.1) | copy-start | bytes 7077892
  41.5 1.7 %copy-start.3 = (bf16[2,1536,384]{2,1,0:T(8,128)(2,1)S(1)}, bf16[2,1536,384]{2,1,0:T(8,128)(2,1)}, u32[]{:S(2)}) copy-start(bf16[2,1536,384]{2,1,0:T(8,128)(2,1)} %refs_11_.1) | copy-start | bytes 7077892
  43.2 1.9 %copy-start.5 = (bf16[48,256,128]{2,1,0:T(8,128)(2,1)S(1)}, bf16[48,256,128]{2,1,0:T(8,128)(2,1)}, u32[]{:S(2)}) copy-start(bf16[48,256,128]{2,1,0:T(8,128)(2,1)} %copy-done.4) | copy-start | bytes 9437188
  45.1 1.4 %copy-start.8 = (bf16[2048,384]{1,0:T(8,128)(2,1)S(1)}, bf16[2048,384]{1,0:T(8,128)(2,1)}, u32[]{:S(2)}) copy-start(bf16[2048,384]{1,0:T(8,128)(2,1)} %copy-done.7) | copy-start | bytes 4718596
  46.5 1.0 copy-start.10
  47.4 0.9 copy-start.12
  48.3 0.9 copy-start.14
  49.2 0.9 copy-start.16
  50.2 0.9 copy-start.21
  51.1 16.8 %copy-start.18 = (bf16[768,192]{1,0:T(8,128)(2,1)S(1)}, bf16[768,192]{1,0:T(8,128)(2,1)}, u32[]{:S(2)}) copy-start(bf16[768,192]{1,0:T(8,128)(2,1)} %copy-done.17) | copy-start | bytes 884740
  57.0 10.9 %copy-start.2 = (bf16[2,384,1536]{2,1,0:T(8,128)(2,1)S(1)}, bf16[2,384,1536]{2,1,0:T(8,128)(2,1)}, u32[]{:S(2)}) copy-start(bf16[2,384,1536]{2,1,0:T(8,128)(2,1)} %refs_10_.1) | copy-start | bytes 7077892
  57.0 6.3 %collective-permute-start.9 = (bf16[96,384]{1,0:T(8,128)(2,1)S(1)}, bf16[96,384]{1,0:T(8,128)(2,1)S(1)}, u32[]{:S(2)}, u32[]{:S(2)}) collective-permute-start(bf16[96,384]{1,0:T(8,128)(2,1)S(1)} %get-tuple-element.43.refs_0_.refs_1_), channel_id=1, source_target_pairs={{0,15},{1,0},{2,1},{3,2},{4,3},{5,4},{6,5},{7,6},{8,7},{9,8},{10,9... | collective-permute-start | bytes 221192 | tf_op jit(solution)/shard_map/ppermute | solution.py:597
  61.4 6.5 %collective-permute-start.8 = (bf16[96,384]{1,0:T(8,128)(2,1)S(1)}, bf16[96,384]{1,0:T(8,128)(2,1)S(1)}, u32[]{:S(2)}, u32[]{:S(2)}) collective-permute-start(bf16[96,384]{1,0:T(8,128)(2,1)S(1)} %get-tuple-element.44.refs_1_.refs_2_), channel_id=1, source_target_pairs={{0,1},{1,2},{2,3},{3,4},{4,5},{5,6},{6,7},{7,8},{8,9},{9,10},{10,1... | collective-permute-start | bytes 221192 | tf_op jit(solution)/shard_map/ppermute | solution.py:597
  67.9 7.3 %copy-start.31 = (s32[1,384]{1,0:T(1,128)S(1)}, s32[1,384]{1,0:T(1,128)}, u32[]{:S(2)}) copy-start(s32[1,384]{1,0:T(1,128)} %refs_3_.5) | copy-start | bytes 4612
  71.6 7.8 %collective-permute-start.14 = (bf16[2,48,384]{2,1,0:T(8,128)(2,1)S(1)}, bf16[2,48,384]{2,1,0:T(8,128)(2,1)S(1)}, u32[]{:S(2)}, u32[]{:S(2)}) collective-permute-start(bf16[2,48,384]{2,1,0:T(8,128)(2,1)S(1)} %get-tuple-element.51), channel_id=1, source_target_pairs={{0,2},{1,3},{2,0},{3,1},{4,6},{5,7},{6,4},{7,5},{8,10},{9,11},{10,... | collective-permute-start | bytes 221192 | tf_op jit(solution)/shard_map/ppermute | solution.py:591
  71.7 7.7 %collective-permute-start.15 = (bf16[2,48,384]{2,1,0:T(8,128)(2,1)S(1)}, bf16[2,48,384]{2,1,0:T(8,128)(2,1)S(1)}, u32[]{:S(2)}, u32[]{:S(2)}) collective-permute-start(bf16[2,48,384]{2,1,0:T(8,128)(2,1)S(1)} %get-tuple-element.52), channel_id=1, source_target_pairs={{0,4},{1,5},{2,6},{3,7},{4,0},{5,1},{6,2},{7,3},{8,12},{9,13},{10,... | collective-permute-start | bytes 221192 | tf_op jit(solution)/shard_map/ppermute | solution.py:591
  71.8 7.7 %collective-permute-start.16 = (bf16[2,48,384]{2,1,0:T(8,128)(2,1)S(1)}, bf16[2,48,384]{2,1,0:T(8,128)(2,1)S(1)}, u32[]{:S(2)}, u32[]{:S(2)}) collective-permute-start(bf16[2,48,384]{2,1,0:T(8,128)(2,1)S(1)} %get-tuple-element.53), channel_id=1, source_target_pairs={{0,6},{1,7},{2,4},{3,5},{4,2},{5,3},{6,0},{7,1},{8,14},{9,15},{10,... | collective-permute-start | bytes 221192 | tf_op jit(solution)/shard_map/ppermute | solution.py:591
  75.2 1.2 %copy-start.25 = (bf16[384,1312]{0,1:T(8,128)(2,1)S(1)}, bf16[384,1312]{0,1:T(8,128)(2,1)}, u32[]{:S(2)}) copy-start(bf16[384,1312]{0,1:T(8,128)(2,1)} %param.25) | copy-start | bytes 3022852
  79.5 7.8 %collective-permute-start.17 = (bf16[4,48,384]{2,1,0:T(8,128)(2,1)S(1)}, bf16[4,48,384]{2,1,0:T(8,128)(2,1)S(1)}, u32[]{:S(2)}, u32[]{:S(2)}) collective-permute-start(bf16[4,48,384]{2,1,0:T(8,128)(2,1)S(1)} %shard_map.137), channel_id=1, source_target_pairs={{0,1},{1,0},{2,3},{3,2},{4,5},{5,4},{6,7},{7,6},{8,9},{9,8},{10,11... | collective-permute-start | bytes 442376 | tf_op jit(solution)/shard_map/ppermute | solution.py:591
  79.6 11.4 %collective-permute-start.10 = (bf16[2,48,384]{2,1,0:T(8,128)(2,1)S(1)}, bf16[2,48,384]{2,1,0:T(8,128)(2,1)S(1)}, u32[]{:S(2)}, u32[]{:S(2)}) collective-permute-start(bf16[2,48,384]{2,1,0:T(8,128)(2,1)S(1)} %get-tuple-element.46), channel_id=1, source_target_pairs={{0,8},{1,9},{2,10},{3,11},{4,12},{5,13},{6,14},{7,15},{8,0},{9,1},... | collective-permute-start | bytes 221192 | tf_op jit(solution)/shard_map/ppermute | solution.py:591
  79.6 13.4 %collective-permute-start.11 = (bf16[2,48,384]{2,1,0:T(8,128)(2,1)S(1)}, bf16[2,48,384]{2,1,0:T(8,128)(2,1)S(1)}, u32[]{:S(2)}, u32[]{:S(2)}) collective-permute-start(bf16[2,48,384]{2,1,0:T(8,128)(2,1)S(1)} %get-tuple-element.47), channel_id=1, source_target_pairs={{0,10},{1,11},{2,8},{3,9},{4,14},{5,15},{6,12},{7,13},{8,2},{9,3},... | collective-permute-start | bytes 221192 | tf_op jit(solution)/shard_map/ppermute | solution.py:591
  82.1 11.0 %collective-permute-start.12 = (bf16[2,48,384]{2,1,0:T(8,128)(2,1)S(1)}, bf16[2,48,384]{2,1,0:T(8,128)(2,1)S(1)}, u32[]{:S(2)}, u32[]{:S(2)}) collective-permute-start(bf16[2,48,384]{2,1,0:T(8,128)(2,1)S(1)} %get-tuple-element.48), channel_id=1, source_target_pairs={{0,12},{1,13},{2,14},{3,15},{4,8},{5,9},{6,10},{7,11},{8,4},{9,5},... | collective-permute-start | bytes 221192 | tf_op jit(solution)/shard_map/ppermute | solution.py:591
  83.1 10.0 %collective-permute-start.13 = (bf16[2,48,384]{2,1,0:T(8,128)(2,1)S(1)}, bf16[2,48,384]{2,1,0:T(8,128)(2,1)S(1)}, u32[]{:S(2)}, u32[]{:S(2)}) collective-permute-start(bf16[2,48,384]{2,1,0:T(8,128)(2,1)S(1)} %get-tuple-element.49), channel_id=1, source_target_pairs={{0,14},{1,15},{2,12},{3,13},{4,10},{5,11},{6,8},{7,9},{8,6},{9,7},... | collective-permute-start | bytes 221192 | tf_op jit(solution)/shard_map/ppermute | solution.py:591
  93.1 1.4 %collective-permute-start.18 = (bf16[4,48,384]{2,1,0:T(8,128)(2,1)S(1)}, bf16[4,48,384]{2,1,0:T(8,128)(2,1)S(1)}, u32[]{:S(2)}, u32[]{:S(2)}) collective-permute-start(bf16[4,48,384]{2,1,0:T(8,128)(2,1)S(1)} %shard_map.139.refs_7_), channel_id=1, source_target_pairs={{0,1},{1,0},{2,3},{3,2},{4,5},{5,4},{6,7},{7,6},{8,9},{9,8},{10,11... | collective-permute-start | bytes 442376 | tf_op jit(solution)/shard_map/ppermute | solution.py:591
  (4 other events, 2.8 us)
